TPU v7x, 512 devices: a whole 4x8x8 slice. The times are simulated.
512 devices in a mesh: seq: 64 (over z_hi, y, core), grp: 8 (over x, z_lo).
Axes of the slice: x: 4, y: 8, z: 8 (z_hi: 4, z_lo: 2; z = z_hi * 2 + z_lo), core: 2. Of those that a mesh axis runs over, the one named last changes fastest.
Arguments:
- embeddings: bfloat16 [1536, 32768], P('grp', 'seq'), may hold values from -6 to 6
- hilbert_order: int32 [32768], P('seq'), may hold values from 0 to 32767, as said below
- cotangent: bfloat16 [1536, 32768], P('grp', 'seq'), may hold values from -6 to 6
- first_conv_weight: bfloat16 [8, 110592], P('grp'), may hold values from -0.25 to 0.25
- first_pointwise_weight: bfloat16 [1536, 1536], P('grp'), may hold values from -0.21875 to 0.21875
- second_conv_weight: bfloat16 [8, 110592], P('grp'), may hold values from -0.25 to 0.25
- second_pointwise_weight: bfloat16 [1536, 1536], P('grp'), may hold values from -0.21875 to 0.21875
Outputs:
- emb_grad: bfloat16 [1536, 32768], P('grp', 'seq')
- first_conv_gradient: bfloat16 [8, 110592], P('grp')
- first_pointwise_gradient: bfloat16 [1536, 1536], P('grp')
- second_conv_gradient: bfloat16 [8, 110592], P('grp')
- second_pointwise_gradient: bfloat16 [1536, 1536], P('grp')
Inputs may be any that keep to these rules, and one draw needn't show every extreme that they name: `hilbert_order`: every aligned block of 512 positions holds each patch index of that same block exactly once.
All inputs are finite; a program needn't handle non-finite values.
Results may differ from a plain program's by a relative error of at most 0.018.
Values may be sent and summed in bfloat16 or wider, within the bound.
No kernel may reach another device: no remote copies, remote signals or barrier semaphores. Data moves between devices by JAX's collectives and lax.ppermute only.
A program may use at most 64 MiB of HBM per device.

v0:
```python
import jax
import jax.numpy as jnp
from jax import lax
from jax.sharding import PartitionSpec as P

CG = 192


def passed_along(block, axis, distance):
    devices = range(lax.axis_size(axis))
    route = [(i - distance, i) for i in devices if i - distance in devices]
    return lax.ppermute(block, axis, route)


def shard_taps(inputs, shift_by):
    earlier = passed_along(inputs, "seq", shift_by)
    following = passed_along(inputs, "seq", -shift_by)
    return (earlier, inputs, following)


def grad_taps(grad_pre, shift_by):
    following = passed_along(grad_pre, "seq", -shift_by)
    earlier = passed_along(grad_pre, "seq", shift_by)
    return (following, grad_pre, earlier)


def tap_weights(conv_weight, tap):
    groups_here = conv_weight.shape[0]
    return conv_weight.reshape(groups_here, 3, CG, CG)[:, tap]


def group_apply(values, weight_tap):
    channels, col_count = values.shape
    groups_here = channels // CG
    return jnp.einsum(
        "git,gio->got",
        values.reshape(groups_here, CG, col_count),
        weight_tap,
        preferred_element_type=jnp.float32,
    ).reshape(channels, col_count)


def group_back(grads, weight_tap):
    channels, col_count = grads.shape
    groups_here = channels // CG
    return jnp.einsum(
        "got,gio->git",
        grads.reshape(groups_here, CG, col_count),
        weight_tap,
        preferred_element_type=jnp.float32,
    ).reshape(channels, col_count)


def group_grad(values, grads):
    channels, col_count = values.shape
    groups_here = channels // CG
    return jnp.einsum(
        "git,got->gio",
        values.reshape(groups_here, CG, col_count),
        grads.reshape(groups_here, CG, col_count),
        preferred_element_type=jnp.float32,
    )


def block_forward_step(inputs, conv_weight, shift_by):
    tap_set = shard_taps(inputs, shift_by)
    hidden = (
        group_apply(tap_set[0], tap_weights(conv_weight, 0))
        + group_apply(tap_set[1], tap_weights(conv_weight, 1))
        + group_apply(tap_set[2], tap_weights(conv_weight, 2))
    )
    activated = jax.nn.silu(hidden).astype(jnp.bfloat16)
    gathered = lax.all_gather(activated, "grp", axis=0, tiled=True)
    return (tap_set, hidden, gathered)


def block_backward_step(
    grad_out, tap_set, hidden, gathered, conv_weight, pointwise, shift_by, gradient_scale
):
    shard_width, col_count = grad_out.shape
    groups_here = conv_weight.shape[0]
    point_grad = lax.dot_general(
        grad_out, gathered, (((1,), (1,)), ((), ())), preferred_element_type=jnp.float32
    )
    weight_rows = lax.all_to_all(pointwise, "grp", split_axis=1, concat_axis=0, tiled=True)
    block_in = lax.all_gather(grad_out, "grp", axis=0, tiled=True)
    width_in = block_in.shape[0]
    shard_count = width_in // shard_width
    partials = jnp.einsum(
        "jot,joi->jit",
        block_in.reshape(shard_count, shard_width, col_count),
        weight_rows.reshape(shard_count, shard_width, shard_width),
        preferred_element_type=jnp.float32,
    )
    rounded = lax.optimization_barrier(partials.astype(jnp.bfloat16))
    grad_hidden = jnp.sum(rounded.astype(jnp.float32), axis=0)
    sigmoid_h = jax.nn.sigmoid(hidden)
    grad_pre = (grad_hidden * sigmoid_h * (1.0 + hidden * (1.0 - sigmoid_h))).astype(jnp.bfloat16)
    conv_grad = jnp.stack(
        [group_grad(tap_values, grad_pre) for tap_values in tap_set], axis=1
    ).reshape(groups_here, 3 * CG * CG)
    moved = grad_taps(grad_pre, shift_by)
    grad_input = (
        grad_out.astype(jnp.float32)
        + group_back(moved[0], tap_weights(conv_weight, 0))
        + group_back(moved[1], tap_weights(conv_weight, 1))
        + group_back(moved[2], tap_weights(conv_weight, 2))
    )
    summed = lax.psum((conv_grad, point_grad), "seq")
    conv_result = (summed[0] * gradient_scale).astype(jnp.bfloat16)
    point_result = (summed[1] * gradient_scale).astype(jnp.bfloat16)
    return (grad_input.astype(jnp.bfloat16), conv_result, point_result)


def local(
    embeddings,
    hilbert_order,
    cotangent,
    first_conv_weight,
    first_pointwise_weight,
    second_conv_weight,
    second_pointwise_weight,
):
    seq_count = lax.axis_size("seq")
    gradient_scale = float(embeddings.shape[1] * seq_count) ** (-0.5)
    near_shift = seq_count // 16
    far_shift = seq_count // 8
    local_index = hilbert_order - lax.axis_index("seq") * hilbert_order.shape[0]
    initial_token_rows = jnp.take(embeddings, local_index, axis=1)
    first_tap_rows, first_hidden_state, near_full = block_forward_step(
        initial_token_rows, first_conv_weight, near_shift
    )
    middle_rows = (
        initial_token_rows.astype(jnp.float32)
        + jnp.dot(first_pointwise_weight, near_full, preferred_element_type=jnp.float32)
    ).astype(jnp.bfloat16)
    second_tap_rows, second_hidden_state, far_full = block_forward_step(
        middle_rows, second_conv_weight, far_shift
    )
    middle_gradient, second_conv_gradient, second_pointwise_gradient = block_backward_step(
        cotangent,
        second_tap_rows,
        second_hidden_state,
        far_full,
        second_conv_weight,
        second_pointwise_weight,
        far_shift,
        gradient_scale,
    )
    start_gradient, first_conv_gradient, first_pointwise_gradient = block_backward_step(
        middle_gradient,
        first_tap_rows,
        first_hidden_state,
        near_full,
        first_conv_weight,
        first_pointwise_weight,
        near_shift,
        gradient_scale,
    )
    emb_grad = jnp.zeros_like(start_gradient).at[:, local_index].set(start_gradient)
    return (
        emb_grad,
        first_conv_gradient,
        first_pointwise_gradient,
        second_conv_gradient,
        second_pointwise_gradient,
    )


def solution(mesh):
    placed = (
        P("grp", "seq"),
        P("seq"),
        P("grp", "seq"),
        P("grp", None),
        P("grp", None),
        P("grp", None),
        P("grp", None),
    )
    return jax.shard_map(
        local,
        mesh=mesh,
        in_specs=placed,
        out_specs=(P("grp", "seq"), P("grp", None), P("grp", None), P("grp", None), P("grp", None)),
        check_vma=False,
    )
```

profile of v0, /device:TPU:1, one launch (start us, length us, event | category | flops | bytes accessed | tf_op | source)
XLA Modules:
  0.0 842.4 jit_solution(17735297071518127190)
XLA Ops:
  9.8 2.0 gather_fusion
  13.2 5.7 collective-permute-start
  20.7 1.6 collective-permute-done.1
  24.8 9.1 %all-to-all-start = ((bf16[192,8,192]{0,2,1:T(8,128)(2,1)}), bf16[192,8,192]{0,2,1:T(8,128)(2,1)S(1)}, u32[]{:S(2)}, u32[]{:S(2)}) async-start(bf16[192,8,192]{0,2,1:T(8,128)(2,1)} %bitcast), calls=%async_computation | async-start | bytes 1572864 | tf_op jit(solution)/shard_map/all_to_all | solution.py:85
  35.5 15.1 %all-to-all-done = bf16[192,8,192]{0,2,1:T(8,128)(2,1)S(1)} async-done(((bf16[192,8,192]{0,2,1:T(8,128)(2,1)}), bf16[192,8,192]{0,2,1:T(8,128)(2,1)S(1)}, u32[]{:S(2)}, u32[]{:S(2)}) %all-to-all-start) | async-done | bytes 589856 | tf_op jit(solution)/shard_map/all_to_all | solution.py:85
  50.7 21.0 %all-gather.5.cloned.1.call-done = bf16[1536,512]{1,0:T(8,128)(2,1)} async-done(((bf16[192,512]{1,0:T(8,128)(2,1)}), bf16[1536,512]{1,0:T(8,128)(2,1)}) %all-gather.5.cloned.1.call-update) | async-done | bytes 1572880 | tf_op jit(solution)/shard_map/all_gather | solution.py:86
  71.6 2.0 convolution_convert_fusion.1
  73.9 49.9 %all-gather.7.cloned.1.call-done = bf16[1536,512]{1,0:T(8,128)(2,1)} async-done(((bf16[192,512]{1,0:T(8,128)(2,1)}), bf16[1536,512]{1,0:T(8,128)(2,1)}) %all-gather.7.cloned.1.call-update) | async-done | bytes 1572880 | tf_op jit(solution)/shard_map/all_gather | solution.py:73
  123.7 1.9 fusion.12
  126.9 7.9 collective-permute-start.2
  139.9 15.3 %collective-permute-start.5 = (bf16[192,512]{1,0:T(8,128)(2,1)S(1)}, bf16[192,512]{1,0:T(8,128)(2,1)S(1)}, u32[]{:S(2)}, u32[]{:S(2)}) collective-permute-start(bf16[192,512]{1,0:T(8,128)(2,1)S(1)} %get-tuple-element.17), channel_id=1, source_target_pairs={{0,64},{8,72},{16,80},{24,88},{32,96},{40,104},{48,112},{56,120},{... | collective-permute-start | bytes 589832 | tf_op jit(solution)/shard_map/ppermute | solution.py:12
  156.6 3.6 collective-permute-done.5
  162.3 3.7 all-to-all-start.1
  168.1 1.7 fusion.27
  169.9 39.5 %all-gather.11.cloned.1.call-done = bf16[1536,512]{1,0:T(8,128)(2,1)} async-done(((bf16[192,512]{1,0:T(8,128)(2,1)}), bf16[1536,512]{1,0:T(8,128)(2,1)}) %all-gather.11.cloned.1.call-update) | async-done | bytes 1572880 | tf_op jit(solution)/shard_map/all_gather | solution.py:73
  209.4 3.1 convolution_bitcast_fusion
  212.5 49.4 %all-gather.9.cloned.1.call-done = bf16[1536,512]{1,0:T(8,128)(2,1)} async-done(((bf16[192,512]{1,0:T(8,128)(2,1)}), bf16[1536,512]{1,0:T(8,128)(2,1)}) %all-gather.9.cloned.1.call-update) | async-done | bytes 1572880 | tf_op jit(solution)/shard_map/all_gather | solution.py:86
  261.9 2.0 fusion
  267.1 4.2 collective-permute-start.7
  273.0 13.5 %collective-permute-done.6 = bf16[192,512]{1,0:T(8,128)(2,1)S(1)} collective-permute-done((bf16[192,512]{1,0:T(8,128)(2,1)S(1)}, bf16[192,512]{1,0:T(8,128)(2,1)S(1)}, u32[]{:S(2)}, u32[]{:S(2)}) %collective-permute-start.6) | collective-permute-done | bytes 196640 | tf_op jit(solution)/shard_map/ppermute | solution.py:12
  287.0 2.4 scatter_custom_fusion
  290.2 540.1 %all-reduce.3.cloned.1.call-done = (f32[1,110592]{1,0:T(1,128)}, f32[192,1536]{1,0:T(8,128)}, f32[1,110592]{1,0:T(1,128)}, f32[192,1536]{1,0:T(8,128)}) async-done(((f32[1,110592]{1,0:T(1,128)}, f32[192,1536]{1,0:T(8,128)}, f32[1,110592]{1,0:T(1,128)}, f32[192,1536]{1,0:T(8,128)}), (f32[1,110592]{1,0:T(1,128)}, f32[192,1536]{1,0:T(8,128)}, f32[1,110592]{1,0:T(1,128)}, ...) | async-done | bytes 3244048 | tf_op jit(solution)/shard_map/psum | solution.py:109
  830.3 3.1 multiply_convert_fusion.2
  833.3 2.5 multiply_convert_fusion
  (98 shorter events, 28.1 us)
Async XLA Ops:
  7.2 64.5 %all-gather.5.cloned.1.call-start = ((), (), s32[]{:S(2)}) async-start(), calls=%async_computation.2 | async-start | bytes 1769472 | tf_op jit(solution)/shard_map/all_gather | solution.py:86
  7.9 11.0 %copy-start.13 = (bf16[1,110592]{1,0:T(2,128)(2,1)S(1)}, bf16[1,110592]{1,0:T(2,128)(2,1)}, u32[]{:S(2)}) copy-start(bf16[1,110592]{1,0:T(2,128)(2,1)} %param.10) | copy-start | bytes 663556
  7.9 115.8 %all-gather.7.cloned.1.call-start = ((), (), s32[]{:S(2)}) async-start(), calls=%async_computation.3 | async-start | bytes 1769472 | tf_op jit(solution)/shard_map/all_gather | solution.py:73
  11.9 10.4 %collective-permute-start.1 = (bf16[192,512]{1,0:T(8,128)(2,1)S(1)}, bf16[192,512]{1,0:T(8,128)(2,1)S(1)}, u32[]{:S(2)}, u32[]{:S(2)}) collective-permute-start(bf16[192,512]{1,0:T(8,128)(2,1)S(1)} %fusion.17), channel_id=1, source_target_pairs={{32,0},{40,8},{48,16},{56,24},{64,32},{72,40},{80,48},{88,56},{96,... | collective-permute-start | bytes 589832 | tf_op jit(solution)/shard_map/ppermute | solution.py:12
  13.2 9.3 %collective-permute-start = (bf16[192,512]{1,0:T(8,128)(2,1)S(1)}, bf16[192,512]{1,0:T(8,128)(2,1)S(1)}, u32[]{:S(2)}, u32[]{:S(2)}) collective-permute-start(bf16[192,512]{1,0:T(8,128)(2,1)S(1)} %fusion.17), channel_id=1, source_target_pairs={{0,32},{8,40},{16,48},{24,56},{32,64},{40,72},{48,80},{56,88},{64,... | collective-permute-start | bytes 589832 | tf_op jit(solution)/shard_map/ppermute | solution.py:12
  20.4 3.3 copy-start.3
  23.7 10.3 %copy-start.14 = (bf16[1,110592]{1,0:T(2,128)(2,1)S(1)}, bf16[1,110592]{1,0:T(2,128)(2,1)}, u32[]{:S(2)}) copy-start(bf16[1,110592]{1,0:T(2,128)(2,1)} %param.12) | copy-start | bytes 663556
  24.8 25.8 %all-to-all-start = ((bf16[192,8,192]{0,2,1:T(8,128)(2,1)}), bf16[192,8,192]{0,2,1:T(8,128)(2,1)S(1)}, u32[]{:S(2)}, u32[]{:S(2)}) async-start(bf16[192,8,192]{0,2,1:T(8,128)(2,1)} %bitcast), calls=%async_computation | async-start | bytes 1572864 | tf_op jit(solution)/shard_map/all_to_all | solution.py:85
  33.9 175.5 %all-gather.11.cloned.1.call-start = ((), (), s32[]{:S(2)}) async-start(), calls=%async_computation.5 | async-start | bytes 1769472 | tf_op jit(solution)/shard_map/all_gather | solution.py:73
  73.6 50.1 %copy-start.2 = (bf16[192,1536]{1,0:T(8,128)(2,1)S(1)}, bf16[192,1536]{1,0:T(8,128)(2,1)}, u32[]{:S(2)}) copy-start(bf16[192,1536]{1,0:T(8,128)(2,1)} %param.11) | copy-start | bytes 1769476
  125.6 10.9 %collective-permute-start.3 = (bf16[192,512]{1,0:T(8,128)(2,1)S(1)}, bf16[192,512]{1,0:T(8,128)(2,1)S(1)}, u32[]{:S(2)}, u32[]{:S(2)}) collective-permute-start(bf16[192,512]{1,0:T(8,128)(2,1)S(1)} %fusion.12), channel_id=1, source_target_pairs={{64,0},{72,8},{80,16},{88,24},{96,32},{104,40},{112,48},{120,56},{... | collective-permute-start | bytes 589832 | tf_op jit(solution)/shard_map/ppermute | solution.py:12
  126.9 10.5 %collective-permute-start.2 = (bf16[192,512]{1,0:T(8,128)(2,1)S(1)}, bf16[192,512]{1,0:T(8,128)(2,1)S(1)}, u32[]{:S(2)}, u32[]{:S(2)}) collective-permute-start(bf16[192,512]{1,0:T(8,128)(2,1)S(1)} %fusion.12), channel_id=1, source_target_pairs={{0,64},{8,72},{16,80},{24,88},{32,96},{40,104},{48,112},{56,120},{... | collective-permute-start | bytes 589832 | tf_op jit(solution)/shard_map/ppermute | solution.py:12
  137.2 19.2 %copy-start.5 = (bf16[192,512]{1,0:T(8,128)(2,1)S(1)}, bf16[192,512]{1,0:T(8,128)(2,1)}, u32[]{:S(2)}) copy-start(bf16[192,512]{1,0:T(8,128)(2,1)} %param.9) | copy-start | bytes 589828
  138.5 123.3 %all-gather.9.cloned.1.call-start = ((), (), s32[]{:S(2)}) async-start(), calls=%async_computation.4 | async-start | bytes 1769472 | tf_op jit(solution)/shard_map/all_gather | solution.py:86
  138.6 17.8 %collective-permute-start.4 = (bf16[192,512]{1,0:T(8,128)(2,1)S(1)}, bf16[192,512]{1,0:T(8,128)(2,1)S(1)}, u32[]{:S(2)}, u32[]{:S(2)}) collective-permute-start(bf16[192,512]{1,0:T(8,128)(2,1)S(1)} %get-tuple-element.17), channel_id=1, source_target_pairs={{64,0},{72,8},{80,16},{88,24},{96,32},{104,40},{112,48},{120,56},{... | collective-permute-start | bytes 589832 | tf_op jit(solution)/shard_map/ppermute | solution.py:12
  139.9 20.3 %collective-permute-start.5 = (bf16[192,512]{1,0:T(8,128)(2,1)S(1)}, bf16[192,512]{1,0:T(8,128)(2,1)S(1)}, u32[]{:S(2)}, u32[]{:S(2)}) collective-permute-start(bf16[192,512]{1,0:T(8,128)(2,1)S(1)} %get-tuple-element.17), channel_id=1, source_target_pairs={{0,64},{8,72},{16,80},{24,88},{32,96},{40,104},{48,112},{56,120},{... | collective-permute-start | bytes 589832 | tf_op jit(solution)/shard_map/ppermute | solution.py:12
  162.3 4.0 copy-start.11
  162.3 4.2 copy-start.19
  162.3 50.2 %all-to-all-start.1 = ((bf16[192,8,192]{0,2,1:T(8,128)(2,1)}), bf16[192,8,192]{0,2,1:T(8,128)(2,1)S(1)}, u32[]{:S(2)}, u32[]{:S(2)}) async-start(bf16[192,8,192]{0,2,1:T(8,128)(2,1)} %bitcast.17), calls=%async_computation.1 | async-start | bytes 1572864 | tf_op jit(solution)/shard_map/all_to_all | solution.py:85
  166.0 664.3 %all-reduce.3.cloned.1.call-start = ((), (), s32[]{:S(2)}) async-start(), calls=%async_computation.6 | async-start | bytes 6488064 | tf_op jit(solution)/shard_map/psum | solution.py:109
  168.1 41.3 %copy-start.6 = (bf16[192,512]{1,0:T(8,128)(2,1)S(1)}, bf16[192,512]{1,0:T(8,128)(2,1)}, u32[]{:S(2)}) copy-start(bf16[192,512]{1,0:T(8,128)(2,1)} %param.9) | copy-start | bytes 589828
  267.1 5.7 copy-start.4
  267.1 19.5 %collective-permute-start.7 = (bf16[192,512]{1,0:T(8,128)(2,1)S(1)}, bf16[192,512]{1,0:T(8,128)(2,1)S(1)}, u32[]{:S(2)}, u32[]{:S(2)}) collective-permute-start(bf16[192,512]{1,0:T(8,128)(2,1)S(1)} %multiply_convert_fusion.5), channel_id=1, source_target_pairs={{0,32},{8,40},{16,48},{24,56},{32,64},{40,72},{48,80},{56,88},{64,... | collective-permute-start | bytes 589832 | tf_op jit(solution)/shard_map/ppermute | solution.py:12
  271.3 15.1 %collective-permute-start.6 = (bf16[192,512]{1,0:T(8,128)(2,1)S(1)}, bf16[192,512]{1,0:T(8,128)(2,1)S(1)}, u32[]{:S(2)}, u32[]{:S(2)}) collective-permute-start(bf16[192,512]{1,0:T(8,128)(2,1)S(1)} %multiply_convert_fusion.5), channel_id=1, source_target_pairs={{32,0},{40,8},{48,16},{56,24},{64,32},{72,40},{80,48},{88,56},{96,... | collective-permute-start | bytes 589832 | tf_op jit(solution)/shard_map/ppermute | solution.py:12
  (11 other events, 19.1 us)
Sparse Core Ops, SparseCore 0:
  10.1 61.5 all-gather.4
  74.3 49.3 all-gather.6
  138.6 70.7 all-gather.10
  211.9 49.9 all-gather.8
  267.2 562.9 all-reduce.2
where the time goes:
time: 843 us; the launch traced here: 842 us
  waiting for transfers between devices  737 us (87%)
  starting transfers between devices  51.4 us (6%)
  matrix products  17 us (2%)
  between operations  14.2 us (2%)
  local copies, waits for them, and re-layouts  13.1 us (2%)
  other arithmetic  9.59 us (1%)
    psum x1, waiting for transfers between devices, block_backward_step(): summed = lax.psum((conv_grad, point_grad), 'seq')  540 us
    all_gather x2, waiting for transfers between devices, block_forward_step(): gathered = lax.all_gather(activated, 'grp', axis=0, tiled=True)  89.4 us
    all_gather x2, waiting for transfers between devices, block_backward_step(): block_in = lax.all_gather(grad_out, 'grp', axis=0, tiled=True)  70.3 us
    ppermute x8, starting transfers between devices, passed_along(): return lax.ppermute(block, axis, route)  38.4 us
    ppermute x8, waiting for transfers between devices, passed_along(): return lax.ppermute(block, axis, route)  21.3 us
  transfers between devices with their start and end apart: 15, of which 12 were waited for; matrix products, arithmetic and copies ran while one was open for 3% of the time, Pallas kernels for 0%

commit v1 on v0

v1 whole, which is shorter than its diff:
```python
import jax
import jax.numpy as jnp
from jax import lax
from jax.sharding import Mesh, PartitionSpec as P

CG = 192
BF = jnp.bfloat16
F32 = jnp.float32
SEQ = ("zh", "yh", "yl", "core")
GRP = ("x", "zl")
SAME = ("zh", "yh")
CHIPS = ("zh", "yh", "yl")


def mm(a, b, ca, cb):
    return lax.dot_general(a, b, (((ca,), (cb,)), ((), ())), preferred_element_type=F32)


def swap(blocks, axes):
    return lax.all_to_all(blocks, axes, 0, 0, tiled=True)


def shifted(values, by):
    rows, cols = values.shape
    if by == 0:
        return values
    filler = jnp.zeros((rows, abs(by)), values.dtype)
    if by > 0:
        return jnp.concatenate([values[:, by:], filler], axis=1)
    return jnp.concatenate([filler, values[:, :by]], axis=1)


def taps(values, by):
    return (shifted(values, -by), values, shifted(values, by))


def conv(values, weight, by):
    return sum(mm(weight[k], tap, 0, 0) for k, tap in enumerate(taps(values, by)))


def conv_back(grads, weight, by):
    return sum(mm(weight[k], tap, 1, 0) for k, tap in enumerate(taps(grads, by)[::-1]))


def conv_grad(values, grads, by):
    return jnp.concatenate([mm(tap, grads, 1, 1) for tap in taps(values, by)], axis=0)


def other_core(values):
    return lax.ppermute(values, "core", [(0, 1), (1, 0)])


def core_sum(partial):
    first = lax.axis_index("core") == 0
    mine = jnp.where(first, partial[0], partial[1])
    got = other_core(jnp.where(first, partial[1], partial[0]))
    return (mine.astype(F32) + got.astype(F32)).astype(BF)


def chips_sum(half, scale):
    return (jnp.sum(swap(half, CHIPS).astype(F32), axis=0) * scale).astype(BF)


def chips_spread(piece):
    everyone = swap(jnp.broadcast_to(piece[None], (32,) + piece.shape), CHIPS)
    other = other_core(everyone)
    first = lax.axis_index("core") == 0
    return jnp.concatenate([jnp.where(first, everyone, other), jnp.where(first, other, everyone)], axis=0)


def conv_rows(grad):
    rows = grad.astype(BF).reshape(864, 128)
    return jnp.pad(rows, ((0, 32), (0, 0))).reshape(2, 32, 14, 128)


def conv_flat(rows):
    return rows.reshape(896 * 128)[: 3 * CG * CG].reshape(1, 3 * CG * CG)


def local(emb, order, cot, cw1, pw1, cw2, pw2):
    scale = float(32768) ** (-0.5)
    cols = emb.shape[1]
    s = lax.axis_index(SEQ)
    index = order - s * cols
    w1 = cw1.reshape(3, CG, CG)
    w2 = cw2.reshape(3, CG, CG)
    onehot = (lax.broadcasted_iota(jnp.int32, (cols, cols), 0) == index[None, :]).astype(BF)
    eye = (
        lax.broadcasted_iota(jnp.int32, (CG, CG), 0) == lax.broadcasted_iota(jnp.int32, (CG, CG), 1)
    ).astype(BF)
    start_t = mm(onehot, emb, 0, 1).astype(BF)
    packed = jnp.concatenate([start_t, cot.T], axis=1).reshape(16, cols // 16, 2 * CG)
    packed = swap(packed, SAME).reshape(cols, 2 * CG)
    start = mm(eye, packed[:, :CG], 1, 1).astype(BF)
    cotq = mm(eye, packed[:, CG:], 1, 1).astype(BF)

    near_hidden = conv(start, w1, 32)
    near_act = jax.nn.silu(near_hidden).astype(BF)
    act_all = swap(jnp.broadcast_to(near_act[None], (8, CG, cols)), GRP).reshape(8 * CG, cols)

    pw2_blocks = pw2.reshape(CG, 8, CG).transpose(1, 0, 2)
    sent = jnp.concatenate([jnp.broadcast_to(cotq[None], (8, CG, cols)), pw2_blocks], axis=2)
    sent = swap(sent, GRP).reshape(8 * CG, cols + CG)
    cot_all, pw2_cols = sent[:, :cols], sent[:, cols:]

    middle = (start.astype(F32) + mm(pw1, act_all, 1, 0)).astype(BF)
    far_hidden = conv(middle, w2, 64)
    far_s = jax.nn.sigmoid(far_hidden)
    far_act = (far_hidden * far_s).astype(BF)
    far_da = mm(pw2_cols, cot_all, 0, 0)
    far_dh = (far_da * far_s * (1.0 + far_hidden * (1.0 - far_s))).astype(BF)
    grad_middle = (cotq.astype(F32) + conv_back(far_dh, w2, 64)).astype(BF)

    parts = mm(pw1, grad_middle, 0, 0).astype(BF).reshape(8, CG, cols)
    got = swap(parts, GRP)
    near_da = jnp.sum(got.astype(F32), axis=0)

    pg2 = mm(cot_all, far_act, 1, 1).astype(BF)
    pg2 = pg2.reshape(8, 2, 32, 3 * CG).transpose(1, 2, 0, 3).reshape(2, 32, 36, 128)
    pg1 = mm(grad_middle, act_all, 1, 1).astype(BF).reshape(2, 32, 36, 128)
    cg2 = conv_rows(conv_grad(middle, far_dh, 64))
    early = chips_sum(core_sum(jnp.concatenate([pg1, pg2, cg2], axis=2)), scale)
    piece2 = swap(early[36:72].reshape(8, 3 * CG), GRP)
    piece2 = piece2.reshape(8, 3, CG).transpose(1, 0, 2).reshape(36, 128)

    near_s = jax.nn.sigmoid(near_hidden)
    near_dh = (near_da * near_s * (1.0 + near_hidden * (1.0 - near_s))).astype(BF)
    grad_start = (grad_middle.astype(F32) + conv_back(near_dh, w1, 32)).astype(BF)
    cg1 = conv_rows(conv_grad(start, near_dh, 32))
    late = chips_sum(core_sum(cg1), scale)
    whole = chips_spread(jnp.concatenate([early[:36], piece2, early[72:], late], axis=0))
    out_pg1 = whole[:, :36].reshape(CG, 8 * CG)
    out_pg2 = whole[:, 36:72].reshape(CG, 8 * CG)
    out_cg2 = conv_flat(whole[:, 72:86])
    out_cg1 = conv_flat(whole[:, 86:])

    back = mm(grad_start, eye, 0, 0).astype(BF).reshape(16, cols // 16, CG)
    back = swap(back, SAME).reshape(cols, CG)
    emb_grad = mm(back, onehot, 0, 1).astype(BF)
    return emb_grad, out_cg1, out_pg1, out_cg2, out_pg2


def solution(mesh):
    fine = Mesh(mesh.devices.reshape(4, 4, 2, 2, 4, 2), SEQ + GRP)
    placed = (P(GRP, SEQ), P(SEQ), P(GRP, SEQ), P(GRP, None), P(GRP, None), P(GRP, None), P(GRP, None))
    return jax.shard_map(
        local,
        mesh=fine,
        in_specs=placed,
        out_specs=(P(GRP, SEQ), P(GRP, None), P(GRP, None), P(GRP, None), P(GRP, None)),
        check_vma=False,
    )
```

time: 843 us -> 278 us (0.33)
  waiting for transfers between devices: 737 us -> 125 us
  starting transfers between devices: 51.4 us -> 72.6 us
  blocking collectives: 0 us -> 19.4 us
  local copies, waits for them, and re-layouts: 13.1 us -> 30.8 us
  between operations: 14.2 us -> 1.46 us
    psum x1 -> x0, waiting for transfers between devices: 540 us -> none  [block_backward_step(): summed = lax.psum((conv_grad, point_grad), 'seq')]
    all_gather x4 -> x0, waiting for transfers between devices: 160 us -> none  [the longest x2 89.4 us: block_forward_step(): gathered = lax.all_gather(activated, 'grp', axis=0, tiled=True)]
    all_to_all x2 -> x8, waiting for transfers between devices: 15.1 us -> 123 us  [swap(): return lax.all_to_all(blocks, axes, 0, 0, tiled=True)]
    all_to_all x2 -> x8, starting transfers between devices: 12.8 us -> 53.3 us  [swap(): return lax.all_to_all(blocks, axes, 0, 0, tiled=True)]
    ppermute x8 -> x3, waiting for transfers between devices: 21.3 us -> 1.78 us  [other_core(): return lax.ppermute(values, 'core', [(0, 1), (1, 0)])]
    all_to_all x0 -> x1, blocking collectives: none -> 19.4 us  [swap(): return lax.all_to_all(blocks, axes, 0, 0, tiled=True)]
    ppermute x8 -> x3, starting transfers between devices: 38.4 us -> 19.2 us  [other_core(): return lax.ppermute(values, 'core', [(0, 1), (1, 0)])]
    reshape x4 -> x13, local copies, waits for them, and re-layouts: 3.03 us -> 13 us  [the longest x2 3.42 us: local(): pg2.reshape(8, 2, 32, 3 * CG).transpose(1, 2, 0, 3).reshape(2, 32, 36, 128)]
  transfers between devices with their start and end apart: 15 -> 11, of which waited for: 12 -> 9; matrix products, arithmetic and copies ran while one was open for 3% -> 6% of each run, Pallas kernels for 0% -> 0%
where the time goes in v1:
time: 278 us; the launch traced here: 276 us
  waiting for transfers between devices  125 us (45%)
  starting transfers between devices  72.6 us (26%)
  local copies, waits for them, and re-layouts  30.8 us (11%)
  blocking collectives  19.4 us (7%)
  matrix products  18.8 us (7%)
  other arithmetic  8.17 us (3%)
    all_to_all x8, waiting for transfers between devices, swap(): return lax.all_to_all(blocks, axes, 0, 0, tiled=True)  123 us
    all_to_all x8, starting transfers between devices, swap(): return lax.all_to_all(blocks, axes, 0, 0, tiled=True)  53.3 us
    all_to_all x1, blocking collectives, swap(): return lax.all_to_all(blocks, axes, 0, 0, tiled=True)  19.4 us
    ppermute x3, starting transfers between devices, other_core(): return lax.ppermute(values, 'core', [(0, 1), (1, 0)])  19.2 us
    dot_general x27, matrix products, mm(): lax.dot_general(a, b, (((ca,), (cb,)), ((), ())), preferred_element_type=...  18.8 us
  transfers between devices with their start and end apart: 11, of which 9 were waited for; matrix products, arithmetic and copies ran while one was open for 6% of the time, Pallas kernels for 0%

profile of v1, /device:TPU:1, one launch (start us, length us, event | category | flops | bytes accessed | tf_op | source)
XLA Modules:
  0.0 276.1 jit_solution(18317388233061888753)
XLA Ops:
  4.6 16.2 %all-to-all-start = ((bf16[16,32,384]{2,1,0:T(8,128)(2,1)}), bf16[16,32,384]{2,1,0:T(8,128)(2,1)S(1)}, u32[]{:S(2)}, u32[]{:S(2)}) async-start(bf16[16,32,384]{2,1,0:T(8,128)(2,1)} %bitcast.1), calls=%async_computation | async-start | bytes 786432 | tf_op jit(solution)/shard_map/all_to_all | solution.py:20
  22.4 14.1 %all-to-all-done = bf16[16,32,384]{2,1,0:T(8,128)(2,1)S(1)} async-done(((bf16[16,32,384]{2,1,0:T(8,128)(2,1)}), bf16[16,32,384]{2,1,0:T(8,128)(2,1)S(1)}, u32[]{:S(2)}, u32[]{:S(2)}) %all-to-all-start) | async-done | bytes 393248 | tf_op jit(solution)/shard_map/all_to_all | solution.py:20
  39.9 4.9 %all-to-all-start.2 = ((bf16[8,192,512]{2,1,0:T(8,128)(2,1)}), bf16[8,192,512]{2,1,0:T(8,128)(2,1)S(1)}, u32[]{:S(2)}, u32[]{:S(2)}) async-start(bf16[8,192,512]{2,1,0:T(8,128)(2,1)} %broadcast_in_dim.7), calls=%async_computation.2 | async-start | bytes 3145728 | tf_op jit(solution)/shard_map/all_to_all | solution.py:20
  49.7 14.0 %all-to-all-done.2 = bf16[8,192,512]{2,1,0:T(8,128)(2,1)S(1)} async-done(((bf16[8,192,512]{2,1,0:T(8,128)(2,1)}), bf16[8,192,512]{2,1,0:T(8,128)(2,1)S(1)}, u32[]{:S(2)}, u32[]{:S(2)}) %all-to-all-start.2) | async-done | bytes 1572896 | tf_op jit(solution)/shard_map/all_to_all | solution.py:20
  63.7 4.8 %all-to-all-start.1 = ((bf16[8,192,704]{2,1,0:T(8,128)(2,1)}), bf16[8,192,704]{2,1,0:T(8,128)(2,1)}, u32[]{:S(2)}, u32[]{:S(2)}) async-start(bf16[8,192,704]{2,1,0:T(8,128)(2,1)} %pad_maximum_fusion), calls=%async_computation.1 | async-start | bytes 4718592 | tf_op jit(solution)/shard_map/all_to_all | solution.py:20
  72.3 22.9 %all-to-all-done.1 = bf16[8,192,704]{2,1,0:T(8,128)(2,1)} async-done(((bf16[8,192,704]{2,1,0:T(8,128)(2,1)}), bf16[8,192,704]{2,1,0:T(8,128)(2,1)}, u32[]{:S(2)}, u32[]{:S(2)}) %all-to-all-start.1) | async-done | bytes 2162720 | tf_op jit(solution)/shard_map/all_to_all | solution.py:20
  95.2 2.3 fusion.19
  98.3 2.9 %convolution_convert_fusion.1 = bf16[1536,192]{0,1:T(8,128)(2,1)} fusion(bf16[1536,704]{1,0:T(8,128)(2,1)} %bitcast.4, f32[192,512]{1,0:T(8,128)S(1)} %copy-done.20), kind=kOutput, calls=%fused_computation.3 | convolution fusion | flops 302776320 | bytes 2555904 | tf_op jit(solution)/shard_map/dot_general | solution.py:16
  113.8 1.8 reshape.124
  116.3 6.0 %collective-permute-start = (bf16[32,86,128]{2,0,1:T(8,128)(2,1)S(1)}, bf16[32,86,128]{2,0,1:T(8,128)(2,1)S(1)}, u32[]{:S(2)}, u32[]{:S(2)}) collective-permute-start(bf16[32,86,128]{2,0,1:T(8,128)(2,1)S(1)} %copy.54), channel_id=1, source_target_pairs={{0,8},{8,0},{1,9},{9,1},{2,10},{10,2},{3,11},{11,3},{4,12},{12,4},... | collective-permute-start | bytes 2113544 | tf_op jit(solution)/shard_map/ppermute | solution.py:50
  122.2 1.8 collective-permute-done
  125.3 7.4 %all-to-all-start.5 = ((bf16[32,86,128]{2,1,0:T(8,128)(2,1)}), bf16[32,86,128]{2,1,0:T(8,128)(2,1)S(1)}, u32[]{:S(2)}, u32[]{:S(2)}) async-start(bf16[32,86,128]{2,1,0:T(8,128)(2,1)} %fusion.1), calls=%async_computation.5 | async-start | bytes 1441792 | tf_op jit(solution)/shard_map/all_to_all | solution.py:20
  134.9 18.5 %all-to-all-done.5 = bf16[32,86,128]{2,1,0:T(8,128)(2,1)S(1)} async-done(((bf16[32,86,128]{2,1,0:T(8,128)(2,1)}), bf16[32,86,128]{2,1,0:T(8,128)(2,1)S(1)}, u32[]{:S(2)}, u32[]{:S(2)}) %all-to-all-start.5) | async-done | bytes 704544 | tf_op jit(solution)/shard_map/all_to_all | solution.py:20
  153.5 3.8 %all-to-all-start.3 = ((bf16[8,192,512]{2,1,0:T(8,128)(2,1)}), bf16[8,192,512]{2,1,0:T(8,128)(2,1)S(1)}, u32[]{:S(2)}, u32[]{:S(2)}) async-start(bf16[8,192,512]{2,1,0:T(8,128)(2,1)} %bitcast.11), calls=%async_computation.3 | async-start | bytes 3145728 | tf_op jit(solution)/shard_map/all_to_all | solution.py:20
  157.4 17.9 %all-to-all-done.3 = bf16[8,192,512]{2,1,0:T(8,128)(2,1)S(1)} async-done(((bf16[8,192,512]{2,1,0:T(8,128)(2,1)}), bf16[8,192,512]{2,1,0:T(8,128)(2,1)S(1)}, u32[]{:S(2)}, u32[]{:S(2)}) %all-to-all-start.3) | async-done | bytes 1572896 | tf_op jit(solution)/shard_map/all_to_all | solution.py:20
  178.0 5.9 %collective-permute-start.1 = (bf16[32,14,128]{2,1,0:T(8,128)(2,1)S(1)}, bf16[32,14,128]{2,1,0:T(8,128)(2,1)S(1)}, u32[]{:S(2)}, u32[]{:S(2)}) collective-permute-start(bf16[32,14,128]{2,1,0:T(8,128)(2,1)S(1)} %select_n.52), channel_id=1, source_target_pairs={{0,8},{8,0},{1,9},{9,1},{2,10},{10,2},{3,11},{11,3},{4,12},{12,4},... | collective-permute-start | bytes 344072 | tf_op jit(solution)/shard_map/ppermute | solution.py:50
  185.9 3.3 %all-to-all-start.6 = ((bf16[8,2,288]{2,1,0:T(2,128)(2,1)}), bf16[8,2,288]{2,1,0:T(2,128)(2,1)S(1)}, u32[]{:S(2)}, u32[]{:S(2)}) async-start(bf16[8,2,288]{2,1,0:T(2,128)(2,1)} %reshape.145), calls=%async_computation.6 | async-start | bytes 24576 | tf_op jit(solution)/shard_map/all_to_all | solution.py:20
  190.0 4.3 %all-to-all-done.6 = bf16[8,2,288]{2,1,0:T(2,128)(2,1)S(1)} async-done(((bf16[8,2,288]{2,1,0:T(2,128)(2,1)}), bf16[8,2,288]{2,1,0:T(2,128)(2,1)S(1)}, u32[]{:S(2)}, u32[]{:S(2)}) %all-to-all-start.6) | async-done | bytes 9248 | tf_op jit(solution)/shard_map/all_to_all | solution.py:20
  194.3 8.8 %all-to-all-start.7 = ((bf16[32,14,128]{2,1,0:T(8,128)(2,1)}), bf16[32,14,128]{2,1,0:T(8,128)(2,1)S(1)}, u32[]{:S(2)}, u32[]{:S(2)}) async-start(bf16[32,14,128]{2,1,0:T(8,128)(2,1)} %add_convert_fusion), calls=%async_computation.7 | async-start | bytes 262144 | tf_op jit(solution)/shard_map/all_to_all | solution.py:20
  203.4 11.2 %all-to-all-done.7 = bf16[32,14,128]{2,1,0:T(8,128)(2,1)S(1)} async-done(((bf16[32,14,128]{2,1,0:T(8,128)(2,1)}), bf16[32,14,128]{2,1,0:T(8,128)(2,1)S(1)}, u32[]{:S(2)}, u32[]{:S(2)}) %all-to-all-start.7) | async-done | bytes 114720 | tf_op jit(solution)/shard_map/all_to_all | solution.py:20
  215.8 4.0 %all-to-all-start.8 = ((bf16[32,100,128]{2,1,0:T(8,128)(2,1)}), bf16[32,100,128]{2,1,0:T(8,128)(2,1)S(1)}, u32[]{:S(2)}, u32[]{:S(2)}) async-start(bf16[32,100,128]{2,1,0:T(8,128)(2,1)} %broadcast_in_dim.8), calls=%async_computation.8 | async-start | bytes 1703936 | tf_op jit(solution)/shard_map/all_to_all | solution.py:20
  220.4 20.2 %all-to-all-done.8 = bf16[32,100,128]{2,1,0:T(8,128)(2,1)S(1)} async-done(((bf16[32,100,128]{2,1,0:T(8,128)(2,1)}), bf16[32,100,128]{2,1,0:T(8,128)(2,1)S(1)}, u32[]{:S(2)}, u32[]{:S(2)}) %all-to-all-start.8) | async-done | bytes 819232 | tf_op jit(solution)/shard_map/all_to_all | solution.py:20
  241.6 7.4 %collective-permute-start.2 = (bf16[32,100,128]{2,0,1:T(8,128)(2,1)}, bf16[32,100,128]{2,0,1:T(8,128)(2,1)S(1)}, u32[]{:S(2)}, u32[]{:S(2)}) collective-permute-start(bf16[32,100,128]{2,0,1:T(8,128)(2,1)} %copy.59), channel_id=1, source_target_pairs={{0,8},{8,0},{1,9},{9,1},{2,10},{10,2},{3,11},{11,3},{4,12},{12,4},... | collective-permute-start | bytes 2457608 | tf_op jit(solution)/shard_map/ppermute | solution.py:50
  249.7 19.4 %all_to_all.50 = bf16[16,32,192]{2,1,0:T(8,128)(2,1)S(1)} all-to-all(bf16[16,32,192]{2,1,0:T(8,128)(2,1)S(1)} %bitcast.82), channel_id=1, replica_groups=mesh['zh'=4,'yh'=4,'yl'=2,'core'=2,'x'=4,'zl'=2] {'zh','yh'}, dimensions={0} | all-to-all | bytes 393216 | tf_op jit(solution)/shard_map/all_to_all | solution.py:20
  (148 shorter events, 50.7 us)
Async XLA Ops:
  0.6 69.5 %copy-start = (bf16[192,1536]{1,0:T(8,128)(2,1)S(1)}, bf16[192,1536]{1,0:T(8,128)(2,1)}, u32[]{:S(2)}) copy-start(bf16[192,1536]{1,0:T(8,128)(2,1)} %param.11) | copy-start | bytes 1769476
  0.6 20.2 %copy-start.18 = (bf16[1,110592]{1,0:T(2,128)(2,1)S(1)}, bf16[1,110592]{1,0:T(2,128)(2,1)}, u32[]{:S(2)}) copy-start(bf16[1,110592]{1,0:T(2,128)(2,1)} %param.10) | copy-start | bytes 663556
  4.6 32.0 %all-to-all-start = ((bf16[16,32,384]{2,1,0:T(8,128)(2,1)}), bf16[16,32,384]{2,1,0:T(8,128)(2,1)S(1)}, u32[]{:S(2)}, u32[]{:S(2)}) async-start(bf16[16,32,384]{2,1,0:T(8,128)(2,1)} %bitcast.1), calls=%async_computation | async-start | bytes 786432 | tf_op jit(solution)/shard_map/all_to_all | solution.py:20
  22.2 15.4 %copy-start.12 = (bf16[192,192]{1,0:T(8,128)(2,1)}, bf16[192,192]{1,0:T(8,128)(2,1)S(1)}, u32[]{:S(2)}) copy-start(bf16[192,192]{1,0:T(8,128)(2,1)S(1)} %squeeze.12) | copy-start | bytes 221188
  22.3 15.3 %copy-start.7 = (bf16[192,192]{1,0:T(8,128)(2,1)}, bf16[192,192]{1,0:T(8,128)(2,1)S(1)}, u32[]{:S(2)}) copy-start(bf16[192,192]{1,0:T(8,128)(2,1)S(1)} %squeeze.13) | copy-start | bytes 221188
  22.4 16.2 %copy-start.21 = (bf16[192,192]{1,0:T(8,128)(2,1)}, bf16[192,192]{1,0:T(8,128)(2,1)S(1)}, u32[]{:S(2)}) copy-start(bf16[192,192]{1,0:T(8,128)(2,1)S(1)} %squeeze.14) | copy-start | bytes 221188
  39.9 23.8 %all-to-all-start.2 = ((bf16[8,192,512]{2,1,0:T(8,128)(2,1)}), bf16[8,192,512]{2,1,0:T(8,128)(2,1)S(1)}, u32[]{:S(2)}, u32[]{:S(2)}) async-start(bf16[8,192,512]{2,1,0:T(8,128)(2,1)} %broadcast_in_dim.7), calls=%async_computation.2 | async-start | bytes 3145728 | tf_op jit(solution)/shard_map/all_to_all | solution.py:20
  49.7 18.8 %copy-start.19 = (bf16[1,110592]{1,0:T(2,128)(2,1)S(1)}, bf16[1,110592]{1,0:T(2,128)(2,1)}, u32[]{:S(2)}) copy-start(bf16[1,110592]{1,0:T(2,128)(2,1)} %param.12) | copy-start | bytes 663556
  63.7 31.5 %all-to-all-start.1 = ((bf16[8,192,704]{2,1,0:T(8,128)(2,1)}), bf16[8,192,704]{2,1,0:T(8,128)(2,1)}, u32[]{:S(2)}, u32[]{:S(2)}) async-start(bf16[8,192,704]{2,1,0:T(8,128)(2,1)} %pad_maximum_fusion), calls=%async_computation.1 | async-start | bytes 4718592 | tf_op jit(solution)/shard_map/all_to_all | solution.py:20
  112.3 3.4 %copy-start.1 = (bf16[2,32,36,128]{3,2,1,0:T(8,128)(2,1)S(1)}, bf16[2,32,36,128]{3,2,1,0:T(8,128)(2,1)}, u32[]{:S(2)}) copy-start(bf16[2,32,36,128]{3,2,1,0:T(8,128)(2,1)} %reshape.126) | copy-start | bytes 1769476
  112.3 3.4 %copy-start.6 = (bf16[2,32,14,128]{3,2,1,0:T(8,128)(2,1)S(1)}, bf16[2,32,14,128]{3,2,1,0:T(8,128)(2,1)}, u32[]{:S(2)}) copy-start(bf16[2,32,14,128]{3,2,1,0:T(8,128)(2,1)} %reshape.127) | copy-start | bytes 688132
  116.3 7.7 %collective-permute-start = (bf16[32,86,128]{2,0,1:T(8,128)(2,1)S(1)}, bf16[32,86,128]{2,0,1:T(8,128)(2,1)S(1)}, u32[]{:S(2)}, u32[]{:S(2)}) collective-permute-start(bf16[32,86,128]{2,0,1:T(8,128)(2,1)S(1)} %copy.54), channel_id=1, source_target_pairs={{0,8},{8,0},{1,9},{9,1},{2,10},{10,2},{3,11},{11,3},{4,12},{12,4},... | collective-permute-start | bytes 2113544 | tf_op jit(solution)/shard_map/ppermute | solution.py:50
  125.3 28.2 %all-to-all-start.5 = ((bf16[32,86,128]{2,1,0:T(8,128)(2,1)}), bf16[32,86,128]{2,1,0:T(8,128)(2,1)S(1)}, u32[]{:S(2)}, u32[]{:S(2)}) async-start(bf16[32,86,128]{2,1,0:T(8,128)(2,1)} %fusion.1), calls=%async_computation.5 | async-start | bytes 1441792 | tf_op jit(solution)/shard_map/all_to_all | solution.py:20
  153.5 21.9 %all-to-all-start.3 = ((bf16[8,192,512]{2,1,0:T(8,128)(2,1)}), bf16[8,192,512]{2,1,0:T(8,128)(2,1)S(1)}, u32[]{:S(2)}, u32[]{:S(2)}) async-start(bf16[8,192,512]{2,1,0:T(8,128)(2,1)} %bitcast.11), calls=%async_computation.3 | async-start | bytes 3145728 | tf_op jit(solution)/shard_map/all_to_all | solution.py:20
  157.4 19.1 %copy-start.5 = (bf16[192,480]{1,0:T(8,128)(2,1)S(1)}, bf16[192,480]{1,0:T(8,128)(2,1)}, u32[]{:S(2)}) copy-start(bf16[192,480]{1,0:T(8,128)(2,1)} %copy-done.4) | copy-start | bytes 552964
  157.4 19.4 %copy-start.16 = (bf16[192,480]{1,0:T(8,128)(2,1)S(1)}, bf16[192,480]{1,0:T(8,128)(2,1)}, u32[]{:S(2)}) copy-start(bf16[192,480]{1,0:T(8,128)(2,1)} %copy-done.15) | copy-start | bytes 552964
  178.0 11.3 %collective-permute-start.1 = (bf16[32,14,128]{2,1,0:T(8,128)(2,1)S(1)}, bf16[32,14,128]{2,1,0:T(8,128)(2,1)S(1)}, u32[]{:S(2)}, u32[]{:S(2)}) collective-permute-start(bf16[32,14,128]{2,1,0:T(8,128)(2,1)S(1)} %select_n.52), channel_id=1, source_target_pairs={{0,8},{8,0},{1,9},{9,1},{2,10},{10,2},{3,11},{11,3},{4,12},{12,4},... | collective-permute-start | bytes 344072 | tf_op jit(solution)/shard_map/ppermute | solution.py:50
  185.9 8.3 %all-to-all-start.6 = ((bf16[8,2,288]{2,1,0:T(2,128)(2,1)}), bf16[8,2,288]{2,1,0:T(2,128)(2,1)S(1)}, u32[]{:S(2)}, u32[]{:S(2)}) async-start(bf16[8,2,288]{2,1,0:T(2,128)(2,1)} %reshape.145), calls=%async_computation.6 | async-start | bytes 24576 | tf_op jit(solution)/shard_map/all_to_all | solution.py:20
  194.3 20.4 %all-to-all-start.7 = ((bf16[32,14,128]{2,1,0:T(8,128)(2,1)}), bf16[32,14,128]{2,1,0:T(8,128)(2,1)S(1)}, u32[]{:S(2)}, u32[]{:S(2)}) async-start(bf16[32,14,128]{2,1,0:T(8,128)(2,1)} %add_convert_fusion), calls=%async_computation.7 | async-start | bytes 262144 | tf_op jit(solution)/shard_map/all_to_all | solution.py:20
  214.7 5.2 %copy-start.13 = (bf16[192,192]{1,0:T(8,128)(2,1)S(1)}, bf16[192,192]{1,0:T(8,128)(2,1)}, u32[]{:S(2)}) copy-start(bf16[192,192]{1,0:T(8,128)(2,1)} %copy-done.12) | copy-start | bytes 221188
  215.8 4.4 %copy-start.8 = (bf16[192,192]{1,0:T(8,128)(2,1)S(1)}, bf16[192,192]{1,0:T(8,128)(2,1)}, u32[]{:S(2)}) copy-start(bf16[192,192]{1,0:T(8,128)(2,1)} %copy-done.7) | copy-start | bytes 221188
  215.8 24.8 %all-to-all-start.8 = ((bf16[32,100,128]{2,1,0:T(8,128)(2,1)}), bf16[32,100,128]{2,1,0:T(8,128)(2,1)S(1)}, u32[]{:S(2)}, u32[]{:S(2)}) async-start(bf16[32,100,128]{2,1,0:T(8,128)(2,1)} %broadcast_in_dim.8), calls=%async_computation.8 | async-start | bytes 1703936 | tf_op jit(solution)/shard_map/all_to_all | solution.py:20
  220.0 29.1 %copy-start.22 = (bf16[192,192]{1,0:T(8,128)(2,1)S(1)}, bf16[192,192]{1,0:T(8,128)(2,1)}, u32[]{:S(2)}) copy-start(bf16[192,192]{1,0:T(8,128)(2,1)} %copy-done.21) | copy-start | bytes 221188
  241.6 28.5 %collective-permute-start.2 = (bf16[32,100,128]{2,0,1:T(8,128)(2,1)}, bf16[32,100,128]{2,0,1:T(8,128)(2,1)S(1)}, u32[]{:S(2)}, u32[]{:S(2)}) collective-permute-start(bf16[32,100,128]{2,0,1:T(8,128)(2,1)} %copy.59), channel_id=1, source_target_pairs={{0,8},{8,0},{1,9},{9,1},{2,10},{10,2},{3,11},{11,3},{4,12},{12,4},... | collective-permute-start | bytes 2457608 | tf_op jit(solution)/shard_map/ppermute | solution.py:50
  (11 other events, 18.3 us)

commit v2 on v1

--- a/solution.py
+++ b/solution.py
@@ -8,7 +8,6 @@
 F32 = jnp.float32
 SEQ = ("zh", "yh", "yl", "core")
 GRP = ("x", "zl")
-SAME = ("zh", "yh")
 CHIPS = ("zh", "yh", "yl")
 
 
@@ -57,17 +56,6 @@
     return (mine.astype(F32) + got.astype(F32)).astype(BF)
 
 
-def chips_sum(half, scale):
-    return (jnp.sum(swap(half, CHIPS).astype(F32), axis=0) * scale).astype(BF)
-
-
-def chips_spread(piece):
-    everyone = swap(jnp.broadcast_to(piece[None], (32,) + piece.shape), CHIPS)
-    other = other_core(everyone)
-    first = lax.axis_index("core") == 0
-    return jnp.concatenate([jnp.where(first, everyone, other), jnp.where(first, other, everyone)], axis=0)
-
-
 def conv_rows(grad):
     rows = grad.astype(BF).reshape(864, 128)
     return jnp.pad(rows, ((0, 32), (0, 0))).reshape(2, 32, 14, 128)
@@ -89,8 +77,8 @@
         lax.broadcasted_iota(jnp.int32, (CG, CG), 0) == lax.broadcasted_iota(jnp.int32, (CG, CG), 1)
     ).astype(BF)
     start_t = mm(onehot, emb, 0, 1).astype(BF)
-    packed = jnp.concatenate([start_t, cot.T], axis=1).reshape(16, cols // 16, 2 * CG)
-    packed = swap(packed, SAME).reshape(cols, 2 * CG)
+    packed = jnp.concatenate([start_t, cot.T], axis=1).reshape(32, cols // 32, 2 * CG)
+    packed = swap(packed, CHIPS).reshape(cols, 2 * CG)
     start = mm(eye, packed[:, :CG], 1, 1).astype(BF)
     cotq = mm(eye, packed[:, CG:], 1, 1).astype(BF)
 
@@ -119,24 +107,28 @@
     pg2 = pg2.reshape(8, 2, 32, 3 * CG).transpose(1, 2, 0, 3).reshape(2, 32, 36, 128)
     pg1 = mm(grad_middle, act_all, 1, 1).astype(BF).reshape(2, 32, 36, 128)
     cg2 = conv_rows(conv_grad(middle, far_dh, 64))
-    early = chips_sum(core_sum(jnp.concatenate([pg1, pg2, cg2], axis=2)), scale)
-    piece2 = swap(early[36:72].reshape(8, 3 * CG), GRP)
-    piece2 = piece2.reshape(8, 3, CG).transpose(1, 0, 2).reshape(36, 128)
+    early = core_sum(jnp.concatenate([pg1, pg2, cg2], axis=2))
 
     near_s = jax.nn.sigmoid(near_hidden)
     near_dh = (near_da * near_s * (1.0 + near_hidden * (1.0 - near_s))).astype(BF)
     grad_start = (grad_middle.astype(F32) + conv_back(near_dh, w1, 32)).astype(BF)
     cg1 = conv_rows(conv_grad(start, near_dh, 32))
-    late = chips_sum(core_sum(cg1), scale)
-    whole = chips_spread(jnp.concatenate([early[:36], piece2, early[72:], late], axis=0))
+    late = core_sum(cg1)
+    back = mm(grad_start, eye, 0, 0).astype(BF).reshape(32, cols * CG // 32 // 128, 128)
+    got = swap(jnp.concatenate([early, late, back], axis=1), CHIPS)
+    piece = (jnp.sum(got[:, :100].astype(F32), axis=0) * scale).astype(BF)
+    piece2 = swap(piece[36:72].reshape(8, 3 * CG), GRP)
+    piece2 = piece2.reshape(8, 3, CG).transpose(1, 0, 2).reshape(36, 128)
+    piece = jnp.concatenate([piece[:36], piece2, piece[72:]], axis=0)
+    everyone = swap(jnp.broadcast_to(piece[None], (32, 100, 128)), CHIPS)
+    other = other_core(everyone)
+    first = lax.axis_index("core") == 0
+    whole = jnp.concatenate([jnp.where(first, everyone, other), jnp.where(first, other, everyone)], axis=0)
     out_pg1 = whole[:, :36].reshape(CG, 8 * CG)
     out_pg2 = whole[:, 36:72].reshape(CG, 8 * CG)
     out_cg2 = conv_flat(whole[:, 72:86])
     out_cg1 = conv_flat(whole[:, 86:])
-
-    back = mm(grad_start, eye, 0, 0).astype(BF).reshape(16, cols // 16, CG)
-    back = swap(back, SAME).reshape(cols, CG)
-    emb_grad = mm(back, onehot, 0, 1).astype(BF)
+    emb_grad = mm(got[:, 100:].reshape(cols, CG), onehot, 0, 1).astype(BF)
     return emb_grad, out_cg1, out_pg1, out_cg2, out_pg2
 
 

time: 278 us -> 237 us (0.85)
  waiting for transfers between devices: 125 us -> 56.4 us
  blocking collectives: 19.4 us -> 64.9 us
  starting transfers between devices: 72.6 us -> 53.3 us
    all_to_all x8 -> x5, waiting for transfers between devices: 123 us -> 54 us  [swap(): return lax.all_to_all(blocks, axes, 0, 0, tiled=True)]
    all_to_all x1 -> x2, blocking collectives: 19.4 us -> 64.9 us  [swap(): return lax.all_to_all(blocks, axes, 0, 0, tiled=True)]
    all_to_all x8 -> x5, starting transfers between devices: 53.3 us -> 37.6 us  [swap(): return lax.all_to_all(blocks, axes, 0, 0, tiled=True)]
    ppermute x3, starting transfers between devices: 19.2 us -> 15.7 us  [other_core(): return lax.ppermute(values, 'core', [(0, 1), (1, 0)])]
  transfers between devices with their start and end apart: 11 -> 8, of which waited for: 9 -> 6; matrix products, arithmetic and copies ran while one was open for 6% -> 12% of each run, Pallas kernels for 0% -> 0%
where the time goes in v2:
time: 237 us; the launch traced here: 234 us
  blocking collectives  64.9 us (27%)
  waiting for transfers between devices  56.4 us (24%)
  starting transfers between devices  53.3 us (22%)
  local copies, waits for them, and re-layouts  30.1 us (13%)
  matrix products  18.1 us (8%)
  other arithmetic  10.1 us (4%)
    all_to_all x2, blocking collectives, swap(): return lax.all_to_all(blocks, axes, 0, 0, tiled=True)  64.9 us
    all_to_all x5, waiting for transfers between devices, swap(): return lax.all_to_all(blocks, axes, 0, 0, tiled=True)  54 us
    all_to_all x5, starting transfers between devices, swap(): return lax.all_to_all(blocks, axes, 0, 0, tiled=True)  37.6 us
    dot_general x27, matrix products, mm(): lax.dot_general(a, b, (((ca,), (cb,)), ((), ())), preferred_element_type=...  18.1 us
    ppermute x3, starting transfers between devices, other_core(): return lax.ppermute(values, 'core', [(0, 1), (1, 0)])  15.7 us
  transfers between devices with their start and end apart: 8, of which 6 were waited for; matrix products, arithmetic and copies ran while one was open for 12% of the time, Pallas kernels for 0%

profile of v2, /device:TPU:1, one launch (start us, length us, event | category | flops | bytes accessed | tf_op | source)
XLA Modules:
  0.0 234.2 jit_solution(16306964019183318489)
XLA Ops:
  4.6 16.5 %all-to-all-start = ((bf16[32,16,384]{2,1,0:T(8,128)(2,1)}), bf16[32,16,384]{2,1,0:T(8,128)(2,1)S(1)}, u32[]{:S(2)}, u32[]{:S(2)}) async-start(bf16[32,16,384]{2,1,0:T(8,128)(2,1)} %bitcast.1), calls=%async_computation | async-start | bytes 786432 | tf_op jit(solution)/shard_map/all_to_all | solution.py:19
  22.7 13.0 %all-to-all-done = bf16[32,16,384]{2,1,0:T(8,128)(2,1)S(1)} async-done(((bf16[32,16,384]{2,1,0:T(8,128)(2,1)}), bf16[32,16,384]{2,1,0:T(8,128)(2,1)S(1)}, u32[]{:S(2)}, u32[]{:S(2)}) %all-to-all-start) | async-done | bytes 393248 | tf_op jit(solution)/shard_map/all_to_all | solution.py:19
  39.0 4.9 %all-to-all-start.2 = ((bf16[8,192,512]{2,1,0:T(8,128)(2,1)}), bf16[8,192,512]{2,1,0:T(8,128)(2,1)S(1)}, u32[]{:S(2)}, u32[]{:S(2)}) async-start(bf16[8,192,512]{2,1,0:T(8,128)(2,1)} %broadcast_in_dim.7), calls=%async_computation.2 | async-start | bytes 3145728 | tf_op jit(solution)/shard_map/all_to_all | solution.py:19
  43.9 1.7 reshape.118
  46.3 1.6 pad_maximum_fusion
  48.0 14.0 %all-to-all-done.2 = bf16[8,192,512]{2,1,0:T(8,128)(2,1)S(1)} async-done(((bf16[8,192,512]{2,1,0:T(8,128)(2,1)}), bf16[8,192,512]{2,1,0:T(8,128)(2,1)S(1)}, u32[]{:S(2)}, u32[]{:S(2)}) %all-to-all-start.2) | async-done | bytes 1572896 | tf_op jit(solution)/shard_map/all_to_all | solution.py:19
  61.9 4.5 %all-to-all-start.1 = ((bf16[8,192,704]{2,1,0:T(8,128)(2,1)}), bf16[8,192,704]{2,1,0:T(8,128)(2,1)}, u32[]{:S(2)}, u32[]{:S(2)}) async-start(bf16[8,192,704]{2,1,0:T(8,128)(2,1)} %pad_maximum_fusion), calls=%async_computation.1 | async-start | bytes 4718592 | tf_op jit(solution)/shard_map/all_to_all | solution.py:19
  70.2 22.0 %all-to-all-done.1 = bf16[8,192,704]{2,1,0:T(8,128)(2,1)} async-done(((bf16[8,192,704]{2,1,0:T(8,128)(2,1)}), bf16[8,192,704]{2,1,0:T(8,128)(2,1)}, u32[]{:S(2)}, u32[]{:S(2)}) %all-to-all-start.1) | async-done | bytes 2162720 | tf_op jit(solution)/shard_map/all_to_all | solution.py:19
  92.2 2.2 fusion.19
  95.7 1.8 fusion
  97.5 2.6 %copy.54 = bf16[1536,512]{1,0:T(8,128)(2,1)} copy(bf16[1536,512]{0,1:T(8,128)(2,1)} %fusion) | data formatting | bytes 3145728 | tf_op jit(solution)/shard_map/convert_element_type | solution.py:102
  100.1 5.6 %all-to-all-start.3 = ((bf16[8,192,512]{2,1,0:T(8,128)(2,1)}), bf16[8,192,512]{2,1,0:T(8,128)(2,1)}, u32[]{:S(2)}, u32[]{:S(2)}) async-start(bf16[8,192,512]{2,1,0:T(8,128)(2,1)} %bitcast.76), calls=%async_computation.3 | async-start | bytes 3145728 | tf_op jit(solution)/shard_map/all_to_all | solution.py:19
  107.8 3.0 %convolution_convert_fusion.1 = bf16[1536,192]{0,1:T(8,128)(2,1)} fusion(bf16[1536,704]{1,0:T(8,128)(2,1)} %bitcast.4, f32[192,512]{1,0:T(8,128)} %fusion.11), kind=kOutput, calls=%fused_computation.3 | convolution fusion | flops 302776320 | bytes 2555904 | tf_op jit(solution)/shard_map/dot_general | solution.py:15
  115.2 1.7 reshape.123
  118.4 1.8 reshape.121
  121.8 5.8 %collective-permute-start = (bf16[32,86,128]{2,0,1:T(8,128)(2,1)S(1)}, bf16[32,86,128]{2,0,1:T(8,128)(2,1)S(1)}, u32[]{:S(2)}, u32[]{:S(2)}) collective-permute-start(bf16[32,86,128]{2,0,1:T(8,128)(2,1)S(1)} %copy.52), channel_id=1, source_target_pairs={{0,8},{8,0},{1,9},{9,1},{2,10},{10,2},{3,11},{11,3},{4,12},{12,4},... | collective-permute-start | bytes 2113544 | tf_op jit(solution)/shard_map/ppermute | solution.py:49
  127.7 1.8 collective-permute-done
  129.8 1.7 convert_reduce_fusion
  134.0 2.3 collective-permute-start.1
  139.0 35.3 %all_to_all.40 = bf16[32,124,128]{2,1,0:T(8,128)(2,1)S(1)} all-to-all(bf16[32,124,128]{2,1,0:T(8,128)(2,1)S(1)} %pad_maximum_fusion.2), channel_id=1, replica_groups=mesh['zh'=4,'yh'=4,'yl'=2,'core'=2,'x'=4,'zl'=2] {'zh','yh','yl'}, dimensions={0} | all-to-all | bytes 2031616 | tf_op jit(solution)/shard_map/all_to_all | solution.py:19
  176.4 6.2 %all-to-all-start.5 = ((bf16[8,2,288]{2,1,0:T(2,128)(2,1)}), bf16[8,2,288]{2,1,0:T(2,128)(2,1)S(1)}, u32[]{:S(2)}, u32[]{:S(2)}) async-start(bf16[8,2,288]{2,1,0:T(2,128)(2,1)} %reshape.145), calls=%async_computation.5 | async-start | bytes 24576 | tf_op jit(solution)/shard_map/all_to_all | solution.py:19
  182.6 5.0 %all-to-all-done.5 = bf16[8,2,288]{2,1,0:T(2,128)(2,1)S(1)} async-done(((bf16[8,2,288]{2,1,0:T(2,128)(2,1)}), bf16[8,2,288]{2,1,0:T(2,128)(2,1)S(1)}, u32[]{:S(2)}, u32[]{:S(2)}) %all-to-all-start.5) | async-done | bytes 9248 | tf_op jit(solution)/shard_map/all_to_all | solution.py:19
  188.2 29.6 %all_to_all.41 = bf16[32,100,128]{2,1,0:T(8,128)(2,1)S(1)} all-to-all(bf16[32,100,128]{2,1,0:T(8,128)(2,1)S(1)} %broadcast_in_dim.8), channel_id=1, replica_groups=mesh['zh'=4,'yh'=4,'yl'=2,'core'=2,'x'=4,'zl'=2] {'zh','yh','yl'}, dimensions={0} | all-to-all | bytes 1638400 | tf_op jit(solution)/shard_map/all_to_all | solution.py:19
  218.8 7.6 %collective-permute-start.2 = (bf16[32,100,128]{2,0,1:T(8,128)(2,1)}, bf16[32,100,128]{2,0,1:T(8,128)(2,1)S(1)}, u32[]{:S(2)}, u32[]{:S(2)}) collective-permute-start(bf16[32,100,128]{2,0,1:T(8,128)(2,1)} %copy.59), channel_id=1, source_target_pairs={{0,8},{8,0},{1,9},{9,1},{2,10},{10,2},{3,11},{11,3},{4,12},{12,4},... | collective-permute-start | bytes 2457608 | tf_op jit(solution)/shard_map/ppermute | solution.py:49
  (131 shorter events, 40.7 us)
Async XLA Ops:
  0.6 67.4 %copy-start = (bf16[192,1536]{1,0:T(8,128)(2,1)S(1)}, bf16[192,1536]{1,0:T(8,128)(2,1)}, u32[]{:S(2)}) copy-start(bf16[192,1536]{1,0:T(8,128)(2,1)} %param.11) | copy-start | bytes 1769476
  0.6 20.4 %copy-start.12 = (bf16[1,110592]{1,0:T(2,128)(2,1)S(1)}, bf16[1,110592]{1,0:T(2,128)(2,1)}, u32[]{:S(2)}) copy-start(bf16[1,110592]{1,0:T(2,128)(2,1)} %param.10) | copy-start | bytes 663556
  4.6 31.1 %all-to-all-start = ((bf16[32,16,384]{2,1,0:T(8,128)(2,1)}), bf16[32,16,384]{2,1,0:T(8,128)(2,1)S(1)}, u32[]{:S(2)}, u32[]{:S(2)}) async-start(bf16[32,16,384]{2,1,0:T(8,128)(2,1)} %bitcast.1), calls=%async_computation | async-start | bytes 786432 | tf_op jit(solution)/shard_map/all_to_all | solution.py:19
  22.5 14.2 %copy-start.8 = (bf16[192,192]{1,0:T(8,128)(2,1)}, bf16[192,192]{1,0:T(8,128)(2,1)S(1)}, u32[]{:S(2)}) copy-start(bf16[192,192]{1,0:T(8,128)(2,1)S(1)} %squeeze.12) | copy-start | bytes 221188
  22.6 14.1 %copy-start.4 = (bf16[192,192]{1,0:T(8,128)(2,1)}, bf16[192,192]{1,0:T(8,128)(2,1)S(1)}, u32[]{:S(2)}) copy-start(bf16[192,192]{1,0:T(8,128)(2,1)S(1)} %squeeze.13) | copy-start | bytes 221188
  22.7 15.0 %copy-start.14 = (bf16[192,192]{1,0:T(8,128)(2,1)}, bf16[192,192]{1,0:T(8,128)(2,1)S(1)}, u32[]{:S(2)}) copy-start(bf16[192,192]{1,0:T(8,128)(2,1)S(1)} %squeeze.14) | copy-start | bytes 221188
  36.1 1.6 copy-start.2
  36.1 1.6 copy-start.10
  39.0 22.9 %all-to-all-start.2 = ((bf16[8,192,512]{2,1,0:T(8,128)(2,1)}), bf16[8,192,512]{2,1,0:T(8,128)(2,1)S(1)}, u32[]{:S(2)}, u32[]{:S(2)}) async-start(bf16[8,192,512]{2,1,0:T(8,128)(2,1)} %broadcast_in_dim.7), calls=%async_computation.2 | async-start | bytes 3145728 | tf_op jit(solution)/shard_map/all_to_all | solution.py:19
  48.0 18.4 %copy-start.13 = (bf16[1,110592]{1,0:T(2,128)(2,1)S(1)}, bf16[1,110592]{1,0:T(2,128)(2,1)}, u32[]{:S(2)}) copy-start(bf16[1,110592]{1,0:T(2,128)(2,1)} %param.12) | copy-start | bytes 663556
  61.9 30.3 %all-to-all-start.1 = ((bf16[8,192,704]{2,1,0:T(8,128)(2,1)}), bf16[8,192,704]{2,1,0:T(8,128)(2,1)}, u32[]{:S(2)}, u32[]{:S(2)}) async-start(bf16[8,192,704]{2,1,0:T(8,128)(2,1)} %pad_maximum_fusion), calls=%async_computation.1 | async-start | bytes 4718592 | tf_op jit(solution)/shard_map/all_to_all | solution.py:19
  68.0 1.2 copy-start.6
  100.1 29.7 %all-to-all-start.3 = ((bf16[8,192,512]{2,1,0:T(8,128)(2,1)}), bf16[8,192,512]{2,1,0:T(8,128)(2,1)}, u32[]{:S(2)}, u32[]{:S(2)}) async-start(bf16[8,192,512]{2,1,0:T(8,128)(2,1)} %bitcast.76), calls=%async_computation.3 | async-start | bytes 3145728 | tf_op jit(solution)/shard_map/all_to_all | solution.py:19
  117.0 3.3 %copy-start.1 = (bf16[2,32,36,128]{3,2,1,0:T(8,128)(2,1)S(1)}, bf16[2,32,36,128]{3,2,1,0:T(8,128)(2,1)}, u32[]{:S(2)}) copy-start(bf16[2,32,36,128]{3,2,1,0:T(8,128)(2,1)} %reshape.123) | copy-start | bytes 1769476
  121.8 7.6 %collective-permute-start = (bf16[32,86,128]{2,0,1:T(8,128)(2,1)S(1)}, bf16[32,86,128]{2,0,1:T(8,128)(2,1)S(1)}, u32[]{:S(2)}, u32[]{:S(2)}) collective-permute-start(bf16[32,86,128]{2,0,1:T(8,128)(2,1)S(1)} %copy.52), channel_id=1, source_target_pairs={{0,8},{8,0},{1,9},{9,1},{2,10},{10,2},{3,11},{11,3},{4,12},{12,4},... | collective-permute-start | bytes 2113544 | tf_op jit(solution)/shard_map/ppermute | solution.py:49
  129.8 1.8 copy-start.16
  129.8 1.9 copy-start.3
  129.8 2.2 copy-start.11
  132.5 3.8 %copy-start.9 = (bf16[192,192]{1,0:T(8,128)(2,1)S(1)}, bf16[192,192]{1,0:T(8,128)(2,1)}, u32[]{:S(2)}) copy-start(bf16[192,192]{1,0:T(8,128)(2,1)} %copy-done.8) | copy-start | bytes 221188
  132.6 3.9 %copy-start.5 = (bf16[192,192]{1,0:T(8,128)(2,1)S(1)}, bf16[192,192]{1,0:T(8,128)(2,1)}, u32[]{:S(2)}) copy-start(bf16[192,192]{1,0:T(8,128)(2,1)} %copy-done.4) | copy-start | bytes 221188
  132.9 3.8 %copy-start.15 = (bf16[192,192]{1,0:T(8,128)(2,1)S(1)}, bf16[192,192]{1,0:T(8,128)(2,1)}, u32[]{:S(2)}) copy-start(bf16[192,192]{1,0:T(8,128)(2,1)} %copy-done.14) | copy-start | bytes 221188
  134.0 3.7 %collective-permute-start.1 = (bf16[32,14,128]{2,1,0:T(8,128)(2,1)}, bf16[32,14,128]{2,1,0:T(8,128)(2,1)}, u32[]{:S(2)}, u32[]{:S(2)}) collective-permute-start(bf16[32,14,128]{2,1,0:T(8,128)(2,1)} %select_n.51), channel_id=1, source_target_pairs={{0,8},{8,0},{1,9},{9,1},{2,10},{10,2},{3,11},{11,3},{4,12},{12,4},... | collective-permute-start | bytes 344072 | tf_op jit(solution)/shard_map/ppermute | solution.py:49
  176.4 11.2 %all-to-all-start.5 = ((bf16[8,2,288]{2,1,0:T(2,128)(2,1)}), bf16[8,2,288]{2,1,0:T(2,128)(2,1)S(1)}, u32[]{:S(2)}, u32[]{:S(2)}) async-start(bf16[8,2,288]{2,1,0:T(2,128)(2,1)} %reshape.145), calls=%async_computation.5 | async-start | bytes 24576 | tf_op jit(solution)/shard_map/all_to_all | solution.py:19
  218.8 9.5 %collective-permute-start.2 = (bf16[32,100,128]{2,0,1:T(8,128)(2,1)}, bf16[32,100,128]{2,0,1:T(8,128)(2,1)S(1)}, u32[]{:S(2)}, u32[]{:S(2)}) collective-permute-start(bf16[32,100,128]{2,0,1:T(8,128)(2,1)} %copy.59), channel_id=1, source_target_pairs={{0,8},{8,0},{1,9},{9,1},{2,10},{10,2},{3,11},{11,3},{4,12},{12,4},... | collective-permute-start | bytes 2457608 | tf_op jit(solution)/shard_map/ppermute | solution.py:49
  (1 other events, 0.9 us)

commit v3 on v2

v3 whole, which is shorter than its diff:
```python
import jax
import jax.numpy as jnp
from jax import lax
from jax.experimental import pallas as pl
from jax.experimental.pallas import tpu as pltpu
from jax.sharding import Mesh, PartitionSpec as P

CG = 192
TOK = 512
NEAR = 32
FAR = 64
BF = jnp.bfloat16
F32 = jnp.float32
SEQ = ("zh", "yh", "yl", "core")
GRP = ("x", "zl")
CHIPS = ("zh", "yh", "yl")
SCALE = float(32768) ** (-0.5)
ROWS = 104


def mm(a, b, ca, cb):
    return lax.dot_general(a, b, (((ca,), (cb,)), ((), ())), preferred_element_type=F32)


def swap(blocks, axes):
    return lax.all_to_all(blocks, axes, 0, 0, tiled=True)


def other_core(values):
    return lax.ppermute(values, "core", [(0, 1), (1, 0)])


def call(kernel, outs, scalars, *arrays, scratch=()):
    vmem = pl.BlockSpec(memory_space=pltpu.VMEM)
    smem = pl.BlockSpec(memory_space=pltpu.SMEM)
    return pl.pallas_call(
        kernel,
        out_shape=[jax.ShapeDtypeStruct(shape, dtype) for shape, dtype in outs],
        in_specs=[smem] * len(scalars) + [vmem] * len(arrays),
        out_specs=[vmem] * len(outs),
        scratch_shapes=[pltpu.VMEM(shape, dtype) for shape, dtype in scratch],
        compiler_params=pltpu.CompilerParams(vmem_limit_bytes=48 * 1024 * 1024),
    )(*scalars, *arrays)


def shifted(values, by):
    if by == 0:
        return values.astype(BF)
    lane = lax.broadcasted_iota(jnp.int32, values.shape, 1)
    rolled = pltpu.roll(values, (-by) % TOK, 1)
    keep = lane < TOK - by if by > 0 else lane >= -by
    return jnp.where(keep, rolled, 0.0).astype(BF)


def conv_back(grads, weight_ref, by):
    return (
        mm(weight_ref[0], shifted(grads, by), 1, 0)
        + mm(weight_ref[1], shifted(grads, 0), 1, 0)
        + mm(weight_ref[2], shifted(grads, -by), 1, 0)
    )


def conv_rows(values, grads, by, rows_ref):
    row = lax.broadcasted_iota(jnp.int32, (CG, CG), 0)
    col = lax.broadcasted_iota(jnp.int32, (CG, CG), 1)
    half = CG // 2
    source = jnp.where(row < half, 2 * row, 2 * row - (CG - 1))
    order = jnp.where(col == source, 1.0, 0.0).astype(BF)
    for tap, distance in enumerate((-by, 0, by)):
        moved = mm(order, shifted(values, distance), 1, 0).astype(BF)
        grad = mm(moved, grads, 1, 1)
        even, odd = grad[:half], grad[half:]
        base = 3 * half * tap
        rows_ref[base : base + half] = even[:, :128]
        rows_ref[base + half : base + 2 * half] = jnp.concatenate([even[:, 128:], odd[:, :64]], axis=1)
        rows_ref[base + 2 * half : base + 3 * half] = odd[:, 64:]


def pack_kernel(base_ref, order_ref, emb_ref, cot_ref, out_ref):
    token = lax.broadcasted_iota(jnp.int32, (TOK, TOK), 0)
    onehot = jnp.where(token == order_ref[...] - base_ref[0], 1.0, 0.0).astype(BF)
    start = mm(emb_ref[...], onehot, 1, 0)
    both = jnp.concatenate([start, cot_ref[...].astype(F32)], axis=0)
    out_ref[...] = both.T.astype(BF)


def near_kernel(tokens_ref, weight_ref, act_ref, hidden_ref, start_ref, cot_ref):
    rows = tokens_ref[...].astype(F32)
    both = rows.T
    start_ref[...] = both[:CG].astype(BF)
    cot_ref[...] = both[CG:].astype(BF)
    start = rows[:, :CG]
    filler = jnp.zeros((NEAR, CG), F32)
    before = jnp.concatenate([filler, start[: TOK - NEAR]], axis=0).astype(BF)
    after = jnp.concatenate([start[NEAR:], filler], axis=0).astype(BF)
    hidden = (
        mm(weight_ref[0], before, 1, 1)
        + mm(weight_ref[1], start.astype(BF), 1, 1)
        + mm(weight_ref[2], after, 1, 1)
    )
    hidden_ref[...] = hidden
    act = (hidden * jax.nn.sigmoid(hidden)).astype(BF)
    for j in range(8):
        act_ref[j] = act


def regroup_kernel(core_ref, sent_ref, act_ref, mine_ref, other_ref, grad_ref):
    for j in range(8):
        grad_ref[j * CG : (j + 1) * CG] = mm(sent_ref[j, :, :TOK], act_ref[...], 1, 1)
    blank = jnp.zeros((8, 64), F32)
    for out_ref, core in ((mine_ref, core_ref[0]), (other_ref, 1 - core_ref[0])):
        for j in range(8):
            for part in range(4):
                piece = grad_ref[pl.ds(pl.multiple_of(j * CG + 96 * core + 24 * part, 8), 24)]
                rest = piece[:, 128:]
                at = 40 * part
                out_ref[j, at : at + 24] = piece[:, :128].astype(out_ref.dtype)
                out_ref[j, at + 24 : at + 32] = jnp.concatenate([rest[:8], rest[8:16]], axis=1).astype(out_ref.dtype)
                out_ref[j, at + 32 : at + 40] = jnp.concatenate([rest[16:], blank], axis=1).astype(out_ref.dtype)


def far_kernel(sent_ref, hidden_ref, cot_ref, weight_ref, dh_ref, grad_ref):
    da = sum(mm(sent_ref[j, :, TOK:], sent_ref[j, :, :TOK], 0, 0) for j in range(8))
    hidden = hidden_ref[...]
    s = jax.nn.sigmoid(hidden)
    dh = (da * s * (1.0 + hidden * (1.0 - s))).astype(BF)
    dh_ref[...] = dh
    back = conv_back(dh.astype(F32), weight_ref, FAR)
    grad_ref[...] = (cot_ref[...].astype(F32) + back).astype(BF)


def parts_kernel(grad_ref, pointwise_ref, mine_ref, other_ref, out_ref):
    grad = grad_ref[...]
    for j in range(8):
        out_ref[j, :, :TOK] = mm(pointwise_ref[j * CG : (j + 1) * CG], grad, 1, 0).astype(BF)
        out_ref[j, :160, TOK:] = (mine_ref[j] + other_ref[j].astype(F32)).astype(BF)
        out_ref[j, 160:, TOK:] = jnp.zeros((32, 128), BF)


def early_kernel(core_ref, grad_ref, act_ref, middle_ref, dh_ref, mine_ref, other_ref, rows_ref):
    conv_rows(middle_ref[...].astype(F32), dh_ref[...], FAR, rows_ref)
    for out_ref, core in ((mine_ref, core_ref[0]), (other_ref, 1 - core_ref[0])):
        acts = act_ref[pl.ds(pl.multiple_of(768 * core, 128), 768)]
        grad = mm(grad_ref[...], acts, 1, 1)
        for j in range(6):
            out_ref[CG * j : CG * (j + 1)] = grad[:, 128 * j : 128 * (j + 1)].astype(out_ref.dtype)
        out_ref[1152:] = rows_ref[pl.ds(pl.multiple_of(432 * core, 8), 432)].astype(out_ref.dtype)


def near_back_kernel(core_ref, got_ref, hidden_ref, start_ref, dh_ref, mine_ref, other_ref, rows_ref):
    da = sum(got_ref[j, :, :TOK].astype(F32) for j in range(8))
    hidden = hidden_ref[...]
    s = jax.nn.sigmoid(hidden)
    dh = (da * s * (1.0 + hidden * (1.0 - s))).astype(BF)
    dh_ref[...] = dh
    conv_rows(start_ref[...].astype(F32), dh, NEAR, rows_ref)
    for out_ref, core in ((mine_ref, core_ref[0]), (other_ref, 1 - core_ref[0])):
        out_ref[...] = rows_ref[pl.ds(pl.multiple_of(432 * core, 8), 432)].astype(out_ref.dtype)


def tokens_kernel(dh_ref, weight_ref, grad_ref, out_ref):
    back = grad_ref[...].astype(F32) + conv_back(dh_ref[...].astype(F32), weight_ref, NEAR)
    rows = back.T
    out_ref[:, :16] = rows[:, :128].reshape(32, 16, 128).astype(BF)
    rest = rows[:, 128:].reshape(32, 16, 64)
    out_ref[:, 16:] = jnp.concatenate([rest[:, :8], rest[:, 8:]], axis=2).astype(BF)


def gather_kernel(got_ref, early_ref, early_other_ref, late_ref, late_other_ref, tokens_ref, out_ref, rows_ref):
    rows_ref[:1584] = early_ref[...] + early_other_ref[...].astype(F32)
    rows_ref[1584:2016] = late_ref[...] + late_other_ref[...].astype(F32)
    rows_ref[2016:] = jnp.zeros((32, 128), F32)
    out_ref[:, :64] = rows_ref[...].reshape(32, 64, 128).astype(BF)
    out_ref[:, 64:ROWS] = got_ref[:, :160, TOK:].astype(F32).reshape(32, 40, 128).astype(BF)
    out_ref[:, ROWS:] = tokens_ref[...]


def sum_kernel(got_ref, out_ref):
    total = got_ref[0, :ROWS].astype(F32)
    for j in range(1, 32):
        total = total + got_ref[j, :ROWS].astype(F32)
    piece = (total * SCALE).astype(BF)
    for j in range(32):
        out_ref[j] = piece


def finish_kernel(core_ref, mine_ref, other_ref, near_pw_ref, far_pw_ref, near_conv_ref, far_conv_ref, all_ref, far_ref):
    first = core_ref[0] == 0
    mine = mine_ref[...].astype(F32)
    other = other_ref[...].astype(F32)
    all_ref[0] = jnp.where(first, mine, other)
    all_ref[1] = jnp.where(first, other, mine)
    for j in range(12):
        for part in range(3):
            near_pw_ref[64 * part : 64 * (part + 1), 128 * j : 128 * (j + 1)] = all_ref[
                j // 6, 3 * (j % 6) + part, :64
            ].astype(BF)
    for core in range(2):
        rows = all_ref[core, 18:, :64].reshape(14 * 64, 128)
        for out_ref, at in ((far_conv_ref, 0), (near_conv_ref, 432)):
            for block in range(9):
                place = 9 * core + block
                tap, column, half = place // 6, place // 2 % 3, place % 2
                out_ref[96 * tap + 48 * half : 96 * tap + 48 * (half + 1), 128 * column : 128 * (column + 1)] = rows[
                    at + 48 * block : at + 48 * (block + 1)
                ].astype(BF)
        for part in range(4):
            at = 96 * core + 24 * part
            for pair in range(4):
                blocks = []
                for j in (2 * pair, 2 * pair + 1):
                    piece = all_ref[core, 4 * j + part, 64:ROWS]
                    rest = jnp.concatenate([piece[24:32, :64], piece[24:32, 64:], piece[32:, :64]], axis=0)
                    blocks.append((piece[:24], rest))
                (even, even_rest), (odd, odd_rest) = blocks
                col = 2 * CG * pair
                far_ref[at : at + 24, col : col + 128] = even
                far_ref[at : at + 24, col + 128 : col + 256] = jnp.concatenate([even_rest, odd[:, :64]], axis=1)
                far_ref[at : at + 24, col + 256 : col + 384] = jnp.concatenate([odd[:, 64:], odd_rest], axis=1)
    far_pw_ref[...] = far_ref[...].astype(BF)


def slide(values, by):
    rows, cols = values.shape
    filler = jnp.zeros((rows, abs(by)), values.dtype)
    if by > 0:
        return jnp.concatenate([values[:, by:], filler], axis=1)
    return jnp.concatenate([filler, values[:, :by]], axis=1)


def local(emb, order, cot, cw1, pw1, cw2, pw2):
    core = lax.axis_index("core").astype(jnp.int32).reshape(1)
    base = (lax.axis_index(SEQ) * TOK).astype(jnp.int32).reshape(1)
    w1 = cw1.reshape(3, CG, CG)
    w2 = cw2.reshape(3, CG, CG)
    w1t = w1.transpose(0, 2, 1)
    pw1t = pw1.T
    pw2_blocks = pw2.reshape(CG, 8, CG).transpose(1, 0, 2)

    (packed,) = call(pack_kernel, [((TOK, 2 * CG), BF)], (base,), order.reshape(1, TOK), emb, cot)
    packed = swap(packed.reshape(32, TOK // 32, 2 * CG), CHIPS).reshape(TOK, 2 * CG)
    act8, near_hidden, start, cotq = call(
        near_kernel,
        [((8, CG, TOK), BF), ((CG, TOK), F32), ((CG, TOK), BF), ((CG, TOK), BF)],
        (),
        packed,
        w1t,
    )
    act_all = swap(act8, GRP).reshape(8 * CG, TOK)

    sent = jnp.concatenate([jnp.broadcast_to(cotq[None], (8, CG, TOK)), pw2_blocks], axis=2)
    sent = swap(sent, GRP)

    middle = (start.astype(F32) + mm(pw1, act_all, 1, 0)).astype(BF)
    far_hidden = (
        mm(w2[0], slide(middle, -FAR), 0, 0) + mm(w2[1], middle, 0, 0) + mm(w2[2], slide(middle, FAR), 0, 0)
    )
    far_act = jax.nn.silu(far_hidden).astype(BF)

    pg2_mine, pg2_other = call(
        regroup_kernel,
        [((8, 160, 128), F32), ((8, 160, 128), BF)],
        (core,),
        sent,
        far_act,
        scratch=[((8 * CG, CG), F32)],
    )
    pg2_other = other_core(pg2_other)
    far_dh, grad_middle = call(
        far_kernel, [((CG, TOK), BF), ((CG, TOK), BF)], (), sent, far_hidden, cotq, w2
    )
    (parts,) = call(parts_kernel, [((8, CG, TOK + 128), BF)], (), grad_middle, pw1t, pg2_mine, pg2_other)
    got = swap(parts, GRP)

    early, early_other = call(
        early_kernel,
        [((1584, 128), F32), ((1584, 128), BF)],
        (core,),
        grad_middle,
        act_all,
        middle,
        far_dh,
        scratch=[((864, 128), F32)],
    )
    early_other = other_core(early_other)

    near_dh, late, late_other = call(
        near_back_kernel,
        [((CG, TOK), BF), ((432, 128), F32), ((432, 128), BF)],
        (core,),
        got,
        near_hidden,
        start,
        scratch=[((864, 128), F32)],
    )
    late_other = other_core(late_other)
    (tokens,) = call(tokens_kernel, [((32, 24, 128), BF)], (), near_dh, w1, grad_middle)
    (bundle,) = call(
        gather_kernel,
        [((32, ROWS + 24, 128), BF)],
        (),
        got,
        early,
        early_other,
        late,
        late_other,
        tokens,
        scratch=[((2048, 128), F32)],
    )
    bundle = swap(bundle, CHIPS)
    (spread,) = call(sum_kernel, [((32, ROWS, 128), BF)], (), bundle)
    spread = swap(spread, CHIPS)

    rest = bundle[:, ROWS + 16 :]
    rest = jnp.concatenate([rest[:, :, :64], rest[:, :, 64:]], axis=1)
    back = jnp.concatenate([bundle[:, ROWS : ROWS + 16], rest], axis=2).reshape(TOK, CG)
    onehot = (lax.broadcasted_iota(jnp.int32, (TOK, TOK), 0) == (order - base)[None, :]).astype(BF)
    emb_grad = mm(back, onehot, 0, 1).astype(BF)

    out_pg1, out_pg2, out_cg1, out_cg2 = call(
        finish_kernel,
        [((CG, 8 * CG), BF), ((CG, 8 * CG), BF), ((288, 384), BF), ((288, 384), BF)],
        (core,),
        spread,
        other_core(spread),
        scratch=[((2, 32, ROWS, 128), F32), ((CG, 8 * CG), F32)],
    )
    flat = (1, 3 * CG * CG)
    return emb_grad, out_cg1.reshape(flat), out_pg1, out_cg2.reshape(flat), out_pg2


def solution(mesh):
    fine = Mesh(mesh.devices.reshape(4, 4, 2, 2, 4, 2), SEQ + GRP)
    placed = (P(GRP, SEQ), P(SEQ), P(GRP, SEQ), P(GRP, None), P(GRP, None), P(GRP, None), P(GRP, None))
    return jax.shard_map(
        local,
        mesh=fine,
        in_specs=placed,
        out_specs=(P(GRP, SEQ), P(GRP, None), P(GRP, None), P(GRP, None), P(GRP, None)),
        check_vma=False,
    )
```

time: 237 us -> 231 us (0.975)
  matrix products: 18.1 us -> 4.52 us
  Pallas kernels: 0 us -> 13.1 us
  waiting for transfers between devices: 56.4 us -> 65 us
  starting transfers between devices: 53.3 us -> 46.3 us
  local copies, waits for them, and re-layouts: 30.1 us -> 25.4 us
  other arithmetic: 10.1 us -> 5.97 us
  blocking collectives: 64.9 us -> 68 us
    unnamed x36 -> x61, local copies, waits for them, and re-layouts: 1.21 us -> 19 us
    dot_general x27 -> x5, matrix products: 18.1 us -> 4.52 us  [mm(): lax.dot_general(a, b, (((ca,), (cb,)), ((), ())), preferred_element_type=...]
    pallas_call x0 -> x11, Pallas kernels: none -> 13.1 us  [call(): pl.pallas_call(kernel, out_shape=[jax.ShapeDtypeStruct(shape, dtype) for...]
    reshape x14 -> x2, local copies, waits for them, and re-layouts: 11.7 us -> 1.36 us  [the longest x1 1.16 us: local(): w2 = cw2.reshape(3, CG, CG)]
    all_to_all x5 -> x4, waiting for transfers between devices: 54 us -> 64 us  [swap(): return lax.all_to_all(blocks, axes, 0, 0, tiled=True)]
    all_to_all x5 -> x4, starting transfers between devices: 37.6 us -> 29.6 us  [swap(): return lax.all_to_all(blocks, axes, 0, 0, tiled=True)]
    convert_element_type x6 -> x0, local copies, waits for them, and re-layouts: 4.81 us -> none  [the longest x1 2.61 us: local(): parts = mm(pw1, grad_middle, 0, 0).astype(BF).reshape(8, CG, cols)]
    unnamed x0 -> x2, other arithmetic: none -> 4.25 us
  transfers between devices with their start and end apart: 8 -> 8, of which waited for: 6 -> 6; matrix products, arithmetic and copies ran while one was open for 12% -> 8% of each run, Pallas kernels for 0% -> 2%
where the time goes in v3:
time: 231 us; the launch traced here: 229 us
  blocking collectives  68 us (29%)
  waiting for transfers between devices  65 us (28%)
  starting transfers between devices  46.3 us (20%)
  local copies, waits for them, and re-layouts  25.4 us (11%)
  Pallas kernels  13.1 us (6%)
  other arithmetic  5.97 us (3%)
  matrix products  4.52 us (2%)
    all_to_all x2, blocking collectives, swap(): return lax.all_to_all(blocks, axes, 0, 0, tiled=True)  68 us
    all_to_all x4, waiting for transfers between devices, swap(): return lax.all_to_all(blocks, axes, 0, 0, tiled=True)  64 us
    all_to_all x4, starting transfers between devices, swap(): return lax.all_to_all(blocks, axes, 0, 0, tiled=True)  29.6 us
    unnamed x61, local copies, waits for them, and re-layouts  19 us
    ppermute x4, starting transfers between devices, other_core(): return lax.ppermute(values, 'core', [(0, 1), (1, 0)])  16.7 us
    pallas_call x11, Pallas kernels, call(): pl.pallas_call(kernel, out_shape=[jax.ShapeDtypeStruct(shape, dtype) for...  13.1 us
  transfers between devices with their start and end apart: 8, of which 6 were waited for; matrix products, arithmetic and copies ran while one was open for 8% of the time, Pallas kernels for 2%

profile of v3, /device:TPU:1, one launch (start us, length us, event | category | flops | bytes accessed | tf_op | source)
XLA Modules:
  0.0 229.4 jit_solution(12332597238176309334)
XLA Ops:
  4.3 16.5 %all-to-all-start = ((bf16[32,16,384]{2,1,0:T(8,128)(2,1)}), bf16[32,16,384]{2,1,0:T(8,128)(2,1)S(1)}, u32[]{:S(2)}, u32[]{:S(2)}) async-start(bf16[32,16,384]{2,1,0:T(8,128)(2,1)} %bitcast.2), calls=%async_computation | async-start | bytes 786432 | tf_op jit(solution)/shard_map/all_to_all | solution.py:26
  20.8 2.2 reduce
  23.5 12.0 %all-to-all-done = bf16[32,16,384]{2,1,0:T(8,128)(2,1)S(1)} async-done(((bf16[32,16,384]{2,1,0:T(8,128)(2,1)}), bf16[32,16,384]{2,1,0:T(8,128)(2,1)S(1)}, u32[]{:S(2)}, u32[]{:S(2)}) %all-to-all-start) | async-done | bytes 393248 | tf_op jit(solution)/shard_map/all_to_all | solution.py:26
  35.4 1.7 shard_map.111
  37.8 4.9 %all-to-all-start.2 = ((bf16[8,192,512]{2,1,0:T(8,128)(2,1)}), bf16[8,192,512]{2,1,0:T(8,128)(2,1)S(1)}, u32[]{:S(2)}, u32[]{:S(2)}) async-start(bf16[8,192,512]{2,1,0:T(8,128)(2,1)} %get-tuple-element.24), calls=%async_computation.2 | async-start | bytes 3145728 | tf_op jit(solution)/shard_map/all_to_all | solution.py:26
  42.8 1.7 reshape.60
  44.8 1.7 pad_maximum_fusion
  46.5 14.3 %all-to-all-done.2 = bf16[8,192,512]{2,1,0:T(8,128)(2,1)S(1)} async-done(((bf16[8,192,512]{2,1,0:T(8,128)(2,1)}), bf16[8,192,512]{2,1,0:T(8,128)(2,1)S(1)}, u32[]{:S(2)}, u32[]{:S(2)}) %all-to-all-start.2) | async-done | bytes 1572896 | tf_op jit(solution)/shard_map/all_to_all | solution.py:26
  61.9 4.5 %all-to-all-start.1 = ((bf16[8,192,704]{2,1,0:T(8,128)(2,1)}), bf16[8,192,704]{2,1,0:T(8,128)(2,1)S(1)}, u32[]{:S(2)}, u32[]{:S(2)}) async-start(bf16[8,192,704]{2,1,0:T(8,128)(2,1)} %pad_maximum_fusion), calls=%async_computation.1 | async-start | bytes 4718592 | tf_op jit(solution)/shard_map/all_to_all | solution.py:26
  66.4 2.3 %slice_reduce_fusion = (bf16[36864]{0:T(1024)(128)(2,1)S(1)}, bf16[36864]{0:T(1024)(128)(2,1)S(1)}, bf16[36864]{0:T(1024)(128)(2,1)S(1)}) fusion(bf16[1,110592]{1,0:T(2,128)(2,1)} %param.12), kind=kLoop, calls=%fused_computation.16 | loop fusion | bytes 442368 | tf_op jit(solution)/shard_map/slice | solution.py:256
  69.0 1.9 fusion.2.middle_ref
  72.7 20.0 %all-to-all-done.1.sent_ref = bf16[8,192,704]{2,1,0:T(8,128)(2,1)S(1)} async-done(((bf16[8,192,704]{2,1,0:T(8,128)(2,1)}), bf16[8,192,704]{2,1,0:T(8,128)(2,1)S(1)}, u32[]{:S(2)}, u32[]{:S(2)}) %all-to-all-start.1) | async-done | bytes 2162720 | tf_op jit(solution)/shard_map/all_to_all | solution.py:26
  95.0 6.3 %collective-permute-start = (bf16[8,160,128]{2,1,0:T(8,128)(2,1)}, bf16[8,160,128]{2,1,0:T(8,128)(2,1)}, u32[]{:S(2)}, u32[]{:S(2)}) collective-permute-start(bf16[8,160,128]{2,1,0:T(8,128)(2,1)} %get-tuple-element.27), channel_id=1, source_target_pairs={{0,8},{8,0},{1,9},{9,1},{2,10},{10,2},{3,11},{11,3},{4,12},{12,4},... | collective-permute-start | bytes 983048 | tf_op jit(solution)/shard_map/ppermute | solution.py:30
  101.3 2.0 reduce.4
  109.4 1.6 shard_map.114
  113.0 3.7 %all-to-all-start.3 = ((bf16[8,192,640]{2,1,0:T(8,128)(2,1)}), bf16[8,192,640]{2,1,0:T(8,128)(2,1)S(1)}, u32[]{:S(2)}, u32[]{:S(2)}) async-start(bf16[8,192,640]{2,1,0:T(8,128)(2,1)} %copy-done.2), calls=%async_computation.3 | async-start | bytes 3932160 | tf_op jit(solution)/shard_map/all_to_all | solution.py:26
  119.5 1.9 shard_map.115
  122.3 2.2 collective-permute-start.1
  124.6 17.7 %all-to-all-done.3.got_ref = bf16[8,192,640]{2,1,0:T(8,128)(2,1)S(1)} async-done(((bf16[8,192,640]{2,1,0:T(8,128)(2,1)}), bf16[8,192,640]{2,1,0:T(8,128)(2,1)S(1)}, u32[]{:S(2)}, u32[]{:S(2)}) %all-to-all-start.3) | async-done | bytes 1966112 | tf_op jit(solution)/shard_map/all_to_all | solution.py:26
  145.2 2.8 %collective-permute-start.2 = (bf16[432,128]{1,0:T(8,128)(2,1)S(1)}, bf16[432,128]{1,0:T(8,128)(2,1)S(1)}, u32[]{:S(2)}, u32[]{:S(2)}) collective-permute-start(bf16[432,128]{1,0:T(8,128)(2,1)S(1)} %get-tuple-element.33), channel_id=1, source_target_pairs={{0,8},{8,0},{1,9},{9,1},{2,10},{10,2},{3,11},{11,3},{4,12},{12,4},... | collective-permute-start | bytes 331784 | tf_op jit(solution)/shard_map/ppermute | solution.py:30
  150.1 35.3 %all_to_all.30.got_ref = bf16[32,128,128]{2,1,0:T(8,128)(2,1)S(1)} all-to-all(bf16[32,128,128]{2,1,0:T(8,128)(2,1)S(1)} %shard_map.118), channel_id=1, replica_groups=mesh['zh'=4,'yh'=4,'yl'=2,'core'=2,'x'=4,'zl'=2] {'zh','yh','yl'}, dimensions={0} | all-to-all | bytes 2097152 | tf_op jit(solution)/shard_map/all_to_all | solution.py:26
  185.5 32.7 %all_to_all.31.mine_ref = bf16[32,104,128]{2,1,0:T(8,128)(2,1)S(1)} all-to-all(bf16[32,104,128]{2,1,0:T(8,128)(2,1)S(1)} %shard_map.119), channel_id=1, replica_groups=mesh['zh'=4,'yh'=4,'yl'=2,'core'=2,'x'=4,'zl'=2] {'zh','yh','yl'}, dimensions={0} | all-to-all | bytes 1703936 | tf_op jit(solution)/shard_map/all_to_all | solution.py:26
  218.3 5.4 %collective-permute-start.3 = (bf16[32,104,128]{2,1,0:T(8,128)(2,1)S(1)}, bf16[32,104,128]{2,1,0:T(8,128)(2,1)S(1)}, u32[]{:S(2)}, u32[]{:S(2)}) collective-permute-start(bf16[32,104,128]{2,1,0:T(8,128)(2,1)S(1)} %all_to_all.31.mine_ref), channel_id=1, source_target_pairs={{0,8},{8,0},{1,9},{9,1},{2,10},{10,2},{3,11},{11,3},{4,12},{12,4},... | collective-permute-start | bytes 2555912 | tf_op jit(solution)/shard_map/ppermute | solution.py:30
  225.7 1.5 shard_map.120
  (89 shorter events, 31.6 us)
Async XLA Ops:
  4.3 31.1 %all-to-all-start = ((bf16[32,16,384]{2,1,0:T(8,128)(2,1)}), bf16[32,16,384]{2,1,0:T(8,128)(2,1)S(1)}, u32[]{:S(2)}, u32[]{:S(2)}) async-start(bf16[32,16,384]{2,1,0:T(8,128)(2,1)} %bitcast.2), calls=%async_computation | async-start | bytes 786432 | tf_op jit(solution)/shard_map/all_to_all | solution.py:26
  23.3 14.6 %copy-start.5 = (bf16[3,192,192]{2,1,0:T(8,128)(2,1)}, bf16[3,192,192]{2,1,0:T(8,128)(2,1)S(1)}, u32[]{:S(2)}) copy-start(bf16[3,192,192]{2,1,0:T(8,128)(2,1)S(1)} %reshape.59.weight_ref) | copy-start | bytes 663556
  37.8 6.8 %copy-start.12 = (bf16[192,512]{1,0:T(8,128)(2,1)}, bf16[192,512]{1,0:T(8,128)(2,1)S(1)}, u32[]{:S(2)}) copy-start(bf16[192,512]{1,0:T(8,128)(2,1)S(1)} %get-tuple-element.22.cot_ref) | copy-start | bytes 589828
  37.8 31.2 %copy-start.14 = (bf16[192,512]{1,0:T(8,128)(2,1)}, bf16[192,512]{1,0:T(8,128)(2,1)S(1)}, u32[]{:S(2)}) copy-start(bf16[192,512]{1,0:T(8,128)(2,1)S(1)} %get-tuple-element.23.start_ref) | copy-start | bytes 589828
  37.8 22.9 %all-to-all-start.2 = ((bf16[8,192,512]{2,1,0:T(8,128)(2,1)}), bf16[8,192,512]{2,1,0:T(8,128)(2,1)S(1)}, u32[]{:S(2)}, u32[]{:S(2)}) async-start(bf16[8,192,512]{2,1,0:T(8,128)(2,1)} %get-tuple-element.24), calls=%async_computation.2 | async-start | bytes 3145728 | tf_op jit(solution)/shard_map/all_to_all | solution.py:26
  46.5 22.6 %copy-start.27 = (bf16[192,1536]{1,0:T(8,128)(2,1)S(1)}, bf16[192,1536]{1,0:T(8,128)(2,1)}, u32[]{:S(2)}) copy-start(bf16[192,1536]{1,0:T(8,128)(2,1)} %param.11) | copy-start | bytes 1769476
  60.7 1.2 copy-start
  61.9 30.8 %all-to-all-start.1 = ((bf16[8,192,704]{2,1,0:T(8,128)(2,1)}), bf16[8,192,704]{2,1,0:T(8,128)(2,1)S(1)}, u32[]{:S(2)}, u32[]{:S(2)}) async-start(bf16[8,192,704]{2,1,0:T(8,128)(2,1)} %pad_maximum_fusion), calls=%async_computation.1 | async-start | bytes 4718592 | tf_op jit(solution)/shard_map/all_to_all | solution.py:26
  71.7 29.6 %copy-start.28 = (bf16[1,110592]{1,0:T(2,128)(2,1)S(1)}, bf16[1,110592]{1,0:T(2,128)(2,1)}, u32[]{:S(2)}) copy-start(bf16[1,110592]{1,0:T(2,128)(2,1)} %param.12) | copy-start | bytes 663556
  95.0 14.4 %collective-permute-start = (bf16[8,160,128]{2,1,0:T(8,128)(2,1)}, bf16[8,160,128]{2,1,0:T(8,128)(2,1)}, u32[]{:S(2)}, u32[]{:S(2)}) collective-permute-start(bf16[8,160,128]{2,1,0:T(8,128)(2,1)} %get-tuple-element.27), channel_id=1, source_target_pairs={{0,8},{8,0},{1,9},{9,1},{2,10},{10,2},{3,11},{11,3},{4,12},{12,4},... | collective-permute-start | bytes 983048 | tf_op jit(solution)/shard_map/ppermute | solution.py:30
  105.8 0.9 copy-start.13
  106.7 1.0 copy-start.18
  107.7 1.7 copy-start.17
  111.0 1.3 copy-start.2
  113.0 3.7 %copy-start.1 = (bf16[8,192,512]{2,1,0:T(8,128)(2,1)S(1)}, bf16[8,192,512]{2,1,0:T(8,128)(2,1)}, u32[]{:S(2)}) copy-start(bf16[8,192,512]{2,1,0:T(8,128)(2,1)} %copy-done) | copy-start | bytes 4718596
  113.0 29.3 %all-to-all-start.3 = ((bf16[8,192,640]{2,1,0:T(8,128)(2,1)}), bf16[8,192,640]{2,1,0:T(8,128)(2,1)S(1)}, u32[]{:S(2)}, u32[]{:S(2)}) async-start(bf16[8,192,640]{2,1,0:T(8,128)(2,1)} %copy-done.2), calls=%async_computation.3 | async-start | bytes 3932160 | tf_op jit(solution)/shard_map/all_to_all | solution.py:26
  122.3 25.7 %copy-start.6 = (bf16[3,192,192]{2,1,0:T(8,128)(2,1)S(1)}, bf16[3,192,192]{2,1,0:T(8,128)(2,1)}, u32[]{:S(2)}) copy-start(bf16[3,192,192]{2,1,0:T(8,128)(2,1)} %copy-done.5) | copy-start | bytes 663556
  122.3 25.7 %copy-start.9 = (bf16[192,512]{1,0:T(8,128)(2,1)S(1)}, bf16[192,512]{1,0:T(8,128)(2,1)}, u32[]{:S(2)}) copy-start(bf16[192,512]{1,0:T(8,128)(2,1)} %copy-done.7) | copy-start | bytes 589828
  122.3 26.6 %copy-start.11 = (f32[1584,128]{1,0:T(8,128)S(1)}, f32[1584,128]{1,0:T(8,128)}, u32[]{:S(2)}) copy-start(f32[1584,128]{1,0:T(8,128)} %copy-done.10) | copy-start | bytes 2433028
  122.3 26.3 %collective-permute-start.1 = (bf16[1584,128]{1,0:T(8,128)(2,1)}, bf16[1584,128]{1,0:T(8,128)(2,1)}, u32[]{:S(2)}, u32[]{:S(2)}) collective-permute-start(bf16[1584,128]{1,0:T(8,128)(2,1)} %get-tuple-element.30), channel_id=1, source_target_pairs={{0,8},{8,0},{1,9},{9,1},{2,10},{10,2},{3,11},{11,3},{4,12},{12,4},... | collective-permute-start | bytes 1216520 | tf_op jit(solution)/shard_map/ppermute | solution.py:30
  143.2 1.0 copy-start.20
  145.2 3.7 %collective-permute-start.2 = (bf16[432,128]{1,0:T(8,128)(2,1)S(1)}, bf16[432,128]{1,0:T(8,128)(2,1)S(1)}, u32[]{:S(2)}, u32[]{:S(2)}) collective-permute-start(bf16[432,128]{1,0:T(8,128)(2,1)S(1)} %get-tuple-element.33), channel_id=1, source_target_pairs={{0,8},{8,0},{1,9},{9,1},{2,10},{10,2},{3,11},{11,3},{4,12},{12,4},... | collective-permute-start | bytes 331784 | tf_op jit(solution)/shard_map/ppermute | solution.py:30
  185.4 38.3 %copy-start.26 = (s32[512]{0:T(512)S(1)}, s32[512]{0:T(512)}, u32[]{:S(2)}) copy-start(s32[512]{0:T(512)} %param.8) | copy-start | bytes 6148
  218.3 7.4 %collective-permute-start.3 = (bf16[32,104,128]{2,1,0:T(8,128)(2,1)S(1)}, bf16[32,104,128]{2,1,0:T(8,128)(2,1)S(1)}, u32[]{:S(2)}, u32[]{:S(2)}) collective-permute-start(bf16[32,104,128]{2,1,0:T(8,128)(2,1)S(1)} %all_to_all.31.mine_ref), channel_id=1, source_target_pairs={{0,8},{8,0},{1,9},{9,1},{2,10},{10,2},{3,11},{11,3},{4,12},{12,4},... | collective-permute-start | bytes 2555912 | tf_op jit(solution)/shard_map/ppermute | solution.py:30
  (13 other events, 10.8 us)

commit v4 on v3

v4 whole, which is shorter than its diff:
```python
import jax
import jax.numpy as jnp
from jax import lax
from jax.experimental import pallas as pl
from jax.experimental.pallas import tpu as pltpu
from jax.sharding import Mesh, PartitionSpec as P

CG = 192
TOK = 512
NEAR = 32
FAR = 64
BF = jnp.bfloat16
F32 = jnp.float32
SEQ = ("zh", "yh", "yl", "core")
GRP = ("x", "zl")
CHIPS = ("zh", "yh", "yl")
SCALE = float(32768) ** (-0.5)
ROWS = 104


def mm(a, b, ca, cb):
    return lax.dot_general(a, b, (((ca,), (cb,)), ((), ())), preferred_element_type=F32)


def swap(blocks, axes):
    return lax.all_to_all(blocks, axes, 0, 0, tiled=True)


def other_core(values):
    return lax.ppermute(values, "core", [(0, 1), (1, 0)])


def call(kernel, outs, scalars, direct, fetched=(), scratch=(), mib=8, space=pl.ANY, flops=0):
    vmem = pl.BlockSpec(memory_space=pltpu.VMEM)
    smem = pl.BlockSpec(memory_space=pltpu.SMEM)
    anywhere = pl.BlockSpec(memory_space=space)
    n_near, n_far, n_out = len(scalars) + len(direct), len(fetched), len(outs)

    def body(*refs):
        near, far, out, rest = (
            refs[:n_near],
            refs[n_near : n_near + n_far],
            refs[n_near + n_far : n_near + n_far + n_out],
            refs[n_near + n_far + n_out :],
        )
        buffers, own = rest[:n_far], rest[n_far:]
        if n_far:
            sems, own = own[-1], own[:-1]
            copies = [pltpu.make_async_copy(far[i], buffers[i], sems.at[i]) for i in range(n_far)]
            for copy in copies:
                copy.start()
            for copy in copies:
                copy.wait()
        kernel(*near, *buffers, *out, *own)

    return pl.pallas_call(
        body,
        out_shape=[jax.ShapeDtypeStruct(shape, dtype) for shape, dtype in outs],
        in_specs=[smem] * len(scalars) + [vmem] * len(direct) + [anywhere] * n_far,
        out_specs=[vmem] * n_out,
        scratch_shapes=[pltpu.VMEM(x.shape, x.dtype) for x in fetched]
        + [pltpu.VMEM(shape, dtype) for shape, dtype in scratch]
        + ([pltpu.SemaphoreType.DMA((n_far,))] if n_far else []),
        compiler_params=pltpu.CompilerParams(vmem_limit_bytes=mib * 1024 * 1024),
        cost_estimate=pl.CostEstimate(flops=flops, bytes_accessed=0, transcendentals=0) if flops else None,
    )(*scalars, *direct, *fetched)


def shifted(values, by):
    if by == 0:
        return values.astype(BF)
    lane = lax.broadcasted_iota(jnp.int32, values.shape, 1)
    rolled = pltpu.roll(values, (-by) % TOK, 1)
    keep = lane < TOK - by if by > 0 else lane >= -by
    return jnp.where(keep, rolled, 0.0).astype(BF)


def conv_back(grads, weight_ref, by):
    return (
        mm(weight_ref[0], shifted(grads, by), 1, 0)
        + mm(weight_ref[1], shifted(grads, 0), 1, 0)
        + mm(weight_ref[2], shifted(grads, -by), 1, 0)
    )


def conv_rows(values, grads, by, rows_ref):
    row = lax.broadcasted_iota(jnp.int32, (CG, CG), 0)
    col = lax.broadcasted_iota(jnp.int32, (CG, CG), 1)
    half = CG // 2
    source = jnp.where(row < half, 2 * row, 2 * row - (CG - 1))
    order = jnp.where(col == source, 1.0, 0.0).astype(BF)
    for tap, distance in enumerate((-by, 0, by)):
        moved = mm(order, shifted(values, distance), 1, 0).astype(BF)
        grad = mm(moved, grads, 1, 1)
        even, odd = grad[:half], grad[half:]
        base = 3 * half * tap
        rows_ref[base : base + half] = even[:, :128]
        rows_ref[base + half : base + 2 * half] = jnp.concatenate([even[:, 128:], odd[:, :64]], axis=1)
        rows_ref[base + 2 * half : base + 3 * half] = odd[:, 64:]


def pack_kernel(base_ref, order_ref, emb_ref, cot_ref, out_ref):
    token = lax.broadcasted_iota(jnp.int32, (TOK, TOK), 0)
    onehot = jnp.where(token == order_ref[...] - base_ref[0], 1.0, 0.0).astype(BF)
    start = mm(emb_ref[...], onehot, 1, 0)
    both = jnp.concatenate([start, cot_ref[...].astype(F32)], axis=0)
    out_ref[...] = both.T.astype(BF)


def near_kernel(tokens_ref, weight_ref, blocks_ref, out_ref, hidden_ref, start_ref):
    rows = tokens_ref[...].astype(F32)
    both = rows.T
    start_ref[...] = both[:CG].astype(BF)
    cot = both[CG:].astype(BF)
    start = rows[:, :CG]
    filler = jnp.zeros((NEAR, CG), F32)
    before = jnp.concatenate([filler, start[: TOK - NEAR]], axis=0).astype(BF)
    after = jnp.concatenate([start[NEAR:], filler], axis=0).astype(BF)
    hidden = (
        mm(weight_ref[0], before, 0, 1)
        + mm(weight_ref[1], start.astype(BF), 0, 1)
        + mm(weight_ref[2], after, 0, 1)
    )
    hidden_ref[...] = hidden
    act = (hidden * jax.nn.sigmoid(hidden)).astype(BF)
    for j in range(8):
        out_ref[j, :, :TOK] = act
        out_ref[j, :, TOK : 2 * TOK] = cot
        out_ref[j, :, 2 * TOK :] = blocks_ref[j]


def mid_kernel(own_ref, sent_ref, start_ref, pointwise_ref, weight_ref, middle_ref, dh_ref, grad_ref, out_ref):
    middle = start_ref[...].astype(F32) + sum(
        mm(pointwise_ref[j * CG : (j + 1) * CG], sent_ref[j, :, :TOK], 0, 0) for j in range(8)
    )
    middle = middle.astype(BF)
    middle_ref[...] = middle
    wide = middle.astype(F32)
    hidden = (
        mm(weight_ref[0], shifted(wide, -FAR), 0, 0)
        + mm(weight_ref[1], middle, 0, 0)
        + mm(weight_ref[2], shifted(wide, FAR), 0, 0)
    )
    s = jax.nn.sigmoid(hidden)
    act = (hidden * s).astype(BF)
    for j in range(8):
        out_ref[j, :, TOK:] = mm(sent_ref[j, :, TOK : 2 * TOK], act, 1, 1).astype(BF)
    da = sum(mm(sent_ref[j, :, 2 * TOK :], sent_ref[j, :, TOK : 2 * TOK], 0, 0) for j in range(8))
    dh = (da * s * (1.0 + hidden * (1.0 - s))).astype(BF)
    dh_ref[...] = dh
    back = conv_back(dh.astype(F32), weight_ref, FAR)
    grad = (sent_ref[own_ref[0], :, TOK : 2 * TOK].astype(F32) + back).astype(BF)
    grad_ref[...] = grad
    for j in range(8):
        out_ref[j, :, :TOK] = mm(pointwise_ref[j * CG : (j + 1) * CG], grad, 1, 0).astype(BF)


def back_kernel(
    core_ref,
    got_ref,
    sent_ref,
    hidden_ref,
    start_ref,
    grad_ref,
    middle_ref,
    far_dh_ref,
    dh_ref,
    mine_ref,
    other_ref,
    far_rows_ref,
    near_rows_ref,
):
    da = sum(got_ref[j, :, :TOK].astype(F32) for j in range(8))
    hidden = hidden_ref[...]
    s = jax.nn.sigmoid(hidden)
    dh = (da * s * (1.0 + hidden * (1.0 - s))).astype(BF)
    dh_ref[...] = dh
    conv_rows(start_ref[...].astype(F32), dh, NEAR, near_rows_ref)
    conv_rows(middle_ref[...].astype(F32), far_dh_ref[...], FAR, far_rows_ref)
    blank = jnp.zeros((8, 64), F32)
    for out_ref, core in ((mine_ref, core_ref[0]), (other_ref, 1 - core_ref[0])):
        grad = jnp.concatenate([mm(grad_ref[...], sent_ref[4 * core + j, :, :TOK], 1, 1) for j in range(4)], axis=1)
        for j in range(6):
            out_ref[CG * j : CG * (j + 1)] = grad[:, 128 * j : 128 * (j + 1)].astype(out_ref.dtype)
        rows = pl.ds(pl.multiple_of(432 * core, 8), 432)
        out_ref[1152:1584] = far_rows_ref[rows].astype(out_ref.dtype)
        out_ref[1584:2016] = near_rows_ref[rows].astype(out_ref.dtype)
        for j in range(8):
            half = got_ref[j, pl.ds(pl.multiple_of(96 * core, 16), 96), TOK:].astype(F32)
            for part in range(4):
                piece = half[24 * part : 24 * (part + 1)]
                rest = piece[:, 128:]
                packed = jnp.concatenate([rest[:8], rest[8:16]], axis=1), jnp.concatenate([rest[16:], blank], axis=1)
                at = 2016 + 160 * j + 40 * part
                out_ref[at : at + 40] = jnp.concatenate([piece[:, :128], *packed], axis=0).astype(out_ref.dtype)


def tokens_kernel(dh_ref, weight_ref, grad_ref, out_ref):
    back = grad_ref[...].astype(F32) + conv_back(dh_ref[...].astype(F32), weight_ref, NEAR)
    rows = back.T
    out_ref[:, :16] = rows[:, :128].reshape(32, 16, 128).astype(BF)
    rest = rows[:, 128:].reshape(32, 16, 64)
    out_ref[:, 16:] = jnp.concatenate([rest[:, :8], rest[:, 8:]], axis=2).astype(BF)


def gather_kernel(mine_ref, other_ref, tokens_ref, out_ref, rows_ref):
    rows_ref[:2016] = mine_ref[:2016] + other_ref[:2016].astype(F32)
    rows_ref[2016:] = jnp.zeros((32, 128), F32)
    out_ref[:, :64] = rows_ref[...].reshape(32, 64, 128).astype(BF)
    rest = mine_ref[2016:] + other_ref[2016:].astype(F32)
    out_ref[:, 64:ROWS] = rest.reshape(32, 40, 128).astype(BF)
    out_ref[:, ROWS:] = tokens_ref[...]


def sum_kernel(got_ref, out_ref):
    total = got_ref[0, :ROWS].astype(F32)
    for j in range(1, 32):
        total = total + got_ref[j, :ROWS].astype(F32)
    piece = (total * SCALE).astype(BF)
    for j in range(32):
        out_ref[j] = piece


def finish_kernel(core_ref, mine_ref, other_ref, near_pw_ref, far_pw_ref, near_conv_ref, far_conv_ref, all_ref, far_ref):
    first = core_ref[0] == 0
    mine = mine_ref[...].astype(F32)
    other = other_ref[...].astype(F32)
    all_ref[0] = jnp.where(first, mine, other)
    all_ref[1] = jnp.where(first, other, mine)
    for j in range(12):
        for part in range(3):
            near_pw_ref[64 * part : 64 * (part + 1), 128 * j : 128 * (j + 1)] = all_ref[
                j // 6, 3 * (j % 6) + part, :64
            ].astype(BF)
    for core in range(2):
        rows = all_ref[core, 18:, :64].reshape(14 * 64, 128)
        for out_ref, at in ((far_conv_ref, 0), (near_conv_ref, 432)):
            for block in range(9):
                place = 9 * core + block
                tap, column, half = place // 6, place // 2 % 3, place % 2
                out_ref[96 * tap + 48 * half : 96 * tap + 48 * (half + 1), 128 * column : 128 * (column + 1)] = rows[
                    at + 48 * block : at + 48 * (block + 1)
                ].astype(BF)
        for part in range(4):
            at = 96 * core + 24 * part
            for pair in range(4):
                blocks = []
                for j in (2 * pair, 2 * pair + 1):
                    piece = all_ref[core, 4 * j + part, 64:ROWS]
                    rest = jnp.concatenate([piece[24:32, :64], piece[24:32, 64:], piece[32:, :64]], axis=0)
                    blocks.append((piece[:24], rest))
                (even, even_rest), (odd, odd_rest) = blocks
                col = 2 * CG * pair
                far_ref[at : at + 24, col : col + 128] = even
                far_ref[at : at + 24, col + 128 : col + 256] = jnp.concatenate([even_rest, odd[:, :64]], axis=1)
                far_ref[at : at + 24, col + 256 : col + 384] = jnp.concatenate([odd[:, 64:], odd_rest], axis=1)
    far_pw_ref[...] = far_ref[...].astype(BF)


def local(emb, order, cot, cw1, pw1, cw2, pw2):
    core = lax.axis_index("core").astype(jnp.int32).reshape(1)
    own = lax.axis_index(GRP).astype(jnp.int32).reshape(1)
    base = (lax.axis_index(SEQ) * TOK).astype(jnp.int32).reshape(1)

    (packed,) = call(pack_kernel, [((TOK, 2 * CG), BF)], (base,), (), (order.reshape(1, TOK), emb, cot), space=pltpu.HBM)
    packed = swap(packed.reshape(32, TOK // 32, 2 * CG), CHIPS).reshape(TOK, 2 * CG)
    packed, own, core, w1, w2, pw1t, pw2_blocks = lax.optimization_barrier(
        (packed, own, core, cw1.reshape(3, CG, CG), cw2.reshape(3, CG, CG), pw1.T, pw2.reshape(CG, 8, CG).transpose(1, 0, 2))
    )
    sent, near_hidden, start = call(
        near_kernel,
        [((8, CG, 2 * TOK + CG), BF), ((CG, TOK), F32), ((CG, TOK), BF)],
        (),
        (packed, w1, pw2_blocks),
    )
    sent = swap(sent, GRP)
    middle, far_dh, grad_middle, parts = call(
        mid_kernel,
        [((CG, TOK), BF), ((CG, TOK), BF), ((CG, TOK), BF), ((8, CG, TOK + CG), BF)],
        (own,),
        (sent,),
        (start, pw1t, w2),
    )
    got = swap(parts, GRP)

    near_dh, mine, other = call(
        back_kernel,
        [((CG, TOK), BF), ((3296, 128), F32), ((3296, 128), BF)],
        (core,),
        (got, sent),
        (near_hidden, start, grad_middle, middle, far_dh),
        scratch=[((864, 128), F32), ((864, 128), F32)],
    )
    other = other_core(other)
    (tokens,) = call(tokens_kernel, [((32, 24, 128), BF)], (), (near_dh,), (w1, grad_middle))
    (bundle,) = call(
        gather_kernel,
        [((32, ROWS + 24, 128), BF)],
        (),
        (),
        (mine, other, tokens),
        scratch=[((2048, 128), F32)],
    )
    bundle = swap(bundle, CHIPS)
    (spread,) = call(sum_kernel, [((32, ROWS, 128), BF)], (), (bundle,))
    spread = swap(spread, CHIPS)

    rest = bundle[:, ROWS + 16 :]
    rest = jnp.concatenate([rest[:, :, :64], rest[:, :, 64:]], axis=1)
    back = jnp.concatenate([bundle[:, ROWS : ROWS + 16], rest], axis=2).reshape(TOK, CG)
    onehot = (lax.broadcasted_iota(jnp.int32, (TOK, TOK), 0) == (order - base)[None, :]).astype(BF)
    emb_grad = mm(back, onehot, 0, 1).astype(BF)

    out_pg1, out_pg2, out_cg1, out_cg2 = call(
        finish_kernel,
        [((CG, 8 * CG), BF), ((CG, 8 * CG), BF), ((288, 384), BF), ((288, 384), BF)],
        (core,),
        (spread, other_core(spread)),
        scratch=[((2, 32, ROWS, 128), F32), ((CG, 8 * CG), F32)],
        mib=12,
    )
    flat = (1, 3 * CG * CG)
    return emb_grad, out_cg1.reshape(flat), out_pg1, out_cg2.reshape(flat), out_pg2


def solution(mesh):
    fine = Mesh(mesh.devices.reshape(4, 4, 2, 2, 4, 2), SEQ + GRP)
    placed = (P(GRP, SEQ), P(SEQ), P(GRP, SEQ), P(GRP, None), P(GRP, None), P(GRP, None), P(GRP, None))
    return jax.shard_map(
        local,
        mesh=fine,
        in_specs=placed,
        out_specs=(P(GRP, SEQ), P(GRP, None), P(GRP, None), P(GRP, None), P(GRP, None)),
        check_vma=False,
    )
```

time: 231 us -> 210 us (0.909)
  blocking collectives: 68 us -> 144 us
  waiting for transfers between devices: 65 us -> 10.2 us
  local copies, waits for them, and re-layouts: 25.4 us -> 7.46 us
  starting transfers between devices: 46.3 us -> 29.1 us
  matrix products: 4.52 us -> 1.06 us
  other arithmetic: 5.97 us -> 3.61 us
    all_to_all x2 -> x4, blocking collectives: 68 us -> 144 us  [swap(): return lax.all_to_all(blocks, axes, 0, 0, tiled=True)]
    all_to_all x4 -> x1, waiting for transfers between devices: 64 us -> 8.36 us  [swap(): return lax.all_to_all(blocks, axes, 0, 0, tiled=True)]
    unnamed x61 -> x15, local copies, waits for them, and re-layouts: 19 us -> 5.02 us
    all_to_all x4 -> x1, starting transfers between devices: 29.6 us -> 16.5 us  [swap(): return lax.all_to_all(blocks, axes, 0, 0, tiled=True)]
    ppermute x4 -> x2, starting transfers between devices: 16.7 us -> 12.6 us  [other_core(): return lax.ppermute(values, 'core', [(0, 1), (1, 0)])]
    dot_general x5 -> x1, matrix products: 4.52 us -> 1.06 us  [mm(): lax.dot_general(a, b, (((ca,), (cb,)), ((), ())), preferred_element_type=...]
    slice x2 -> x0, local copies, waits for them, and re-layouts: 2.44 us -> none  [the longest x1 2.32 us: local(): w2[2]]
    pallas_call x11 -> x8, Pallas kernels: 13.1 us -> 11.9 us  [call(): pl.pallas_call(body, out_shape=[jax.ShapeDtypeStruct(shape, dtype) for sh...]
  transfers between devices with their start and end apart: 8 -> 3, of which waited for: 6 -> 3; matrix products, arithmetic and copies ran while one was open for 8% -> 4% of each run, Pallas kernels for 2% -> 0%
where the time goes in v4:
time: 210 us; the launch traced here: 209 us
  blocking collectives  144 us (69%)
  starting transfers between devices  29.1 us (14%)
  Pallas kernels  11.9 us (6%)
  waiting for transfers between devices  10.2 us (5%)
  local copies, waits for them, and re-layouts  7.46 us (4%)
  other arithmetic  3.61 us (2%)
    all_to_all x4, blocking collectives, swap(): return lax.all_to_all(blocks, axes, 0, 0, tiled=True)  144 us
    all_to_all x1, starting transfers between devices, swap(): return lax.all_to_all(blocks, axes, 0, 0, tiled=True)  16.5 us
    ppermute x2, starting transfers between devices, other_core(): return lax.ppermute(values, 'core', [(0, 1), (1, 0)])  12.6 us
    pallas_call x8, Pallas kernels, call(): pl.pallas_call(body, out_shape=[jax.ShapeDtypeStruct(shape, dtype) for sh...  11.9 us
    all_to_all x1, waiting for transfers between devices, swap(): return lax.all_to_all(blocks, axes, 0, 0, tiled=True)  8.36 us
    unnamed x15, local copies, waits for them, and re-layouts  5.02 us
  transfers between devices with their start and end apart: 3, of which 3 were waited for; matrix products, arithmetic and copies ran while one was open for 4% of the time, Pallas kernels for 0%

profile of v4, /device:TPU:1, one launch (start us, length us, event | category | flops | bytes accessed | tf_op | source)
XLA Modules:
  0.0 208.5 jit_solution(2460684987770186005)
XLA Ops:
  0.7 0.9 copy-done
  1.6 0.9 copy-done.1
  3.2 1.7 shard_map.110
  4.9 16.5 %all-to-all-start = ((bf16[32,16,384]{2,1,0:T(8,128)(2,1)}), bf16[32,16,384]{2,1,0:T(8,128)(2,1)S(1)}, u32[]{:S(2)}, u32[]{:S(2)}) async-start(bf16[32,16,384]{2,1,0:T(8,128)(2,1)} %bitcast.2), calls=%async_computation | async-start | bytes 786432 | tf_op jit(solution)/shard_map/all_to_all | solution.py:26
  21.4 1.8 reshape.56
  23.6 1.3 reduce
  25.2 2.2 %reduce.1 = bf16[110592]{0:T(1024)(128)(2,1)S(1)} reduce(bf16[1,110592]{1,0:T(2,128)(2,1)} %param.12, bf16[]{:T(256)} %constant.33), dimensions={0}, to_apply=%param.12.reduce_sub_computation | reduce | bytes 442370 | tf_op args[5]
  27.6 8.4 %all-to-all-done = bf16[32,16,384]{2,1,0:T(8,128)(2,1)S(1)} async-done(((bf16[32,16,384]{2,1,0:T(8,128)(2,1)}), bf16[32,16,384]{2,1,0:T(8,128)(2,1)S(1)}, u32[]{:S(2)}, u32[]{:S(2)}) %all-to-all-start) | async-done | bytes 393248 | tf_op jit(solution)/shard_map/all_to_all | solution.py:26
  36.6 48.4 %all_to_all.25.refs_1_.refs_2_ = bf16[8,192,1216]{2,1,0:T(8,128)(2,1)S(1)} all-to-all(bf16[8,192,1216]{2,1,0:T(8,128)(2,1)S(1)} %get-tuple-element.31), channel_id=1, replica_groups=mesh['zh'=4,'yh'=4,'yl'=2,'core'=2,'x'=4,'zl'=2] {'x','zl'}, dimensions={0} | all-to-all | bytes 7471104 | tf_op jit(solution)/shard_map/all_to_all | solution.py:26
  85.0 3.2 %shard_map.112 = (bf16[192,512]{1,0:T(8,128)(2,1)S(1)}, bf16[192,512]{1,0:T(8,128)(2,1)S(1)}, bf16[192,512]{1,0:T(8,128)(2,1)S(1)}, bf16[8,192,704]{2,1,0:T(8,128)(2,1)S(1)}) custom-call(s32[1]{0:T(128)} %bitcast.4.refs_0_, bf16[8,192,1216]{2,1,0:T(8,128)(2,1)S(1)} %all_to_all.25.refs_1_.refs_2_, bf16[192,512]{1,0:T(8,128)(2,1)S(1)} %get-tuple-element.32.refs_2_.refs_4_, ...), custom_call_target="tpu_custom_call" | custom-call | tf_op jit(solution)/shard_map/pallas_call | solution.py:56
  88.2 27.9 %all_to_all.26.refs_1_ = bf16[8,192,704]{2,1,0:T(8,128)(2,1)S(1)} all-to-all(bf16[8,192,704]{2,1,0:T(8,128)(2,1)S(1)} %get-tuple-element.35), channel_id=1, replica_groups=mesh['zh'=4,'yh'=4,'yl'=2,'core'=2,'x'=4,'zl'=2] {'x','zl'}, dimensions={0} | all-to-all | bytes 4325376 | tf_op jit(solution)/shard_map/all_to_all | solution.py:26
  116.1 3.0 %shard_map.113 = (bf16[192,512]{1,0:T(8,128)(2,1)S(1)}, f32[3296,128]{1,0:T(8,128)S(1)}, bf16[3296,128]{1,0:T(8,128)(2,1)S(1)}) custom-call(s32[1]{0:T(128)} %bitcast.5.refs_0_, bf16[8,192,704]{2,1,0:T(8,128)(2,1)S(1)} %all_to_all.26.refs_1_, bf16[8,192,1216]{2,1,0:T(8,128)(2,1)S(1)} %all_to_all.25.refs_1_.refs_2_, ...), custom_call_target="tpu_custom_call" | custom-call | tf_op jit(solution)/shard_map/pallas_call | solution.py:56
  119.1 7.2 %collective-permute-start = (bf16[3296,128]{1,0:T(8,128)(2,1)S(1)}, bf16[3296,128]{1,0:T(8,128)(2,1)S(1)}, u32[]{:S(2)}, u32[]{:S(2)}) collective-permute-start(bf16[3296,128]{1,0:T(8,128)(2,1)S(1)} %get-tuple-element.41), channel_id=1, source_target_pairs={{0,8},{8,0},{1,9},{9,1},{2,10},{10,2},{3,11},{11,3},{4,12},{12,4},... | collective-permute-start | bytes 2531336 | tf_op jit(solution)/shard_map/ppermute | solution.py:30
  126.3 0.9 shard_map.114.refs_2_
  127.2 1.1 collective-permute-done.refs_1_
  128.3 0.8 shard_map.115
  129.1 35.3 %all_to_all.27.refs_0_ = bf16[32,128,128]{2,1,0:T(8,128)(2,1)S(1)} all-to-all(bf16[32,128,128]{2,1,0:T(8,128)(2,1)S(1)} %shard_map.115), channel_id=1, replica_groups=mesh['zh'=4,'yh'=4,'yl'=2,'core'=2,'x'=4,'zl'=2] {'zh','yh','yl'}, dimensions={0} | all-to-all | bytes 2097152 | tf_op jit(solution)/shard_map/all_to_all | solution.py:26
  164.6 32.8 %all_to_all.28.refs_1_ = bf16[32,104,128]{2,1,0:T(8,128)(2,1)S(1)} all-to-all(bf16[32,104,128]{2,1,0:T(8,128)(2,1)S(1)} %shard_map.116), channel_id=1, replica_groups=mesh['zh'=4,'yh'=4,'yl'=2,'core'=2,'x'=4,'zl'=2] {'zh','yh','yl'}, dimensions={0} | all-to-all | bytes 1703936 | tf_op jit(solution)/shard_map/all_to_all | solution.py:26
  197.4 5.4 %collective-permute-start.1 = (bf16[32,104,128]{2,1,0:T(8,128)(2,1)S(1)}, bf16[32,104,128]{2,1,0:T(8,128)(2,1)S(1)}, u32[]{:S(2)}, u32[]{:S(2)}) collective-permute-start(bf16[32,104,128]{2,1,0:T(8,128)(2,1)S(1)} %all_to_all.28.refs_1_), channel_id=1, source_target_pairs={{0,8},{8,0},{1,9},{9,1},{2,10},{10,2},{3,11},{11,3},{4,12},{12,4},... | collective-permute-start | bytes 2555912 | tf_op jit(solution)/shard_map/ppermute | solution.py:30
  203.0 1.1 convolution_convert_fusion
  204.1 0.7 collective-permute-done.1.refs_2_
  204.8 1.6 shard_map.117
  206.3 1.1 copy.15
  207.4 1.1 copy.16
  (20 shorter events, 2.5 us)
Async XLA Ops:
  0.6 0.9 copy-start
  1.6 0.9 copy-start.1
  2.5 0.7 copy-start.2
  3.2 20.2 %copy-start.4 = (bf16[192,1536]{1,0:T(8,128)(2,1)S(1)}, bf16[192,1536]{1,0:T(8,128)(2,1)}, u32[]{:S(2)}) copy-start(bf16[192,1536]{1,0:T(8,128)(2,1)} %param.11) | copy-start | bytes 1769476
  4.9 31.1 %all-to-all-start = ((bf16[32,16,384]{2,1,0:T(8,128)(2,1)}), bf16[32,16,384]{2,1,0:T(8,128)(2,1)S(1)}, u32[]{:S(2)}, u32[]{:S(2)}) async-start(bf16[32,16,384]{2,1,0:T(8,128)(2,1)} %bitcast.2), calls=%async_computation | async-start | bytes 786432 | tf_op jit(solution)/shard_map/all_to_all | solution.py:26
  21.4 2.3 %copy-start.5 = (bf16[1,110592]{1,0:T(2,128)(2,1)S(1)}, bf16[1,110592]{1,0:T(2,128)(2,1)}, u32[]{:S(2)}) copy-start(bf16[1,110592]{1,0:T(2,128)(2,1)} %param.10) | copy-start | bytes 663556
  119.1 9.1 %collective-permute-start = (bf16[3296,128]{1,0:T(8,128)(2,1)S(1)}, bf16[3296,128]{1,0:T(8,128)(2,1)S(1)}, u32[]{:S(2)}, u32[]{:S(2)}) collective-permute-start(bf16[3296,128]{1,0:T(8,128)(2,1)S(1)} %get-tuple-element.41), channel_id=1, source_target_pairs={{0,8},{8,0},{1,9},{9,1},{2,10},{10,2},{3,11},{11,3},{4,12},{12,4},... | collective-permute-start | bytes 2531336 | tf_op jit(solution)/shard_map/ppermute | solution.py:30
  129.1 73.7 %copy-start.3 = (s32[512]{0:T(512)S(1)}, s32[512]{0:T(512)}, u32[]{:S(2)}) copy-start(s32[512]{0:T(512)} %param.8) | copy-start | bytes 6148
  197.4 7.4 %collective-permute-start.1 = (bf16[32,104,128]{2,1,0:T(8,128)(2,1)S(1)}, bf16[32,104,128]{2,1,0:T(8,128)(2,1)S(1)}, u32[]{:S(2)}, u32[]{:S(2)}) collective-permute-start(bf16[32,104,128]{2,1,0:T(8,128)(2,1)S(1)} %all_to_all.28.refs_1_), channel_id=1, source_target_pairs={{0,8},{8,0},{1,9},{9,1},{2,10},{10,2},{3,11},{11,3},{4,12},{12,4},... | collective-permute-start | bytes 2555912 | tf_op jit(solution)/shard_map/ppermute | solution.py:30

commit v5 on v4

--- a/solution.py
+++ b/solution.py
@@ -107,7 +107,18 @@
     out_ref[...] = both.T.astype(BF)
 
 
-def near_kernel(tokens_ref, weight_ref, blocks_ref, out_ref, hidden_ref, start_ref):
+def pieces_kernel(own_ref, weight_ref, *refs):
+    outs, slots_ref = refs[:8], refs[8]
+    own = own_ref[0]
+    for j in range(8):
+        step = (j // 2 + 4 - own // 2) % 4
+        flip = (j % 2 + own) % 2
+        slots_ref[2 * step + flip] = weight_ref[:, j * CG : (j + 1) * CG]
+    for j in range(8):
+        outs[j][...] = slots_ref[j]
+
+
+def near_kernel(tokens_ref, weight_ref, out_ref, hidden_ref, start_ref):
     rows = tokens_ref[...].astype(F32)
     both = rows.T
     start_ref[...] = both[:CG].astype(BF)
@@ -125,11 +136,11 @@
     act = (hidden * jax.nn.sigmoid(hidden)).astype(BF)
     for j in range(8):
         out_ref[j, :, :TOK] = act
-        out_ref[j, :, TOK : 2 * TOK] = cot
-        out_ref[j, :, 2 * TOK :] = blocks_ref[j]
-
-
-def mid_kernel(own_ref, sent_ref, start_ref, pointwise_ref, weight_ref, middle_ref, dh_ref, grad_ref, out_ref):
+        out_ref[j, :, TOK:] = cot
+
+
+def mid_kernel(own_ref, sent_ref, start_ref, pointwise_ref, weight_ref, *refs):
+    columns, (middle_ref, dh_ref, grad_ref, out_ref) = refs[:8], refs[8:]
     middle = start_ref[...].astype(F32) + sum(
         mm(pointwise_ref[j * CG : (j + 1) * CG], sent_ref[j, :, :TOK], 0, 0) for j in range(8)
     )
@@ -144,15 +155,23 @@
     s = jax.nn.sigmoid(hidden)
     act = (hidden * s).astype(BF)
     for j in range(8):
-        out_ref[j, :, TOK:] = mm(sent_ref[j, :, TOK : 2 * TOK], act, 1, 1).astype(BF)
-    da = sum(mm(sent_ref[j, :, 2 * TOK :], sent_ref[j, :, TOK : 2 * TOK], 0, 0) for j in range(8))
+        grad = mm(sent_ref[j, :, TOK:], act, 1, 1)
+        rest = grad[:, 128:]
+        rows = jnp.concatenate([grad[:, :128], jnp.concatenate([rest[:96], rest[96:]], axis=1)], axis=0)
+        for part in range(4):
+            out_ref[j, CG:, 128 * part : 128 * (part + 1)] = rows[72 * part : 72 * (part + 1)].astype(BF)
+    own = own_ref[0]
+    da = jnp.zeros((CG, TOK), F32)
+    for j in range(8):
+        source = 2 * ((own // 2 + 4 - j // 2) % 4) + (own + j) % 2
+        da = da + mm(columns[j][...], sent_ref[source, :, TOK:], 0, 0)
     dh = (da * s * (1.0 + hidden * (1.0 - s))).astype(BF)
     dh_ref[...] = dh
     back = conv_back(dh.astype(F32), weight_ref, FAR)
-    grad = (sent_ref[own_ref[0], :, TOK : 2 * TOK].astype(F32) + back).astype(BF)
+    grad = (sent_ref[own, :, TOK:].astype(F32) + back).astype(BF)
     grad_ref[...] = grad
     for j in range(8):
-        out_ref[j, :, :TOK] = mm(pointwise_ref[j * CG : (j + 1) * CG], grad, 1, 0).astype(BF)
+        out_ref[j, :CG] = mm(pointwise_ref[j * CG : (j + 1) * CG], grad, 1, 0).astype(BF)
 
 
 def back_kernel(
@@ -169,8 +188,12 @@
     other_ref,
     far_rows_ref,
     near_rows_ref,
+    seq_ref,
 ):
-    da = sum(got_ref[j, :, :TOK].astype(F32) for j in range(8))
+    for j in range(8):
+        for part in range(4):
+            seq_ref[j, 72 * part : 72 * (part + 1)] = got_ref[j, CG:, 128 * part : 128 * (part + 1)].astype(F32)
+    da = sum(got_ref[j, :CG].astype(F32) for j in range(8))
     hidden = hidden_ref[...]
     s = jax.nn.sigmoid(hidden)
     dh = (da * s * (1.0 + hidden * (1.0 - s))).astype(BF)
@@ -186,13 +209,14 @@
         out_ref[1152:1584] = far_rows_ref[rows].astype(out_ref.dtype)
         out_ref[1584:2016] = near_rows_ref[rows].astype(out_ref.dtype)
         for j in range(8):
-            half = got_ref[j, pl.ds(pl.multiple_of(96 * core, 16), 96), TOK:].astype(F32)
+            wide = seq_ref[j, pl.ds(pl.multiple_of(96 * core, 8), 96)]
+            thin = jnp.where(core == 0, seq_ref[j, CG:, :64], seq_ref[j, CG:, 64:])
             for part in range(4):
-                piece = half[24 * part : 24 * (part + 1)]
-                rest = piece[:, 128:]
+                piece = wide[24 * part : 24 * (part + 1)]
+                rest = thin[24 * part : 24 * (part + 1)]
                 packed = jnp.concatenate([rest[:8], rest[8:16]], axis=1), jnp.concatenate([rest[16:], blank], axis=1)
                 at = 2016 + 160 * j + 40 * part
-                out_ref[at : at + 40] = jnp.concatenate([piece[:, :128], *packed], axis=0).astype(out_ref.dtype)
+                out_ref[at : at + 40] = jnp.concatenate([piece, *packed], axis=0).astype(out_ref.dtype)
 
 
 def tokens_kernel(dh_ref, weight_ref, grad_ref, out_ref):
@@ -257,29 +281,34 @@
     far_pw_ref[...] = far_ref[...].astype(BF)
 
 
-def local(emb, order, cot, cw1, pw1, cw2, pw2):
+def step(emb, order, cot, cw1, pw1, cw2, pw2):
     core = lax.axis_index("core").astype(jnp.int32).reshape(1)
     own = lax.axis_index(GRP).astype(jnp.int32).reshape(1)
     base = (lax.axis_index(SEQ) * TOK).astype(jnp.int32).reshape(1)
 
     (packed,) = call(pack_kernel, [((TOK, 2 * CG), BF)], (base,), (), (order.reshape(1, TOK), emb, cot), space=pltpu.HBM)
     packed = swap(packed.reshape(32, TOK // 32, 2 * CG), CHIPS).reshape(TOK, 2 * CG)
-    packed, own, core, w1, w2, pw1t, pw2_blocks = lax.optimization_barrier(
-        (packed, own, core, cw1.reshape(3, CG, CG), cw2.reshape(3, CG, CG), pw1.T, pw2.reshape(CG, 8, CG).transpose(1, 0, 2))
+    pieces = call(pieces_kernel, [((CG, CG), BF)] * 8, (own,), (), (pw2,), scratch=[((8, CG, CG), BF)])
+    columns = [pieces[0]]
+    for j in range(1, 8):
+        route = [(a, 2 * ((a // 2 + j // 2) % 4) + (a + j) % 2) for a in range(8)]
+        columns.append(lax.ppermute(pieces[j], GRP, route))
+    packed, own, core, w1, w2, pw1t, columns = lax.optimization_barrier(
+        (packed, own, core, cw1.reshape(3, CG, CG), cw2.reshape(3, CG, CG), pw1.T, columns)
     )
     sent, near_hidden, start = call(
         near_kernel,
-        [((8, CG, 2 * TOK + CG), BF), ((CG, TOK), F32), ((CG, TOK), BF)],
+        [((8, CG, 2 * TOK), BF), ((CG, TOK), F32), ((CG, TOK), BF)],
         (),
-        (packed, w1, pw2_blocks),
+        (packed, w1),
     )
     sent = swap(sent, GRP)
     middle, far_dh, grad_middle, parts = call(
         mid_kernel,
-        [((CG, TOK), BF), ((CG, TOK), BF), ((CG, TOK), BF), ((8, CG, TOK + CG), BF)],
+        [((CG, TOK), BF), ((CG, TOK), BF), ((CG, TOK), BF), ((8, CG + 72, TOK), BF)],
         (own,),
         (sent,),
-        (start, pw1t, w2),
+        (start, pw1t, w2, *columns),
     )
     got = swap(parts, GRP)
 
@@ -289,7 +318,7 @@
         (core,),
         (got, sent),
         (near_hidden, start, grad_middle, middle, far_dh),
-        scratch=[((864, 128), F32), ((864, 128), F32)],
+        scratch=[((864, 128), F32), ((864, 128), F32), ((8, 288, 128), F32)],
     )
     other = other_core(other)
     (tokens,) = call(tokens_kernel, [((32, 24, 128), BF)], (), (near_dh,), (w1, grad_middle))
@@ -327,7 +356,7 @@
     fine = Mesh(mesh.devices.reshape(4, 4, 2, 2, 4, 2), SEQ + GRP)
     placed = (P(GRP, SEQ), P(SEQ), P(GRP, SEQ), P(GRP, None), P(GRP, None), P(GRP, None), P(GRP, None))
     return jax.shard_map(
-        local,
+        step,
         mesh=fine,
         in_specs=placed,
         out_specs=(P(GRP, SEQ), P(GRP, None), P(GRP, None), P(GRP, None), P(GRP, None)),

time: 210 us -> 216 us (1.029)
  starting transfers between devices: 29.1 us -> 51.9 us
  blocking collectives: 144 us -> 135 us
  waiting for transfers between devices: 10.2 us -> 1.82 us
    ppermute x0 -> x7, starting transfers between devices: none -> 22.6 us  [step(): columns.append(lax.ppermute(pieces[j], GRP, route))]
    all_to_all x4, blocking collectives: 144 us -> 135 us  [swap(): return lax.all_to_all(blocks, axes, 0, 0, tiled=True)]
    all_to_all x1, waiting for transfers between devices: 8.36 us -> 0.01 us  [swap(): return lax.all_to_all(blocks, axes, 0, 0, tiled=True)]
    pallas_call x8 -> x9, Pallas kernels: 11.9 us -> 13.5 us  [call(): pl.pallas_call(body, out_shape=[jax.ShapeDtypeStruct(shape, dtype) for sh...]
    unnamed x15 -> x17, local copies, waits for them, and re-layouts: 5.02 us -> 6.07 us
  transfers between devices with their start and end apart: 3 -> 10, of which waited for: 3 -> 2; matrix products, arithmetic and copies ran while one was open for 4% -> 3% of each run, Pallas kernels for 0% -> 1%
where the time goes in v5:
time: 216 us; the launch traced here: 215 us
  blocking collectives  135 us (62%)
  starting transfers between devices  51.9 us (24%)
  Pallas kernels  13.5 us (6%)
  local copies, waits for them, and re-layouts  6.58 us (3%)
  other arithmetic  3.61 us (2%)
    all_to_all x4, blocking collectives, swap(): return lax.all_to_all(blocks, axes, 0, 0, tiled=True)  135 us
    ppermute x7, starting transfers between devices, step(): columns.append(lax.ppermute(pieces[j], GRP, route))  22.6 us
    all_to_all x1, starting transfers between devices, swap(): return lax.all_to_all(blocks, axes, 0, 0, tiled=True)  16.5 us
    pallas_call x9, Pallas kernels, call(): pl.pallas_call(body, out_shape=[jax.ShapeDtypeStruct(shape, dtype) for sh...  13.5 us
    ppermute x2, starting transfers between devices, other_core(): return lax.ppermute(values, 'core', [(0, 1), (1, 0)])  12.8 us
    unnamed x17, local copies, waits for them, and re-layouts  6.07 us
  transfers between devices with their start and end apart: 10, of which 2 were waited for; matrix products, arithmetic and copies ran while one was open for 3% of the time, Pallas kernels for 1%

profile of v5, /device:TPU:1, one launch (start us, length us, event | category | flops | bytes accessed | tf_op | source)
XLA Modules:
  0.0 214.6 jit_solution(6617816560379694349)
XLA Ops:
  3.2 1.7 shard_map.110
  4.9 16.5 %all-to-all-start = ((bf16[32,16,384]{2,1,0:T(8,128)(2,1)}), bf16[32,16,384]{2,1,0:T(8,128)(2,1)S(1)}, u32[]{:S(2)}, u32[]{:S(2)}) async-start(bf16[32,16,384]{2,1,0:T(8,128)(2,1)} %bitcast.2), calls=%async_computation | async-start | bytes 786432 | tf_op jit(solution)/shard_map/all_to_all | solution.py:26
  22.8 3.1 %collective-permute-start = (bf16[192,192]{1,0:T(8,128)(2,1)S(1)}, bf16[192,192]{1,0:T(8,128)(2,1)S(1)}, u32[]{:S(2)}, u32[]{:S(2)}) collective-permute-start(bf16[192,192]{1,0:T(8,128)(2,1)S(1)} %get-tuple-element.42), channel_id=1, source_target_pairs={{0,1},{1,0},{2,3},{3,2},{4,5},{5,4},{6,7},{7,6},{8,9},{9,8},{10,11... | collective-permute-start | bytes 221192 | tf_op jit(solution)/shard_map/ppermute | solution.py:295
  25.9 3.1 %collective-permute-start.1 = (bf16[192,192]{1,0:T(8,128)(2,1)S(1)}, bf16[192,192]{1,0:T(8,128)(2,1)S(1)}, u32[]{:S(2)}, u32[]{:S(2)}) collective-permute-start(bf16[192,192]{1,0:T(8,128)(2,1)S(1)} %get-tuple-element.43), channel_id=1, source_target_pairs={{0,2},{1,3},{2,4},{3,5},{4,6},{5,7},{6,0},{7,1},{8,10},{9,11},{10,... | collective-permute-start | bytes 221192 | tf_op jit(solution)/shard_map/ppermute | solution.py:295
  29.0 3.1 %collective-permute-start.2 = (bf16[192,192]{1,0:T(8,128)(2,1)S(1)}, bf16[192,192]{1,0:T(8,128)(2,1)S(1)}, u32[]{:S(2)}, u32[]{:S(2)}) collective-permute-start(bf16[192,192]{1,0:T(8,128)(2,1)S(1)} %get-tuple-element.44), channel_id=1, source_target_pairs={{0,3},{1,2},{2,5},{3,4},{4,7},{5,6},{6,1},{7,0},{8,11},{9,10},{10,... | collective-permute-start | bytes 221192 | tf_op jit(solution)/shard_map/ppermute | solution.py:295
  32.2 3.3 %collective-permute-start.3 = (bf16[192,192]{1,0:T(8,128)(2,1)S(1)}, bf16[192,192]{1,0:T(8,128)(2,1)S(1)}, u32[]{:S(2)}, u32[]{:S(2)}) collective-permute-start(bf16[192,192]{1,0:T(8,128)(2,1)S(1)} %get-tuple-element.45), channel_id=1, source_target_pairs={{0,4},{1,5},{2,6},{3,7},{4,0},{5,1},{6,2},{7,3},{8,12},{9,13},{10,... | collective-permute-start | bytes 221192 | tf_op jit(solution)/shard_map/ppermute | solution.py:295
  35.5 4.4 %collective-permute-start.4 = (bf16[192,192]{1,0:T(8,128)(2,1)S(1)}, bf16[192,192]{1,0:T(8,128)(2,1)S(1)}, u32[]{:S(2)}, u32[]{:S(2)}) collective-permute-start(bf16[192,192]{1,0:T(8,128)(2,1)S(1)} %get-tuple-element.46), channel_id=1, source_target_pairs={{0,5},{1,4},{2,7},{3,6},{4,1},{5,0},{6,3},{7,2},{8,13},{9,12},{10,... | collective-permute-start | bytes 221192 | tf_op jit(solution)/shard_map/ppermute | solution.py:295
  39.9 3.4 %collective-permute-start.5 = (bf16[192,192]{1,0:T(8,128)(2,1)S(1)}, bf16[192,192]{1,0:T(8,128)(2,1)S(1)}, u32[]{:S(2)}, u32[]{:S(2)}) collective-permute-start(bf16[192,192]{1,0:T(8,128)(2,1)S(1)} %get-tuple-element.47), channel_id=1, source_target_pairs={{0,6},{1,7},{2,0},{3,1},{4,2},{5,3},{6,4},{7,5},{8,14},{9,15},{10,... | collective-permute-start | bytes 221192 | tf_op jit(solution)/shard_map/ppermute | solution.py:295
  43.3 2.2 %collective-permute-start.6 = (bf16[192,192]{1,0:T(8,128)(2,1)S(1)}, bf16[192,192]{1,0:T(8,128)(2,1)S(1)}, u32[]{:S(2)}, u32[]{:S(2)}) collective-permute-start(bf16[192,192]{1,0:T(8,128)(2,1)S(1)} %get-tuple-element.48), channel_id=1, source_target_pairs={{0,7},{1,6},{2,1},{3,0},{4,3},{5,2},{6,5},{7,4},{8,15},{9,14},{10,... | collective-permute-start | bytes 221192 | tf_op jit(solution)/shard_map/ppermute | solution.py:295
  45.7 1.3 reduce
  47.3 2.2 %reduce.1 = bf16[110592]{0:T(1024)(128)(2,1)S(1)} reduce(bf16[1,110592]{1,0:T(2,128)(2,1)} %param.12, bf16[]{:T(256)} %constant.33), dimensions={0}, to_apply=%param.12.reduce_sub_computation | reduce | bytes 442370 | tf_op args[5]
  50.4 38.6 %all_to_all.25.refs_1_.refs_2_ = bf16[8,192,1024]{2,1,0:T(8,128)(2,1)S(1)} all-to-all(bf16[8,192,1024]{2,1,0:T(8,128)(2,1)S(1)} %get-tuple-element.53), channel_id=1, replica_groups=mesh['zh'=4,'yh'=4,'yl'=2,'core'=2,'x'=4,'zl'=2] {'x','zl'}, dimensions={0} | all-to-all | bytes 6291456 | tf_op jit(solution)/shard_map/all_to_all | solution.py:26
  89.0 4.3 %shard_map.113 = (bf16[192,512]{1,0:T(8,128)(2,1)S(1)}, bf16[192,512]{1,0:T(8,128)(2,1)S(1)}, bf16[192,512]{1,0:T(8,128)(2,1)S(1)}, bf16[8,264,512]{2,1,0:T(8,128)(2,1)S(1)}) custom-call(s32[1]{0:T(128)} %bitcast.4.refs_0_, bf16[8,192,1024]{2,1,0:T(8,128)(2,1)S(1)} %all_to_all.25.refs_1_.refs_2_, bf16[192,512]{1,0:T(8,128)(2,1)S(1)} %get-tuple-element.54.refs_2_.refs_4_, ...), custom_call_target="tpu_custom_call" | custom-call | tf_op jit(solution)/shard_map/pallas_call | solution.py:56
  93.3 26.0 %all_to_all.26.refs_1_ = bf16[8,264,512]{2,1,0:T(8,128)(2,1)S(1)} all-to-all(bf16[8,264,512]{2,1,0:T(8,128)(2,1)S(1)} %get-tuple-element.65), channel_id=1, replica_groups=mesh['zh'=4,'yh'=4,'yl'=2,'core'=2,'x'=4,'zl'=2] {'x','zl'}, dimensions={0} | all-to-all | bytes 4325376 | tf_op jit(solution)/shard_map/all_to_all | solution.py:26
  119.3 3.1 %shard_map.114 = (bf16[192,512]{1,0:T(8,128)(2,1)S(1)}, f32[3296,128]{1,0:T(8,128)S(1)}, bf16[3296,128]{1,0:T(8,128)(2,1)S(1)}) custom-call(s32[1]{0:T(128)} %bitcast.5.refs_0_, bf16[8,264,512]{2,1,0:T(8,128)(2,1)S(1)} %all_to_all.26.refs_1_, bf16[8,192,1024]{2,1,0:T(8,128)(2,1)S(1)} %all_to_all.25.refs_1_.refs_2_, ...), custom_call_target="tpu_custom_call" | custom-call | tf_op jit(solution)/shard_map/pallas_call | solution.py:56
  122.4 7.0 %collective-permute-start.7 = (bf16[3296,128]{1,0:T(8,128)(2,1)S(1)}, bf16[3296,128]{1,0:T(8,128)(2,1)S(1)}, u32[]{:S(2)}, u32[]{:S(2)}) collective-permute-start(bf16[3296,128]{1,0:T(8,128)(2,1)S(1)} %get-tuple-element.71), channel_id=1, source_target_pairs={{0,8},{8,0},{1,9},{9,1},{2,10},{10,2},{3,11},{11,3},{4,12},{12,4},... | collective-permute-start | bytes 2531336 | tf_op jit(solution)/shard_map/ppermute | solution.py:30
  130.3 1.1 collective-permute-done.7.refs_1_
  132.2 38.3 %all_to_all.27.refs_0_ = bf16[32,128,128]{2,1,0:T(8,128)(2,1)S(1)} all-to-all(bf16[32,128,128]{2,1,0:T(8,128)(2,1)S(1)} %shard_map.116), channel_id=1, replica_groups=mesh['zh'=4,'yh'=4,'yl'=2,'core'=2,'x'=4,'zl'=2] {'zh','yh','yl'}, dimensions={0} | all-to-all | bytes 2097152 | tf_op jit(solution)/shard_map/all_to_all | solution.py:26
  170.7 32.4 %all_to_all.28.refs_1_ = bf16[32,104,128]{2,1,0:T(8,128)(2,1)S(1)} all-to-all(bf16[32,104,128]{2,1,0:T(8,128)(2,1)S(1)} %shard_map.117), channel_id=1, replica_groups=mesh['zh'=4,'yh'=4,'yl'=2,'core'=2,'x'=4,'zl'=2] {'zh','yh','yl'}, dimensions={0} | all-to-all | bytes 1703936 | tf_op jit(solution)/shard_map/all_to_all | solution.py:26
  203.1 5.8 %collective-permute-start.8 = (bf16[32,104,128]{2,1,0:T(8,128)(2,1)S(1)}, bf16[32,104,128]{2,1,0:T(8,128)(2,1)S(1)}, u32[]{:S(2)}, u32[]{:S(2)}) collective-permute-start(bf16[32,104,128]{2,1,0:T(8,128)(2,1)S(1)} %all_to_all.28.refs_1_), channel_id=1, source_target_pairs={{0,8},{8,0},{1,9},{9,1},{2,10},{10,2},{3,11},{11,3},{4,12},{12,4},... | collective-permute-start | bytes 2555912 | tf_op jit(solution)/shard_map/ppermute | solution.py:30
  209.1 1.1 convolution_convert_fusion
  210.9 1.6 shard_map.118
  212.4 1.1 copy.13
  213.5 1.1 copy.14
  (35 shorter events, 8.0 us)
Async XLA Ops:
  0.6 0.9 copy-start.1
  1.6 0.9 copy-start.2
  2.5 0.7 copy-start.3
  3.2 42.3 %copy-start.5 = (bf16[192,1536]{1,0:T(8,128)(2,1)S(1)}, bf16[192,1536]{1,0:T(8,128)(2,1)}, u32[]{:S(2)}) copy-start(bf16[192,1536]{1,0:T(8,128)(2,1)} %param.11) | copy-start | bytes 1769476
  3.2 42.5 %copy-start.6 = (bf16[1,110592]{1,0:T(2,128)(2,1)S(1)}, bf16[1,110592]{1,0:T(2,128)(2,1)}, u32[]{:S(2)}) copy-start(bf16[1,110592]{1,0:T(2,128)(2,1)} %param.10) | copy-start | bytes 663556
  4.9 44.9 %all-to-all-start = ((bf16[32,16,384]{2,1,0:T(8,128)(2,1)}), bf16[32,16,384]{2,1,0:T(8,128)(2,1)S(1)}, u32[]{:S(2)}, u32[]{:S(2)}) async-start(bf16[32,16,384]{2,1,0:T(8,128)(2,1)} %bitcast.2), calls=%async_computation | async-start | bytes 786432 | tf_op jit(solution)/shard_map/all_to_all | solution.py:26
  21.4 1.1 copy-start
  22.8 17.1 %collective-permute-start = (bf16[192,192]{1,0:T(8,128)(2,1)S(1)}, bf16[192,192]{1,0:T(8,128)(2,1)S(1)}, u32[]{:S(2)}, u32[]{:S(2)}) collective-permute-start(bf16[192,192]{1,0:T(8,128)(2,1)S(1)} %get-tuple-element.42), channel_id=1, source_target_pairs={{0,1},{1,0},{2,3},{3,2},{4,5},{5,4},{6,7},{7,6},{8,9},{9,8},{10,11... | collective-permute-start | bytes 221192 | tf_op jit(solution)/shard_map/ppermute | solution.py:295
  25.9 17.4 %collective-permute-start.1 = (bf16[192,192]{1,0:T(8,128)(2,1)S(1)}, bf16[192,192]{1,0:T(8,128)(2,1)S(1)}, u32[]{:S(2)}, u32[]{:S(2)}) collective-permute-start(bf16[192,192]{1,0:T(8,128)(2,1)S(1)} %get-tuple-element.43), channel_id=1, source_target_pairs={{0,2},{1,3},{2,4},{3,5},{4,6},{5,7},{6,0},{7,1},{8,10},{9,11},{10,... | collective-permute-start | bytes 221192 | tf_op jit(solution)/shard_map/ppermute | solution.py:295
  29.0 20.7 %collective-permute-start.2 = (bf16[192,192]{1,0:T(8,128)(2,1)S(1)}, bf16[192,192]{1,0:T(8,128)(2,1)S(1)}, u32[]{:S(2)}, u32[]{:S(2)}) collective-permute-start(bf16[192,192]{1,0:T(8,128)(2,1)S(1)} %get-tuple-element.44), channel_id=1, source_target_pairs={{0,3},{1,2},{2,5},{3,4},{4,7},{5,6},{6,1},{7,0},{8,11},{9,10},{10,... | collective-permute-start | bytes 221192 | tf_op jit(solution)/shard_map/ppermute | solution.py:295
  32.2 17.6 %collective-permute-start.3 = (bf16[192,192]{1,0:T(8,128)(2,1)S(1)}, bf16[192,192]{1,0:T(8,128)(2,1)S(1)}, u32[]{:S(2)}, u32[]{:S(2)}) collective-permute-start(bf16[192,192]{1,0:T(8,128)(2,1)S(1)} %get-tuple-element.45), channel_id=1, source_target_pairs={{0,4},{1,5},{2,6},{3,7},{4,0},{5,1},{6,2},{7,3},{8,12},{9,13},{10,... | collective-permute-start | bytes 221192 | tf_op jit(solution)/shard_map/ppermute | solution.py:295
  35.5 14.2 %collective-permute-start.4 = (bf16[192,192]{1,0:T(8,128)(2,1)S(1)}, bf16[192,192]{1,0:T(8,128)(2,1)S(1)}, u32[]{:S(2)}, u32[]{:S(2)}) collective-permute-start(bf16[192,192]{1,0:T(8,128)(2,1)S(1)} %get-tuple-element.46), channel_id=1, source_target_pairs={{0,5},{1,4},{2,7},{3,6},{4,1},{5,0},{6,3},{7,2},{8,13},{9,12},{10,... | collective-permute-start | bytes 221192 | tf_op jit(solution)/shard_map/ppermute | solution.py:295
  39.9 9.9 %collective-permute-start.5 = (bf16[192,192]{1,0:T(8,128)(2,1)S(1)}, bf16[192,192]{1,0:T(8,128)(2,1)S(1)}, u32[]{:S(2)}, u32[]{:S(2)}) collective-permute-start(bf16[192,192]{1,0:T(8,128)(2,1)S(1)} %get-tuple-element.47), channel_id=1, source_target_pairs={{0,6},{1,7},{2,0},{3,1},{4,2},{5,3},{6,4},{7,5},{8,14},{9,15},{10,... | collective-permute-start | bytes 221192 | tf_op jit(solution)/shard_map/ppermute | solution.py:295
  43.3 6.5 %collective-permute-start.6 = (bf16[192,192]{1,0:T(8,128)(2,1)S(1)}, bf16[192,192]{1,0:T(8,128)(2,1)S(1)}, u32[]{:S(2)}, u32[]{:S(2)}) collective-permute-start(bf16[192,192]{1,0:T(8,128)(2,1)S(1)} %get-tuple-element.48), channel_id=1, source_target_pairs={{0,7},{1,6},{2,1},{3,0},{4,3},{5,2},{6,5},{7,4},{8,15},{9,14},{10,... | collective-permute-start | bytes 221192 | tf_op jit(solution)/shard_map/ppermute | solution.py:295
  122.4 9.0 %collective-permute-start.7 = (bf16[3296,128]{1,0:T(8,128)(2,1)S(1)}, bf16[3296,128]{1,0:T(8,128)(2,1)S(1)}, u32[]{:S(2)}, u32[]{:S(2)}) collective-permute-start(bf16[3296,128]{1,0:T(8,128)(2,1)S(1)} %get-tuple-element.71), channel_id=1, source_target_pairs={{0,8},{8,0},{1,9},{9,1},{2,10},{10,2},{3,11},{11,3},{4,12},{12,4},... | collective-permute-start | bytes 2531336 | tf_op jit(solution)/shard_map/ppermute | solution.py:30
  170.6 38.3 %copy-start.4 = (s32[512]{0:T(512)S(1)}, s32[512]{0:T(512)}, u32[]{:S(2)}) copy-start(s32[512]{0:T(512)} %param.8) | copy-start | bytes 6148
  203.1 7.7 %collective-permute-start.8 = (bf16[32,104,128]{2,1,0:T(8,128)(2,1)S(1)}, bf16[32,104,128]{2,1,0:T(8,128)(2,1)S(1)}, u32[]{:S(2)}, u32[]{:S(2)}) collective-permute-start(bf16[32,104,128]{2,1,0:T(8,128)(2,1)S(1)} %all_to_all.28.refs_1_), channel_id=1, source_target_pairs={{0,8},{8,0},{1,9},{9,1},{2,10},{10,2},{3,11},{11,3},{4,12},{12,4},... | collective-permute-start | bytes 2555912 | tf_op jit(solution)/shard_map/ppermute | solution.py:30

commit v6 on v4

--- a/solution.py
+++ b/solution.py
@@ -99,12 +99,21 @@
         rows_ref[base + 2 * half : base + 3 * half] = odd[:, 64:]
 
 
-def pack_kernel(base_ref, order_ref, emb_ref, cot_ref, out_ref):
+def pack_kernel(base_ref, both_ref, order_ref, out_ref):
     token = lax.broadcasted_iota(jnp.int32, (TOK, TOK), 0)
     onehot = jnp.where(token == order_ref[...] - base_ref[0], 1.0, 0.0).astype(BF)
-    start = mm(emb_ref[...], onehot, 1, 0)
-    both = jnp.concatenate([start, cot_ref[...].astype(F32)], axis=0)
+    start = mm(both_ref[:CG], onehot, 1, 0)
+    both = jnp.concatenate([start, both_ref[CG:].astype(F32)], axis=0)
     out_ref[...] = both.T.astype(BF)
+
+
+def halves_kernel(core_ref, weight_ref, out_ref):
+    half = weight_ref[pl.ds(pl.multiple_of(96 * core_ref[0], 16), 96)].astype(F32)
+    blank = jnp.zeros((96, 64), F32)
+    for j in range(8):
+        block = half[:, CG * j : CG * (j + 1)]
+        out_ref[j, :96] = block[:, :128].astype(BF)
+        out_ref[j, 96:] = jnp.concatenate([block[:, 128:], blank], axis=1).astype(BF)
 
 
 def near_kernel(tokens_ref, weight_ref, blocks_ref, out_ref, hidden_ref, start_ref):
@@ -129,7 +138,7 @@
         out_ref[j, :, 2 * TOK :] = blocks_ref[j]
 
 
-def mid_kernel(own_ref, sent_ref, start_ref, pointwise_ref, weight_ref, middle_ref, dh_ref, grad_ref, out_ref):
+def mid_kernel(sent_ref, start_ref, pointwise_ref, weight_ref, middle_ref, hidden_ref, rows_ref):
     middle = start_ref[...].astype(F32) + sum(
         mm(pointwise_ref[j * CG : (j + 1) * CG], sent_ref[j, :, :TOK], 0, 0) for j in range(8)
     )
@@ -141,18 +150,51 @@
         + mm(weight_ref[1], middle, 0, 0)
         + mm(weight_ref[2], shifted(wide, FAR), 0, 0)
     )
+    hidden_ref[...] = hidden
+    act = (hidden * jax.nn.sigmoid(hidden)).astype(BF)
+    blank = jnp.zeros((64, TOK), BF)
+    lower = jnp.concatenate([act[128:], blank], axis=0)
+    upper = jnp.concatenate([blank, act[128:]], axis=0)
+    for j in range(8):
+        cot = sent_ref[j, :, TOK : 2 * TOK]
+        rows_ref[j, :CG] = mm(cot, act[:128], 1, 1).astype(BF)
+        rows_ref[j, CG:] = (mm(cot[:96], lower, 1, 1) + mm(cot[96:], upper, 1, 1)).astype(BF)
+
+
+def far_kernel(
+    own_ref,
+    core_ref,
+    sent_ref,
+    other_ref,
+    hidden_ref,
+    pointwise_ref,
+    weight_ref,
+    rows_ref,
+    dh_ref,
+    grad_ref,
+    out_ref,
+    columns_ref,
+):
+    core, own = core_ref[0], own_ref[0]
+    mine = pl.ds(pl.multiple_of(96 * core, 16), 96)
+    other = pl.ds(pl.multiple_of(96 - 96 * core, 16), 96)
+    for j in range(8):
+        columns_ref[j, mine, :128] = sent_ref[j, :96, 2 * TOK :]
+        columns_ref[j, mine, 128:] = sent_ref[j, 96:, 2 * TOK : 2 * TOK + 64]
+        columns_ref[j, other, :128] = other_ref[j, :96]
+        columns_ref[j, other, 128:] = other_ref[j, 96:, :64]
+    hidden = hidden_ref[...]
     s = jax.nn.sigmoid(hidden)
-    act = (hidden * s).astype(BF)
-    for j in range(8):
-        out_ref[j, :, TOK:] = mm(sent_ref[j, :, TOK : 2 * TOK], act, 1, 1).astype(BF)
-    da = sum(mm(sent_ref[j, :, 2 * TOK :], sent_ref[j, :, TOK : 2 * TOK], 0, 0) for j in range(8))
+    da = sum(mm(columns_ref[j], sent_ref[j, :, TOK : 2 * TOK], 0, 0) for j in range(8))
     dh = (da * s * (1.0 + hidden * (1.0 - s))).astype(BF)
     dh_ref[...] = dh
     back = conv_back(dh.astype(F32), weight_ref, FAR)
-    grad = (sent_ref[own_ref[0], :, TOK : 2 * TOK].astype(F32) + back).astype(BF)
+    grad = (sent_ref[own, :, TOK : 2 * TOK].astype(F32) + back).astype(BF)
     grad_ref[...] = grad
     for j in range(8):
-        out_ref[j, :, :TOK] = mm(pointwise_ref[j * CG : (j + 1) * CG], grad, 1, 0).astype(BF)
+        out_ref[j, :CG] = mm(pointwise_ref[j * CG : (j + 1) * CG], grad, 1, 0).astype(BF)
+        for part in range(4):
+            out_ref[j, CG:, 128 * part : 128 * (part + 1)] = rows_ref[j, 72 * part : 72 * (part + 1)]
 
 
 def back_kernel(
@@ -169,8 +211,12 @@
     other_ref,
     far_rows_ref,
     near_rows_ref,
+    seq_ref,
 ):
-    da = sum(got_ref[j, :, :TOK].astype(F32) for j in range(8))
+    for j in range(8):
+        for part in range(4):
+            seq_ref[j, 72 * part : 72 * (part + 1)] = got_ref[j, CG:, 128 * part : 128 * (part + 1)].astype(F32)
+    da = sum(got_ref[j, :CG].astype(F32) for j in range(8))
     hidden = hidden_ref[...]
     s = jax.nn.sigmoid(hidden)
     dh = (da * s * (1.0 + hidden * (1.0 - s))).astype(BF)
@@ -186,13 +232,14 @@
         out_ref[1152:1584] = far_rows_ref[rows].astype(out_ref.dtype)
         out_ref[1584:2016] = near_rows_ref[rows].astype(out_ref.dtype)
         for j in range(8):
-            half = got_ref[j, pl.ds(pl.multiple_of(96 * core, 16), 96), TOK:].astype(F32)
+            wide = seq_ref[j, pl.ds(pl.multiple_of(96 * core, 8), 96)]
+            thin = jnp.where(core == 0, seq_ref[j, CG:, :64], seq_ref[j, CG:, 64:])
             for part in range(4):
-                piece = half[24 * part : 24 * (part + 1)]
-                rest = piece[:, 128:]
+                piece = wide[24 * part : 24 * (part + 1)]
+                rest = thin[24 * part : 24 * (part + 1)]
                 packed = jnp.concatenate([rest[:8], rest[8:16]], axis=1), jnp.concatenate([rest[16:], blank], axis=1)
                 at = 2016 + 160 * j + 40 * part
-                out_ref[at : at + 40] = jnp.concatenate([piece[:, :128], *packed], axis=0).astype(out_ref.dtype)
+                out_ref[at : at + 40] = jnp.concatenate([piece, *packed], axis=0).astype(out_ref.dtype)
 
 
 def tokens_kernel(dh_ref, weight_ref, grad_ref, out_ref):
@@ -257,29 +304,39 @@
     far_pw_ref[...] = far_ref[...].astype(BF)
 
 
-def local(emb, order, cot, cw1, pw1, cw2, pw2):
+def step(emb, order, cot, cw1, pw1, cw2, pw2):
     core = lax.axis_index("core").astype(jnp.int32).reshape(1)
     own = lax.axis_index(GRP).astype(jnp.int32).reshape(1)
     base = (lax.axis_index(SEQ) * TOK).astype(jnp.int32).reshape(1)
 
-    (packed,) = call(pack_kernel, [((TOK, 2 * CG), BF)], (base,), (), (order.reshape(1, TOK), emb, cot), space=pltpu.HBM)
+    (packed,) = call(pack_kernel, [((TOK, 2 * CG), BF)], (base,), (jnp.concatenate([emb, cot], axis=0),), (order.reshape(1, TOK),))
     packed = swap(packed.reshape(32, TOK // 32, 2 * CG), CHIPS).reshape(TOK, 2 * CG)
-    packed, own, core, w1, w2, pw1t, pw2_blocks = lax.optimization_barrier(
-        (packed, own, core, cw1.reshape(3, CG, CG), cw2.reshape(3, CG, CG), pw1.T, pw2.reshape(CG, 8, CG).transpose(1, 0, 2))
+    (halves,) = call(halves_kernel, [((8, CG, 128), BF)], (core,), (), (pw2,))
+    packed, own, core, w1, w2, pw1t, halves = lax.optimization_barrier(
+        (packed, own, core, cw1.reshape(3, CG, CG), cw2.reshape(3, CG, CG), pw1.T, halves)
     )
     sent, near_hidden, start = call(
         near_kernel,
-        [((8, CG, 2 * TOK + CG), BF), ((CG, TOK), F32), ((CG, TOK), BF)],
+        [((8, CG, 2 * TOK + 128), BF), ((CG, TOK), F32), ((CG, TOK), BF)],
         (),
-        (packed, w1, pw2_blocks),
+        (packed, w1, halves),
     )
     sent = swap(sent, GRP)
-    middle, far_dh, grad_middle, parts = call(
+    halves = other_core(sent[:, :, 2 * TOK :])
+    middle, far_hidden, pg2_rows = call(
         mid_kernel,
-        [((CG, TOK), BF), ((CG, TOK), BF), ((CG, TOK), BF), ((8, CG, TOK + CG), BF)],
-        (own,),
+        [((CG, TOK), BF), ((CG, TOK), F32), ((8, CG + 96, 128), BF)],
+        (),
         (sent,),
         (start, pw1t, w2),
+    )
+    far_dh, grad_middle, parts = call(
+        far_kernel,
+        [((CG, TOK), BF), ((CG, TOK), BF), ((8, CG + 72, TOK), BF)],
+        (own, core),
+        (sent, halves),
+        (far_hidden, pw1t, w2, pg2_rows),
+        scratch=[((8, CG, CG), BF)],
     )
     got = swap(parts, GRP)
 
@@ -289,7 +346,7 @@
         (core,),
         (got, sent),
         (near_hidden, start, grad_middle, middle, far_dh),
-        scratch=[((864, 128), F32), ((864, 128), F32)],
+        scratch=[((864, 128), F32), ((864, 128), F32), ((8, 288, 128), F32)],
     )
     other = other_core(other)
     (tokens,) = call(tokens_kernel, [((32, 24, 128), BF)], (), (near_dh,), (w1, grad_middle))
@@ -327,7 +384,7 @@
     fine = Mesh(mesh.devices.reshape(4, 4, 2, 2, 4, 2), SEQ + GRP)
     placed = (P(GRP, SEQ), P(SEQ), P(GRP, SEQ), P(GRP, None), P(GRP, None), P(GRP, None), P(GRP, None))
     return jax.shard_map(
-        local,
+        step,
         mesh=fine,
         in_specs=placed,
         out_specs=(P(GRP, SEQ), P(GRP, None), P(GRP, None), P(GRP, None), P(GRP, None)),

time: 210 us -> 208 us (level)
  blocking collectives: 144 us -> 140 us
  local copies, waits for them, and re-layouts: 7.46 us -> 3.75 us
  starting transfers between devices: 29.1 us -> 31.9 us
  waiting for transfers between devices: 10.2 us -> 12.7 us
    all_to_all x4, blocking collectives: 144 us -> 140 us  [swap(): return lax.all_to_all(blocks, axes, 0, 0, tiled=True)]
    ppermute x2 -> x3, starting transfers between devices: 12.6 us -> 15.2 us  [other_core(): return lax.ppermute(values, 'core', [(0, 1), (1, 0)])]
    all_to_all x1, waiting for transfers between devices: 8.36 us -> 10.9 us  [swap(): return lax.all_to_all(blocks, axes, 0, 0, tiled=True)]
    pallas_call x8 -> x10, Pallas kernels: 11.9 us -> 13.3 us  [call(): pl.pallas_call(body, out_shape=[jax.ShapeDtypeStruct(shape, dtype) for sh...]
  transfers between devices with their start and end apart: 3 -> 4, of which waited for: 3 -> 3; matrix products, arithmetic and copies ran while one was open for 4% -> 2% of each run, Pallas kernels for 0% -> 2%
where the time goes in v6:
time: 208 us; the launch traced here: 207 us
  blocking collectives  140 us (67%)
  starting transfers between devices  31.9 us (15%)
  Pallas kernels  13.3 us (6%)
  waiting for transfers between devices  12.7 us (6%)
  other arithmetic  3.79 us (2%)
  local copies, waits for them, and re-layouts  3.75 us (2%)
    all_to_all x4, blocking collectives, swap(): return lax.all_to_all(blocks, axes, 0, 0, tiled=True)  140 us
    all_to_all x1, starting transfers between devices, swap(): return lax.all_to_all(blocks, axes, 0, 0, tiled=True)  16.6 us
    ppermute x3, starting transfers between devices, other_core(): return lax.ppermute(values, 'core', [(0, 1), (1, 0)])  15.2 us
    pallas_call x10, Pallas kernels, call(): pl.pallas_call(body, out_shape=[jax.ShapeDtypeStruct(shape, dtype) for sh...  13.3 us
    all_to_all x1, waiting for transfers between devices, swap(): return lax.all_to_all(blocks, axes, 0, 0, tiled=True)  10.9 us
  transfers between devices with their start and end apart: 4, of which 3 were waited for; matrix products, arithmetic and copies ran while one was open for 2% of the time, Pallas kernels for 2%

profile of v6, /device:TPU:1, one launch (start us, length us, event | category | flops | bytes accessed | tf_op | source)
XLA Modules:
  0.0 207.0 jit_solution(12129043104416765079)
XLA Ops:
  0.7 1.1 pad_maximum_fusion.refs_1_
  2.5 1.2 shard_map.110
  3.6 16.6 %all-to-all-start = ((bf16[32,16,384]{2,1,0:T(8,128)(2,1)}), bf16[32,16,384]{2,1,0:T(8,128)(2,1)S(1)}, u32[]{:S(2)}, u32[]{:S(2)}) async-start(bf16[32,16,384]{2,1,0:T(8,128)(2,1)} %bitcast.2), calls=%async_computation | async-start | bytes 786432 | tf_op jit(solution)/shard_map/all_to_all | solution.py:26
  20.6 1.3 reduce
  22.1 1.3 reduce.1
  23.9 10.9 %all-to-all-done = bf16[32,16,384]{2,1,0:T(8,128)(2,1)S(1)} async-done(((bf16[32,16,384]{2,1,0:T(8,128)(2,1)}), bf16[32,16,384]{2,1,0:T(8,128)(2,1)S(1)}, u32[]{:S(2)}, u32[]{:S(2)}) %all-to-all-start) | async-done | bytes 393248 | tf_op jit(solution)/shard_map/all_to_all | solution.py:26
  35.6 43.8 %all_to_all.25.refs_0_.refs_2_ = bf16[8,192,1152]{2,1,0:T(8,128)(2,1)S(1)} all-to-all(bf16[8,192,1152]{2,1,0:T(8,128)(2,1)S(1)} %get-tuple-element.33), channel_id=1, replica_groups=mesh['zh'=4,'yh'=4,'yl'=2,'core'=2,'x'=4,'zl'=2] {'x','zl'}, dimensions={0} | all-to-all | bytes 7077888 | tf_op jit(solution)/shard_map/all_to_all | solution.py:26
  79.5 6.6 %collective-permute-start = (bf16[8,192,128]{2,1,0:T(8,128)(2,1)S(1)}, bf16[8,192,128]{2,1,0:T(8,128)(2,1)S(1)}, u32[]{:S(2)}, u32[]{:S(2)}) collective-permute-start(bf16[8,192,128]{2,1,0:T(8,128)(2,1)S(1)} %slice.19), channel_id=1, source_target_pairs={{0,8},{8,0},{1,9},{9,1},{2,10},{10,2},{3,11},{11,3},{4,12},{12,4},... | collective-permute-start | bytes 1179656 | tf_op jit(solution)/shard_map/ppermute | solution.py:30
  86.0 2.5 %shard_map.113 = (bf16[192,512]{1,0:T(8,128)(2,1)S(1)}, f32[192,512]{1,0:T(8,128)S(1)}, bf16[8,288,128]{2,1,0:T(8,128)(2,1)S(1)}) custom-call(bf16[8,192,1152]{2,1,0:T(8,128)(2,1)S(1)} %all_to_all.25.refs_0_.refs_2_, bf16[192,512]{1,0:T(8,128)(2,1)S(1)} %get-tuple-element.34.refs_1_.refs_4_, bf16[1536,192]{1,0:T(8,128)(2,1)S(1)} %bitcast.15, ...), custom_call_target="tpu_custom_call" | custom-call | tf_op jit(solution)/shard_map/pallas_call | solution.py:56
  88.5 2.2 %shard_map.114 = (bf16[192,512]{1,0:T(8,128)(2,1)S(1)}, bf16[192,512]{1,0:T(8,128)(2,1)S(1)}, bf16[8,264,512]{2,1,0:T(8,128)(2,1)S(1)}) custom-call(s32[1]{0:T(128)} %bitcast.4.refs_0_, s32[1]{0:T(128)} %bitcast.5.refs_0_.refs_1_, bf16[8,192,1152]{2,1,0:T(8,128)(2,1)S(1)} %all_to_all.25.refs_0_.refs_2_, ...), custom_call_target="tpu_custom_call" | custom-call | tf_op jit(solution)/shard_map/pallas_call | solution.py:56
  90.7 30.1 %all_to_all.26.refs_1_ = bf16[8,264,512]{2,1,0:T(8,128)(2,1)S(1)} all-to-all(bf16[8,264,512]{2,1,0:T(8,128)(2,1)S(1)} %get-tuple-element.39), channel_id=1, replica_groups=mesh['zh'=4,'yh'=4,'yl'=2,'core'=2,'x'=4,'zl'=2] {'x','zl'}, dimensions={0} | all-to-all | bytes 4325376 | tf_op jit(solution)/shard_map/all_to_all | solution.py:26
  120.9 3.1 %shard_map.115 = (bf16[192,512]{1,0:T(8,128)(2,1)S(1)}, f32[3296,128]{1,0:T(8,128)S(1)}, bf16[3296,128]{1,0:T(8,128)(2,1)S(1)}) custom-call(s32[1]{0:T(128)} %bitcast.5.refs_0_.refs_1_, bf16[8,264,512]{2,1,0:T(8,128)(2,1)S(1)} %all_to_all.26.refs_1_, bf16[8,192,1152]{2,1,0:T(8,128)(2,1)S(1)} %all_to_all.25.refs_0_.refs_2_, ...), custom_call_target="tpu_custom_call" | custom-call | tf_op jit(solution)/shard_map/pallas_call | solution.py:56
  124.0 2.9 %collective-permute-start.1 = (bf16[3296,128]{1,0:T(8,128)(2,1)S(1)}, bf16[3296,128]{1,0:T(8,128)(2,1)S(1)}, u32[]{:S(2)}, u32[]{:S(2)}) collective-permute-start(bf16[3296,128]{1,0:T(8,128)(2,1)S(1)} %get-tuple-element.45), channel_id=1, source_target_pairs={{0,8},{8,0},{1,9},{9,1},{2,10},{10,2},{3,11},{11,3},{4,12},{12,4},... | collective-permute-start | bytes 2531336 | tf_op jit(solution)/shard_map/ppermute | solution.py:30
  126.9 0.9 shard_map.116.refs_2_
  127.8 1.1 collective-permute-done.1.refs_1_
  128.9 0.8 shard_map.117
  129.7 33.1 %all_to_all.27.refs_0_ = bf16[32,128,128]{2,1,0:T(8,128)(2,1)S(1)} all-to-all(bf16[32,128,128]{2,1,0:T(8,128)(2,1)S(1)} %shard_map.117), channel_id=1, replica_groups=mesh['zh'=4,'yh'=4,'yl'=2,'core'=2,'x'=4,'zl'=2] {'zh','yh','yl'}, dimensions={0} | all-to-all | bytes 2097152 | tf_op jit(solution)/shard_map/all_to_all | solution.py:26
  162.9 32.6 %all_to_all.28.refs_1_ = bf16[32,104,128]{2,1,0:T(8,128)(2,1)S(1)} all-to-all(bf16[32,104,128]{2,1,0:T(8,128)(2,1)S(1)} %shard_map.118), channel_id=1, replica_groups=mesh['zh'=4,'yh'=4,'yl'=2,'core'=2,'x'=4,'zl'=2] {'zh','yh','yl'}, dimensions={0} | all-to-all | bytes 1703936 | tf_op jit(solution)/shard_map/all_to_all | solution.py:26
  195.5 5.8 %collective-permute-start.2 = (bf16[32,104,128]{2,1,0:T(8,128)(2,1)S(1)}, bf16[32,104,128]{2,1,0:T(8,128)(2,1)S(1)}, u32[]{:S(2)}, u32[]{:S(2)}) collective-permute-start(bf16[32,104,128]{2,1,0:T(8,128)(2,1)S(1)} %all_to_all.28.refs_1_), channel_id=1, source_target_pairs={{0,8},{8,0},{1,9},{9,1},{2,10},{10,2},{3,11},{11,3},{4,12},{12,4},... | collective-permute-start | bytes 2555912 | tf_op jit(solution)/shard_map/ppermute | solution.py:30
  201.5 1.1 convolution_convert_fusion
  202.5 0.7 collective-permute-done.2.refs_2_
  203.3 1.6 shard_map.119
  204.8 1.1 copy.13
  205.9 1.1 copy.14
  (24 shorter events, 2.7 us)
Async XLA Ops:
  0.6 19.7 %copy-start.3 = (bf16[192,1536]{1,0:T(8,128)(2,1)S(1)}, bf16[192,1536]{1,0:T(8,128)(2,1)}, u32[]{:S(2)}) copy-start(bf16[192,1536]{1,0:T(8,128)(2,1)} %param.11) | copy-start | bytes 1769476
  1.8 0.7 copy-start.1
  2.5 18.1 %copy-start.4 = (bf16[1,110592]{1,0:T(2,128)(2,1)S(1)}, bf16[1,110592]{1,0:T(2,128)(2,1)}, u32[]{:S(2)}) copy-start(bf16[1,110592]{1,0:T(2,128)(2,1)} %param.10) | copy-start | bytes 663556
  2.5 19.7 %copy-start.5 = (bf16[1,110592]{1,0:T(2,128)(2,1)S(1)}, bf16[1,110592]{1,0:T(2,128)(2,1)}, u32[]{:S(2)}) copy-start(bf16[1,110592]{1,0:T(2,128)(2,1)} %param.12) | copy-start | bytes 663556
  3.6 20.0 %copy-start = (bf16[192,1536]{1,0:T(8,128)(2,1)S(1)}, bf16[192,1536]{1,0:T(8,128)(2,1)}, u32[]{:S(2)}) copy-start(bf16[192,1536]{1,0:T(8,128)(2,1)} %refs_1_.1) | copy-start | bytes 1769476
  3.6 31.3 %all-to-all-start = ((bf16[32,16,384]{2,1,0:T(8,128)(2,1)}), bf16[32,16,384]{2,1,0:T(8,128)(2,1)S(1)}, u32[]{:S(2)}, u32[]{:S(2)}) async-start(bf16[32,16,384]{2,1,0:T(8,128)(2,1)} %bitcast.2), calls=%async_computation | async-start | bytes 786432 | tf_op jit(solution)/shard_map/all_to_all | solution.py:26
  79.5 9.0 %collective-permute-start = (bf16[8,192,128]{2,1,0:T(8,128)(2,1)S(1)}, bf16[8,192,128]{2,1,0:T(8,128)(2,1)S(1)}, u32[]{:S(2)}, u32[]{:S(2)}) collective-permute-start(bf16[8,192,128]{2,1,0:T(8,128)(2,1)S(1)} %slice.19), channel_id=1, source_target_pairs={{0,8},{8,0},{1,9},{9,1},{2,10},{10,2},{3,11},{11,3},{4,12},{12,4},... | collective-permute-start | bytes 1179656 | tf_op jit(solution)/shard_map/ppermute | solution.py:30
  124.0 4.9 %collective-permute-start.1 = (bf16[3296,128]{1,0:T(8,128)(2,1)S(1)}, bf16[3296,128]{1,0:T(8,128)(2,1)S(1)}, u32[]{:S(2)}, u32[]{:S(2)}) collective-permute-start(bf16[3296,128]{1,0:T(8,128)(2,1)S(1)} %get-tuple-element.45), channel_id=1, source_target_pairs={{0,8},{8,0},{1,9},{9,1},{2,10},{10,2},{3,11},{11,3},{4,12},{12,4},... | collective-permute-start | bytes 2531336 | tf_op jit(solution)/shard_map/ppermute | solution.py:30
  162.8 38.5 %copy-start.2 = (s32[512]{0:T(512)S(1)}, s32[512]{0:T(512)}, u32[]{:S(2)}) copy-start(s32[512]{0:T(512)} %param.8) | copy-start | bytes 6148
  195.5 7.8 %collective-permute-start.2 = (bf16[32,104,128]{2,1,0:T(8,128)(2,1)S(1)}, bf16[32,104,128]{2,1,0:T(8,128)(2,1)S(1)}, u32[]{:S(2)}, u32[]{:S(2)}) collective-permute-start(bf16[32,104,128]{2,1,0:T(8,128)(2,1)S(1)} %all_to_all.28.refs_1_), channel_id=1, source_target_pairs={{0,8},{8,0},{1,9},{9,1},{2,10},{10,2},{3,11},{11,3},{4,12},{12,4},... | collective-permute-start | bytes 2555912 | tf_op jit(solution)/shard_map/ppermute | solution.py:30

commit v7 on v6

--- a/solution.py
+++ b/solution.py
@@ -138,7 +138,9 @@
         out_ref[j, :, 2 * TOK :] = blocks_ref[j]
 
 
-def mid_kernel(sent_ref, start_ref, pointwise_ref, weight_ref, middle_ref, hidden_ref, rows_ref):
+def mid_kernel(
+    core_ref, sent_ref, start_ref, pointwise_ref, weight_ref, middle_ref, hidden_ref, mine_ref, other_ref
+):
     middle = start_ref[...].astype(F32) + sum(
         mm(pointwise_ref[j * CG : (j + 1) * CG], sent_ref[j, :, :TOK], 0, 0) for j in range(8)
     )
@@ -156,9 +158,16 @@
     lower = jnp.concatenate([act[128:], blank], axis=0)
     upper = jnp.concatenate([blank, act[128:]], axis=0)
     for j in range(8):
-        cot = sent_ref[j, :, TOK : 2 * TOK]
-        rows_ref[j, :CG] = mm(cot, act[:128], 1, 1).astype(BF)
-        rows_ref[j, CG:] = (mm(cot[:96], lower, 1, 1) + mm(cot[96:], upper, 1, 1)).astype(BF)
+        other_ref[j, :CG] = sent_ref[j, :, 2 * TOK :]
+        for out_ref, at, core in ((mine_ref, 0, core_ref[0]), (other_ref, CG, 1 - core_ref[0])):
+            cot = sent_ref[j, pl.ds(pl.multiple_of(96 * core, 16), 96), TOK : 2 * TOK]
+            wide = mm(cot, act[:128], 1, 1)
+            thin = mm(cot[:48], lower, 1, 1) + mm(cot[48:], upper, 1, 1)
+            for part in range(4):
+                row = at + 40 * part
+                rest = thin[16 * part : 16 * (part + 1)] if part < 3 else jnp.zeros((16, 128), F32)
+                piece = jnp.concatenate([wide[24 * part : 24 * (part + 1)], rest], axis=0)
+                out_ref[j, row : row + 40] = piece.astype(out_ref.dtype)
 
 
 def far_kernel(
@@ -182,7 +191,7 @@
         columns_ref[j, mine, :128] = sent_ref[j, :96, 2 * TOK :]
         columns_ref[j, mine, 128:] = sent_ref[j, 96:, 2 * TOK : 2 * TOK + 64]
         columns_ref[j, other, :128] = other_ref[j, :96]
-        columns_ref[j, other, 128:] = other_ref[j, 96:, :64]
+        columns_ref[j, other, 128:] = other_ref[j, 96:CG, :64]
     hidden = hidden_ref[...]
     s = jax.nn.sigmoid(hidden)
     da = sum(mm(columns_ref[j], sent_ref[j, :, TOK : 2 * TOK], 0, 0) for j in range(8))
@@ -194,7 +203,15 @@
     for j in range(8):
         out_ref[j, :CG] = mm(pointwise_ref[j * CG : (j + 1) * CG], grad, 1, 0).astype(BF)
         for part in range(4):
-            out_ref[j, CG:, 128 * part : 128 * (part + 1)] = rows_ref[j, 72 * part : 72 * (part + 1)]
+            rows = slice(40 * part, 40 * (part + 1))
+            theirs = other_ref[j, CG + 40 * part : CG + 40 * (part + 1)].astype(F32)
+            out_ref[j, CG:, 128 * part : 128 * (part + 1)] = (rows_ref[j, rows] + theirs).astype(BF)
+
+
+def columns_of(grad, sent_ref, core, out_ref):
+    half = jnp.concatenate([mm(grad, sent_ref[4 * core + j, :, :TOK], 1, 1) for j in range(4)], axis=1)
+    for j in range(6):
+        out_ref[CG * j : CG * (j + 1)] = half[:, 128 * j : 128 * (j + 1)].astype(out_ref.dtype)
 
 
 def back_kernel(
@@ -211,11 +228,8 @@
     other_ref,
     far_rows_ref,
     near_rows_ref,
-    seq_ref,
 ):
-    for j in range(8):
-        for part in range(4):
-            seq_ref[j, 72 * part : 72 * (part + 1)] = got_ref[j, CG:, 128 * part : 128 * (part + 1)].astype(F32)
+    core = core_ref[0]
     da = sum(got_ref[j, :CG].astype(F32) for j in range(8))
     hidden = hidden_ref[...]
     s = jax.nn.sigmoid(hidden)
@@ -223,26 +237,17 @@
     dh_ref[...] = dh
     conv_rows(start_ref[...].astype(F32), dh, NEAR, near_rows_ref)
     conv_rows(middle_ref[...].astype(F32), far_dh_ref[...], FAR, far_rows_ref)
-    blank = jnp.zeros((8, 64), F32)
-    for out_ref, core in ((mine_ref, core_ref[0]), (other_ref, 1 - core_ref[0])):
-        grad = jnp.concatenate([mm(grad_ref[...], sent_ref[4 * core + j, :, :TOK], 1, 1) for j in range(4)], axis=1)
-        for j in range(6):
-            out_ref[CG * j : CG * (j + 1)] = grad[:, 128 * j : 128 * (j + 1)].astype(out_ref.dtype)
-        rows = pl.ds(pl.multiple_of(432 * core, 8), 432)
-        out_ref[1152:1584] = far_rows_ref[rows].astype(out_ref.dtype)
-        out_ref[1584:2016] = near_rows_ref[rows].astype(out_ref.dtype)
-        for j in range(8):
-            wide = seq_ref[j, pl.ds(pl.multiple_of(96 * core, 8), 96)]
-            thin = jnp.where(core == 0, seq_ref[j, CG:, :64], seq_ref[j, CG:, 64:])
-            for part in range(4):
-                piece = wide[24 * part : 24 * (part + 1)]
-                rest = thin[24 * part : 24 * (part + 1)]
-                packed = jnp.concatenate([rest[:8], rest[8:16]], axis=1), jnp.concatenate([rest[16:], blank], axis=1)
-                at = 2016 + 160 * j + 40 * part
-                out_ref[at : at + 40] = jnp.concatenate([piece, *packed], axis=0).astype(out_ref.dtype)
-
-
-def tokens_kernel(dh_ref, weight_ref, grad_ref, out_ref):
+    mine = pl.ds(pl.multiple_of(432 * core, 8), 432)
+    mine_ref[:432] = far_rows_ref[mine]
+    mine_ref[432:] = near_rows_ref[mine]
+    other = pl.ds(pl.multiple_of(432 - 432 * core, 8), 432)
+    other_ref[1152:1584] = far_rows_ref[other].astype(BF)
+    other_ref[1584:] = near_rows_ref[other].astype(BF)
+    columns_of(grad_ref[...], sent_ref, 1 - core, other_ref)
+
+
+def keep_kernel(core_ref, sent_ref, dh_ref, weight_ref, grad_ref, mine_ref, out_ref):
+    columns_of(grad_ref[...], sent_ref, core_ref[0], mine_ref)
     back = grad_ref[...].astype(F32) + conv_back(dh_ref[...].astype(F32), weight_ref, NEAR)
     rows = back.T
     out_ref[:, :16] = rows[:, :128].reshape(32, 16, 128).astype(BF)
@@ -250,12 +255,14 @@
     out_ref[:, 16:] = jnp.concatenate([rest[:, :8], rest[:, 8:]], axis=2).astype(BF)
 
 
-def gather_kernel(mine_ref, other_ref, tokens_ref, out_ref, rows_ref):
-    rows_ref[:2016] = mine_ref[:2016] + other_ref[:2016].astype(F32)
+def gather_kernel(got_ref, columns_ref, conv_ref, other_ref, tokens_ref, out_ref, rows_ref):
+    rows_ref[:1152] = columns_ref[...] + other_ref[:1152].astype(F32)
+    rows_ref[1152:2016] = conv_ref[...] + other_ref[1152:].astype(F32)
     rows_ref[2016:] = jnp.zeros((32, 128), F32)
     out_ref[:, :64] = rows_ref[...].reshape(32, 64, 128).astype(BF)
-    rest = mine_ref[2016:] + other_ref[2016:].astype(F32)
-    out_ref[:, 64:ROWS] = rest.reshape(32, 40, 128).astype(BF)
+    for j in range(8):
+        for part in range(4):
+            out_ref[4 * j + part, 64:ROWS] = got_ref[j, CG:, 128 * part : 128 * (part + 1)]
     out_ref[:, ROWS:] = tokens_ref[...]
 
 
@@ -288,19 +295,19 @@
                 out_ref[96 * tap + 48 * half : 96 * tap + 48 * (half + 1), 128 * column : 128 * (column + 1)] = rows[
                     at + 48 * block : at + 48 * (block + 1)
                 ].astype(BF)
-        for part in range(4):
-            at = 96 * core + 24 * part
-            for pair in range(4):
-                blocks = []
-                for j in (2 * pair, 2 * pair + 1):
-                    piece = all_ref[core, 4 * j + part, 64:ROWS]
-                    rest = jnp.concatenate([piece[24:32, :64], piece[24:32, 64:], piece[32:, :64]], axis=0)
-                    blocks.append((piece[:24], rest))
-                (even, even_rest), (odd, odd_rest) = blocks
-                col = 2 * CG * pair
-                far_ref[at : at + 24, col : col + 128] = even
-                far_ref[at : at + 24, col + 128 : col + 256] = jnp.concatenate([even_rest, odd[:, :64]], axis=1)
-                far_ref[at : at + 24, col + 256 : col + 384] = jnp.concatenate([odd[:, 64:], odd_rest], axis=1)
+        at = 96 * core
+        for pair in range(4):
+            blocks = []
+            for j in (2 * pair, 2 * pair + 1):
+                pieces = [all_ref[core, 4 * j + part, 64:ROWS] for part in range(4)]
+                rest = jnp.concatenate([piece[24:] for piece in pieces[:3]], axis=0)
+                wide = jnp.concatenate([piece[:24] for piece in pieces], axis=0)
+                blocks.append((wide, jnp.concatenate([rest[:, :64], rest[:, 64:]], axis=0)))
+            (even, even_rest), (odd, odd_rest) = blocks
+            col = 2 * CG * pair
+            far_ref[at : at + 96, col : col + 128] = even
+            far_ref[at : at + 96, col + 128 : col + 256] = jnp.concatenate([even_rest, odd[:, :64]], axis=1)
+            far_ref[at : at + 96, col + 256 : col + 384] = jnp.concatenate([odd[:, 64:], odd_rest], axis=1)
     far_pw_ref[...] = far_ref[...].astype(BF)
 
 
@@ -309,7 +316,8 @@
     own = lax.axis_index(GRP).astype(jnp.int32).reshape(1)
     base = (lax.axis_index(SEQ) * TOK).astype(jnp.int32).reshape(1)
 
-    (packed,) = call(pack_kernel, [((TOK, 2 * CG), BF)], (base,), (jnp.concatenate([emb, cot], axis=0),), (order.reshape(1, TOK),))
+    both = jnp.concatenate([emb, cot], axis=0)
+    (packed,) = call(pack_kernel, [((TOK, 2 * CG), BF)], (base,), (both,), (order.reshape(1, TOK),))
     packed = swap(packed.reshape(32, TOK // 32, 2 * CG), CHIPS).reshape(TOK, 2 * CG)
     (halves,) = call(halves_kernel, [((8, CG, 128), BF)], (core,), (), (pw2,))
     packed, own, core, w1, w2, pw1t, halves = lax.optimization_barrier(
@@ -322,40 +330,46 @@
         (packed, w1, halves),
     )
     sent = swap(sent, GRP)
-    halves = other_core(sent[:, :, 2 * TOK :])
-    middle, far_hidden, pg2_rows = call(
+    middle, far_hidden, pg2_mine, halves = call(
         mid_kernel,
-        [((CG, TOK), BF), ((CG, TOK), F32), ((8, CG + 96, 128), BF)],
-        (),
+        [((CG, TOK), BF), ((CG, TOK), F32), ((8, 160, 128), F32), ((8, CG + 160, 128), BF)],
+        (core,),
         (sent,),
         (start, pw1t, w2),
     )
+    halves = other_core(halves)
     far_dh, grad_middle, parts = call(
         far_kernel,
-        [((CG, TOK), BF), ((CG, TOK), BF), ((8, CG + 72, TOK), BF)],
+        [((CG, TOK), BF), ((CG, TOK), BF), ((8, CG + 40, TOK), BF)],
         (own, core),
         (sent, halves),
-        (far_hidden, pw1t, w2, pg2_rows),
+        (far_hidden, pw1t, w2, pg2_mine),
         scratch=[((8, CG, CG), BF)],
     )
     got = swap(parts, GRP)
 
-    near_dh, mine, other = call(
+    near_dh, conv_mine, other = call(
         back_kernel,
-        [((CG, TOK), BF), ((3296, 128), F32), ((3296, 128), BF)],
+        [((CG, TOK), BF), ((864, 128), F32), ((2016, 128), BF)],
         (core,),
         (got, sent),
         (near_hidden, start, grad_middle, middle, far_dh),
-        scratch=[((864, 128), F32), ((864, 128), F32), ((8, 288, 128), F32)],
+        scratch=[((864, 128), F32), ((864, 128), F32)],
     )
     other = other_core(other)
-    (tokens,) = call(tokens_kernel, [((32, 24, 128), BF)], (), (near_dh,), (w1, grad_middle))
+    pg1_mine, tokens = call(
+        keep_kernel,
+        [((1152, 128), F32), ((32, 24, 128), BF)],
+        (core,),
+        (sent, near_dh),
+        (w1, grad_middle),
+    )
     (bundle,) = call(
         gather_kernel,
         [((32, ROWS + 24, 128), BF)],
         (),
-        (),
-        (mine, other, tokens),
+        (got,),
+        (pg1_mine, conv_mine, other, tokens),
         scratch=[((2048, 128), F32)],
     )
     bundle = swap(bundle, CHIPS)

time: 208 us -> 207 us (level)
  blocking collectives: 140 us -> 136 us
    all_to_all x4, blocking collectives: 140 us -> 136 us  [swap(): return lax.all_to_all(blocks, axes, 0, 0, tiled=True)]
    unnamed x15 -> x11, local copies, waits for them, and re-layouts: 3.18 us -> 4.23 us
  transfers between devices with their start and end apart: 4 -> 4, of which waited for: 3 -> 4; matrix products, arithmetic and copies ran while one was open for 2% -> 3% of each run, Pallas kernels for 2% -> 1%
where the time goes in v7:
time: 207 us; the launch traced here: 205 us
  blocking collectives  136 us (66%)
  starting transfers between devices  32.2 us (16%)
  Pallas kernels  13.8 us (7%)
  waiting for transfers between devices  11.9 us (6%)
  local copies, waits for them, and re-layouts  4.73 us (2%)
  other arithmetic  4.72 us (2%)
    all_to_all x4, blocking collectives, swap(): return lax.all_to_all(blocks, axes, 0, 0, tiled=True)  136 us
    all_to_all x1, starting transfers between devices, swap(): return lax.all_to_all(blocks, axes, 0, 0, tiled=True)  16.5 us
    ppermute x3, starting transfers between devices, other_core(): return lax.ppermute(values, 'core', [(0, 1), (1, 0)])  15.7 us
    pallas_call x10, Pallas kernels, call(): pl.pallas_call(body, out_shape=[jax.ShapeDtypeStruct(shape, dtype) for sh...  13.8 us
    all_to_all x1, waiting for transfers between devices, swap(): return lax.all_to_all(blocks, axes, 0, 0, tiled=True)  8.97 us
    unnamed x11, local copies, waits for them, and re-layouts  4.23 us
  transfers between devices with their start and end apart: 4, of which 4 were waited for; matrix products, arithmetic and copies ran while one was open for 3% of the time, Pallas kernels for 1%

profile of v7, /device:TPU:1, one launch (start us, length us, event | category | flops | bytes accessed | tf_op | source)
XLA Modules:
  0.0 205.4 jit_solution(4765102169277132330)
XLA Ops:
  0.7 1.1 pad_maximum_fusion.refs_1_
  2.5 1.2 shard_map.110
  3.6 16.5 %all-to-all-start = ((bf16[32,16,384]{2,1,0:T(8,128)(2,1)}), bf16[32,16,384]{2,1,0:T(8,128)(2,1)S(1)}, u32[]{:S(2)}, u32[]{:S(2)}) async-start(bf16[32,16,384]{2,1,0:T(8,128)(2,1)} %bitcast.2), calls=%async_computation | async-start | bytes 786432 | tf_op jit(solution)/shard_map/all_to_all | solution.py:26
  20.1 1.3 copy.12
  21.5 2.2 %reduce = bf16[110592]{0:T(1024)(128)(2,1)S(1)} reduce(bf16[1,110592]{1,0:T(2,128)(2,1)} %param.10, bf16[]{:T(256)} %constant.33), dimensions={0}, to_apply=%param.10.reduce_sub_computation | reduce | bytes 442370 | tf_op args[3]
  23.9 1.3 reduce.1
  25.8 9.0 %all-to-all-done = bf16[32,16,384]{2,1,0:T(8,128)(2,1)S(1)} async-done(((bf16[32,16,384]{2,1,0:T(8,128)(2,1)}), bf16[32,16,384]{2,1,0:T(8,128)(2,1)S(1)}, u32[]{:S(2)}, u32[]{:S(2)}) %all-to-all-start) | async-done | bytes 393248 | tf_op jit(solution)/shard_map/all_to_all | solution.py:26
  35.4 43.8 %all_to_all.25.refs_1_.refs_2_ = bf16[8,192,1152]{2,1,0:T(8,128)(2,1)S(1)} all-to-all(bf16[8,192,1152]{2,1,0:T(8,128)(2,1)S(1)} %get-tuple-element.36), channel_id=1, replica_groups=mesh['zh'=4,'yh'=4,'yl'=2,'core'=2,'x'=4,'zl'=2] {'x','zl'}, dimensions={0} | all-to-all | bytes 7077888 | tf_op jit(solution)/shard_map/all_to_all | solution.py:26
  79.2 2.9 %shard_map.113 = (bf16[192,512]{1,0:T(8,128)(2,1)S(1)}, f32[192,512]{1,0:T(8,128)S(1)}, f32[8,160,128]{2,1,0:T(8,128)S(1)}, bf16[8,352,128]{2,1,0:T(8,128)(2,1)S(1)}) custom-call(s32[1]{0:T(128)} %bitcast.5.refs_0_.refs_1_, bf16[8,192,1152]{2,1,0:T(8,128)(2,1)S(1)} %all_to_all.25.refs_1_.refs_2_, bf16[192,512]{1,0:T(8,128)(2,1)S(1)} %get-tuple-element.37.refs_2_.refs_4_, ...), custom_call_target="tpu_custom_call" | custom-call | tf_op jit(solution)/shard_map/pallas_call | solution.py:56
  82.1 6.6 %collective-permute-start = (bf16[8,352,128]{2,1,0:T(8,128)(2,1)S(1)}, bf16[8,352,128]{2,1,0:T(8,128)(2,1)S(1)}, u32[]{:S(2)}, u32[]{:S(2)}) collective-permute-start(bf16[8,352,128]{2,1,0:T(8,128)(2,1)S(1)} %get-tuple-element.40), channel_id=1, source_target_pairs={{0,8},{8,0},{1,9},{9,1},{2,10},{10,2},{3,11},{11,3},{4,12},{12,4},... | collective-permute-start | bytes 2162696 | tf_op jit(solution)/shard_map/ppermute | solution.py:30
  88.7 1.8 collective-permute-done.refs_3_
  90.5 2.3 %shard_map.114 = (bf16[192,512]{1,0:T(8,128)(2,1)S(1)}, bf16[192,512]{1,0:T(8,128)(2,1)S(1)}, bf16[8,232,512]{2,1,0:T(8,128)(2,1)S(1)}) custom-call(s32[1]{0:T(128)} %bitcast.4.refs_0_, s32[1]{0:T(128)} %bitcast.5.refs_0_.refs_1_, bf16[8,192,1152]{2,1,0:T(8,128)(2,1)S(1)} %all_to_all.25.refs_1_.refs_2_, ...), custom_call_target="tpu_custom_call" | custom-call | tf_op jit(solution)/shard_map/pallas_call | solution.py:56
  92.8 26.8 %all_to_all.26.refs_1_.refs_0_ = bf16[8,232,512]{2,1,0:T(8,128)(2,1)S(1)} all-to-all(bf16[8,232,512]{2,1,0:T(8,128)(2,1)S(1)} %get-tuple-element.43), channel_id=1, replica_groups=mesh['zh'=4,'yh'=4,'yl'=2,'core'=2,'x'=4,'zl'=2] {'x','zl'}, dimensions={0} | all-to-all | bytes 3801088 | tf_op jit(solution)/shard_map/all_to_all | solution.py:26
  119.6 2.8 %shard_map.115 = (bf16[192,512]{1,0:T(8,128)(2,1)S(1)}, f32[864,128]{1,0:T(8,128)S(1)}, bf16[2016,128]{1,0:T(8,128)(2,1)S(1)}) custom-call(s32[1]{0:T(128)} %bitcast.5.refs_0_.refs_1_, bf16[8,232,512]{2,1,0:T(8,128)(2,1)S(1)} %all_to_all.26.refs_1_.refs_0_, bf16[8,192,1152]{2,1,0:T(8,128)(2,1)S(1)} %all_to_all.25.refs_1_.refs_2_, ...), custom_call_target="tpu_custom_call" | custom-call | tf_op jit(solution)/shard_map/pallas_call | solution.py:56
  122.4 3.4 %collective-permute-start.1 = (bf16[2016,128]{1,0:T(8,128)(2,1)S(1)}, bf16[2016,128]{1,0:T(8,128)(2,1)S(1)}, u32[]{:S(2)}, u32[]{:S(2)}) collective-permute-start(bf16[2016,128]{1,0:T(8,128)(2,1)S(1)} %get-tuple-element.51), channel_id=1, source_target_pairs={{0,8},{8,0},{1,9},{9,1},{2,10},{10,2},{3,11},{11,3},{4,12},{12,4},... | collective-permute-start | bytes 1548296 | tf_op jit(solution)/shard_map/ppermute | solution.py:30
  125.8 1.1 shard_map.116
  127.3 1.2 shard_map.117
  128.4 33.1 %all_to_all.27.refs_0_ = bf16[32,128,128]{2,1,0:T(8,128)(2,1)S(1)} all-to-all(bf16[32,128,128]{2,1,0:T(8,128)(2,1)S(1)} %shard_map.117), channel_id=1, replica_groups=mesh['zh'=4,'yh'=4,'yl'=2,'core'=2,'x'=4,'zl'=2] {'zh','yh','yl'}, dimensions={0} | all-to-all | bytes 2097152 | tf_op jit(solution)/shard_map/all_to_all | solution.py:26
  161.7 32.4 %all_to_all.28.refs_1_ = bf16[32,104,128]{2,1,0:T(8,128)(2,1)S(1)} all-to-all(bf16[32,104,128]{2,1,0:T(8,128)(2,1)S(1)} %shard_map.118), channel_id=1, replica_groups=mesh['zh'=4,'yh'=4,'yl'=2,'core'=2,'x'=4,'zl'=2] {'zh','yh','yl'}, dimensions={0} | all-to-all | bytes 1703936 | tf_op jit(solution)/shard_map/all_to_all | solution.py:26
  194.1 5.7 %collective-permute-start.2 = (bf16[32,104,128]{2,1,0:T(8,128)(2,1)S(1)}, bf16[32,104,128]{2,1,0:T(8,128)(2,1)S(1)}, u32[]{:S(2)}, u32[]{:S(2)}) collective-permute-start(bf16[32,104,128]{2,1,0:T(8,128)(2,1)S(1)} %all_to_all.28.refs_1_), channel_id=1, source_target_pairs={{0,8},{8,0},{1,9},{9,1},{2,10},{10,2},{3,11},{11,3},{4,12},{12,4},... | collective-permute-start | bytes 2555912 | tf_op jit(solution)/shard_map/ppermute | solution.py:30
  200.0 1.1 convolution_convert_fusion
  201.8 1.4 shard_map.119
  203.2 1.1 copy.13
  204.3 1.1 copy.14
  (19 shorter events, 3.5 us)
Async XLA Ops:
  0.6 24.8 %copy-start = (bf16[192,1536]{1,0:T(8,128)(2,1)S(1)}, bf16[192,1536]{1,0:T(8,128)(2,1)}, u32[]{:S(2)}) copy-start(bf16[192,1536]{1,0:T(8,128)(2,1)} %refs_1_.1) | copy-start | bytes 1769476
  1.8 0.7 copy-start.1
  2.5 21.5 %copy-start.3 = (bf16[1,110592]{1,0:T(2,128)(2,1)S(1)}, bf16[1,110592]{1,0:T(2,128)(2,1)}, u32[]{:S(2)}) copy-start(bf16[1,110592]{1,0:T(2,128)(2,1)} %param.12) | copy-start | bytes 663556
  3.6 31.1 %all-to-all-start = ((bf16[32,16,384]{2,1,0:T(8,128)(2,1)}), bf16[32,16,384]{2,1,0:T(8,128)(2,1)S(1)}, u32[]{:S(2)}, u32[]{:S(2)}) async-start(bf16[32,16,384]{2,1,0:T(8,128)(2,1)} %bitcast.2), calls=%async_computation | async-start | bytes 786432 | tf_op jit(solution)/shard_map/all_to_all | solution.py:26
  82.1 8.4 %collective-permute-start = (bf16[8,352,128]{2,1,0:T(8,128)(2,1)S(1)}, bf16[8,352,128]{2,1,0:T(8,128)(2,1)S(1)}, u32[]{:S(2)}, u32[]{:S(2)}) collective-permute-start(bf16[8,352,128]{2,1,0:T(8,128)(2,1)S(1)} %get-tuple-element.40), channel_id=1, source_target_pairs={{0,8},{8,0},{1,9},{9,1},{2,10},{10,2},{3,11},{11,3},{4,12},{12,4},... | collective-permute-start | bytes 2162696 | tf_op jit(solution)/shard_map/ppermute | solution.py:30
  122.4 4.9 %collective-permute-start.1 = (bf16[2016,128]{1,0:T(8,128)(2,1)S(1)}, bf16[2016,128]{1,0:T(8,128)(2,1)S(1)}, u32[]{:S(2)}, u32[]{:S(2)}) collective-permute-start(bf16[2016,128]{1,0:T(8,128)(2,1)S(1)} %get-tuple-element.51), channel_id=1, source_target_pairs={{0,8},{8,0},{1,9},{9,1},{2,10},{10,2},{3,11},{11,3},{4,12},{12,4},... | collective-permute-start | bytes 1548296 | tf_op jit(solution)/shard_map/ppermute | solution.py:30
  128.4 71.4 %copy-start.2 = (s32[512]{0:T(512)S(1)}, s32[512]{0:T(512)}, u32[]{:S(2)}) copy-start(s32[512]{0:T(512)} %param.8) | copy-start | bytes 6148
  194.1 7.7 %collective-permute-start.2 = (bf16[32,104,128]{2,1,0:T(8,128)(2,1)S(1)}, bf16[32,104,128]{2,1,0:T(8,128)(2,1)S(1)}, u32[]{:S(2)}, u32[]{:S(2)}) collective-permute-start(bf16[32,104,128]{2,1,0:T(8,128)(2,1)S(1)} %all_to_all.28.refs_1_), channel_id=1, source_target_pairs={{0,8},{8,0},{1,9},{9,1},{2,10},{10,2},{3,11},{11,3},{4,12},{12,4},... | collective-permute-start | bytes 2555912 | tf_op jit(solution)/shard_map/ppermute | solution.py:30

commit v8 on v7

--- a/solution.py
+++ b/solution.py
@@ -139,7 +139,7 @@
 
 
 def mid_kernel(
-    core_ref, sent_ref, start_ref, pointwise_ref, weight_ref, middle_ref, hidden_ref, mine_ref, other_ref
+    core_ref, sent_ref, start_ref, pointwise_ref, weight_ref, middle_ref, hidden_ref, act_ref, other_ref
 ):
     middle = start_ref[...].astype(F32) + sum(
         mm(pointwise_ref[j * CG : (j + 1) * CG], sent_ref[j, :, :TOK], 0, 0) for j in range(8)
@@ -154,20 +154,29 @@
     )
     hidden_ref[...] = hidden
     act = (hidden * jax.nn.sigmoid(hidden)).astype(BF)
+    act_ref[...] = act
+    for j in range(8):
+        other_ref[j, :CG] = sent_ref[j, :, 2 * TOK :]
+    block_of(act, sent_ref, 1 - core_ref[0], other_ref, CG)
+
+
+def block_of(act, sent_ref, core, out_ref, at):
     blank = jnp.zeros((64, TOK), BF)
     lower = jnp.concatenate([act[128:], blank], axis=0)
     upper = jnp.concatenate([blank, act[128:]], axis=0)
     for j in range(8):
-        other_ref[j, :CG] = sent_ref[j, :, 2 * TOK :]
-        for out_ref, at, core in ((mine_ref, 0, core_ref[0]), (other_ref, CG, 1 - core_ref[0])):
-            cot = sent_ref[j, pl.ds(pl.multiple_of(96 * core, 16), 96), TOK : 2 * TOK]
-            wide = mm(cot, act[:128], 1, 1)
-            thin = mm(cot[:48], lower, 1, 1) + mm(cot[48:], upper, 1, 1)
-            for part in range(4):
-                row = at + 40 * part
-                rest = thin[16 * part : 16 * (part + 1)] if part < 3 else jnp.zeros((16, 128), F32)
-                piece = jnp.concatenate([wide[24 * part : 24 * (part + 1)], rest], axis=0)
-                out_ref[j, row : row + 40] = piece.astype(out_ref.dtype)
+        cot = sent_ref[j, pl.ds(pl.multiple_of(96 * core, 16), 96), TOK : 2 * TOK]
+        wide = mm(cot, act[:128], 1, 1)
+        thin = mm(cot[:48], lower, 1, 1) + mm(cot[48:], upper, 1, 1)
+        for part in range(4):
+            row = at + 40 * part
+            rest = thin[16 * part : 16 * (part + 1)] if part < 3 else jnp.zeros((16, 128), F32)
+            piece = jnp.concatenate([wide[24 * part : 24 * (part + 1)], rest], axis=0)
+            out_ref[j, row : row + 40] = piece.astype(out_ref.dtype)
+
+
+def block_kernel(core_ref, sent_ref, act_ref, mine_ref):
+    block_of(act_ref[...], sent_ref, core_ref[0], mine_ref, 0)
 
 
 def far_kernel(
@@ -330,14 +339,15 @@
         (packed, w1, halves),
     )
     sent = swap(sent, GRP)
-    middle, far_hidden, pg2_mine, halves = call(
+    middle, far_hidden, far_act, halves = call(
         mid_kernel,
-        [((CG, TOK), BF), ((CG, TOK), F32), ((8, 160, 128), F32), ((8, CG + 160, 128), BF)],
+        [((CG, TOK), BF), ((CG, TOK), F32), ((CG, TOK), BF), ((8, CG + 160, 128), BF)],
         (core,),
         (sent,),
         (start, pw1t, w2),
     )
     halves = other_core(halves)
+    (pg2_mine,) = call(block_kernel, [((8, 160, 128), F32)], (core,), (sent, far_act))
     far_dh, grad_middle, parts = call(
         far_kernel,
         [((CG, TOK), BF), ((CG, TOK), BF), ((8, CG + 40, TOK), BF)],

time: 207 us -> 206 us (level)
    pallas_call x10 -> x11, Pallas kernels: 13.8 us -> 14 us  [call(): pl.pallas_call(body, out_shape=[jax.ShapeDtypeStruct(shape, dtype) for sh...]
where the time goes in v8:
time: 206 us; the launch traced here: 205 us
  blocking collectives  136 us (66%)
  starting transfers between devices  32.2 us (16%)
  Pallas kernels  14 us (7%)
  waiting for transfers between devices  11 us (5%)
  local copies, waits for them, and re-layouts  4.73 us (2%)
  other arithmetic  4.72 us (2%)
    all_to_all x4, blocking collectives, swap(): return lax.all_to_all(blocks, axes, 0, 0, tiled=True)  136 us
    all_to_all x1, starting transfers between devices, swap(): return lax.all_to_all(blocks, axes, 0, 0, tiled=True)  16.5 us
    ppermute x3, starting transfers between devices, other_core(): return lax.ppermute(values, 'core', [(0, 1), (1, 0)])  15.7 us
    pallas_call x11, Pallas kernels, call(): pl.pallas_call(body, out_shape=[jax.ShapeDtypeStruct(shape, dtype) for sh...  14 us
    all_to_all x1, waiting for transfers between devices, swap(): return lax.all_to_all(blocks, axes, 0, 0, tiled=True)  8.97 us
    unnamed x11, local copies, waits for them, and re-layouts  4.23 us
  transfers between devices with their start and end apart: 4, of which 4 were waited for; matrix products, arithmetic and copies ran while one was open for 3% of the time, Pallas kernels for 1%

profile of v8, /device:TPU:1, one launch (start us, length us, event | category | flops | bytes accessed | tf_op | source)
XLA Modules:
  0.0 204.8 jit_solution(4363769452635986097)
XLA Ops:
  0.7 1.1 pad_maximum_fusion.refs_1_
  2.5 1.2 shard_map.110
  3.6 16.5 %all-to-all-start = ((bf16[32,16,384]{2,1,0:T(8,128)(2,1)}), bf16[32,16,384]{2,1,0:T(8,128)(2,1)S(1)}, u32[]{:S(2)}, u32[]{:S(2)}) async-start(bf16[32,16,384]{2,1,0:T(8,128)(2,1)} %bitcast.2), calls=%async_computation | async-start | bytes 786432 | tf_op jit(solution)/shard_map/all_to_all | solution.py:26
  20.1 1.3 copy.12
  21.5 2.2 %reduce = bf16[110592]{0:T(1024)(128)(2,1)S(1)} reduce(bf16[1,110592]{1,0:T(2,128)(2,1)} %param.10, bf16[]{:T(256)} %constant.33), dimensions={0}, to_apply=%param.10.reduce_sub_computation | reduce | bytes 442370 | tf_op args[3]
  23.9 1.3 reduce.1
  25.8 9.0 %all-to-all-done = bf16[32,16,384]{2,1,0:T(8,128)(2,1)S(1)} async-done(((bf16[32,16,384]{2,1,0:T(8,128)(2,1)}), bf16[32,16,384]{2,1,0:T(8,128)(2,1)S(1)}, u32[]{:S(2)}, u32[]{:S(2)}) %all-to-all-start) | async-done | bytes 393248 | tf_op jit(solution)/shard_map/all_to_all | solution.py:26
  35.4 43.8 %all_to_all.25.refs_1_.refs_2_ = bf16[8,192,1152]{2,1,0:T(8,128)(2,1)S(1)} all-to-all(bf16[8,192,1152]{2,1,0:T(8,128)(2,1)S(1)} %get-tuple-element.36), channel_id=1, replica_groups=mesh['zh'=4,'yh'=4,'yl'=2,'core'=2,'x'=4,'zl'=2] {'x','zl'}, dimensions={0} | all-to-all | bytes 7077888 | tf_op jit(solution)/shard_map/all_to_all | solution.py:26
  79.2 2.2 %shard_map.113 = (bf16[192,512]{1,0:T(8,128)(2,1)S(1)}, f32[192,512]{1,0:T(8,128)S(1)}, bf16[192,512]{1,0:T(8,128)(2,1)S(1)}, bf16[8,352,128]{2,1,0:T(8,128)(2,1)S(1)}) custom-call(s32[1]{0:T(128)} %bitcast.5.refs_0_.refs_1_, bf16[8,192,1152]{2,1,0:T(8,128)(2,1)S(1)} %all_to_all.25.refs_1_.refs_2_, bf16[192,512]{1,0:T(8,128)(2,1)S(1)} %get-tuple-element.37.refs_2_.refs_4_, ...), custom_call_target="tpu_custom_call" | custom-call | tf_op jit(solution)/shard_map/pallas_call | solution.py:56
  81.5 6.6 %collective-permute-start = (bf16[8,352,128]{2,1,0:T(8,128)(2,1)S(1)}, bf16[8,352,128]{2,1,0:T(8,128)(2,1)S(1)}, u32[]{:S(2)}, u32[]{:S(2)}) collective-permute-start(bf16[8,352,128]{2,1,0:T(8,128)(2,1)S(1)} %get-tuple-element.40), channel_id=1, source_target_pairs={{0,8},{8,0},{1,9},{9,1},{2,10},{10,2},{3,11},{11,3},{4,12},{12,4},... | collective-permute-start | bytes 2162696 | tf_op jit(solution)/shard_map/ppermute | solution.py:30
  88.0 0.9 shard_map.114.refs_7_
  89.8 2.3 %shard_map.115 = (bf16[192,512]{1,0:T(8,128)(2,1)S(1)}, bf16[192,512]{1,0:T(8,128)(2,1)S(1)}, bf16[8,232,512]{2,1,0:T(8,128)(2,1)S(1)}) custom-call(s32[1]{0:T(128)} %bitcast.4.refs_0_, s32[1]{0:T(128)} %bitcast.5.refs_0_.refs_1_, bf16[8,192,1152]{2,1,0:T(8,128)(2,1)S(1)} %all_to_all.25.refs_1_.refs_2_, ...), custom_call_target="tpu_custom_call" | custom-call | tf_op jit(solution)/shard_map/pallas_call | solution.py:56
  92.1 26.8 %all_to_all.26.refs_1_.refs_0_ = bf16[8,232,512]{2,1,0:T(8,128)(2,1)S(1)} all-to-all(bf16[8,232,512]{2,1,0:T(8,128)(2,1)S(1)} %get-tuple-element.43), channel_id=1, replica_groups=mesh['zh'=4,'yh'=4,'yl'=2,'core'=2,'x'=4,'zl'=2] {'x','zl'}, dimensions={0} | all-to-all | bytes 3801088 | tf_op jit(solution)/shard_map/all_to_all | solution.py:26
  118.9 2.8 %shard_map.116 = (bf16[192,512]{1,0:T(8,128)(2,1)S(1)}, f32[864,128]{1,0:T(8,128)S(1)}, bf16[2016,128]{1,0:T(8,128)(2,1)S(1)}) custom-call(s32[1]{0:T(128)} %bitcast.5.refs_0_.refs_1_, bf16[8,232,512]{2,1,0:T(8,128)(2,1)S(1)} %all_to_all.26.refs_1_.refs_0_, bf16[8,192,1152]{2,1,0:T(8,128)(2,1)S(1)} %all_to_all.25.refs_1_.refs_2_, ...), custom_call_target="tpu_custom_call" | custom-call | tf_op jit(solution)/shard_map/pallas_call | solution.py:56
  121.7 3.4 %collective-permute-start.1 = (bf16[2016,128]{1,0:T(8,128)(2,1)S(1)}, bf16[2016,128]{1,0:T(8,128)(2,1)S(1)}, u32[]{:S(2)}, u32[]{:S(2)}) collective-permute-start(bf16[2016,128]{1,0:T(8,128)(2,1)S(1)} %get-tuple-element.51), channel_id=1, source_target_pairs={{0,8},{8,0},{1,9},{9,1},{2,10},{10,2},{3,11},{11,3},{4,12},{12,4},... | collective-permute-start | bytes 1548296 | tf_op jit(solution)/shard_map/ppermute | solution.py:30
  125.1 1.1 shard_map.117
  126.6 1.2 shard_map.118
  127.8 33.1 %all_to_all.27.refs_0_ = bf16[32,128,128]{2,1,0:T(8,128)(2,1)S(1)} all-to-all(bf16[32,128,128]{2,1,0:T(8,128)(2,1)S(1)} %shard_map.118), channel_id=1, replica_groups=mesh['zh'=4,'yh'=4,'yl'=2,'core'=2,'x'=4,'zl'=2] {'zh','yh','yl'}, dimensions={0} | all-to-all | bytes 2097152 | tf_op jit(solution)/shard_map/all_to_all | solution.py:26
  161.0 32.4 %all_to_all.28.refs_1_ = bf16[32,104,128]{2,1,0:T(8,128)(2,1)S(1)} all-to-all(bf16[32,104,128]{2,1,0:T(8,128)(2,1)S(1)} %shard_map.119), channel_id=1, replica_groups=mesh['zh'=4,'yh'=4,'yl'=2,'core'=2,'x'=4,'zl'=2] {'zh','yh','yl'}, dimensions={0} | all-to-all | bytes 1703936 | tf_op jit(solution)/shard_map/all_to_all | solution.py:26
  193.4 5.7 %collective-permute-start.2 = (bf16[32,104,128]{2,1,0:T(8,128)(2,1)S(1)}, bf16[32,104,128]{2,1,0:T(8,128)(2,1)S(1)}, u32[]{:S(2)}, u32[]{:S(2)}) collective-permute-start(bf16[32,104,128]{2,1,0:T(8,128)(2,1)S(1)} %all_to_all.28.refs_1_), channel_id=1, source_target_pairs={{0,8},{8,0},{1,9},{9,1},{2,10},{10,2},{3,11},{11,3},{4,12},{12,4},... | collective-permute-start | bytes 2555912 | tf_op jit(solution)/shard_map/ppermute | solution.py:30
  199.4 1.1 convolution_convert_fusion
  201.1 1.4 shard_map.120
  202.6 1.1 copy.13
  203.7 1.1 copy.14
  (20 shorter events, 4.4 us)
Async XLA Ops:
  0.6 24.8 %copy-start = (bf16[192,1536]{1,0:T(8,128)(2,1)S(1)}, bf16[192,1536]{1,0:T(8,128)(2,1)}, u32[]{:S(2)}) copy-start(bf16[192,1536]{1,0:T(8,128)(2,1)} %refs_1_.1) | copy-start | bytes 1769476
  1.8 0.7 copy-start.1
  2.5 21.5 %copy-start.3 = (bf16[1,110592]{1,0:T(2,128)(2,1)S(1)}, bf16[1,110592]{1,0:T(2,128)(2,1)}, u32[]{:S(2)}) copy-start(bf16[1,110592]{1,0:T(2,128)(2,1)} %param.12) | copy-start | bytes 663556
  3.6 31.1 %all-to-all-start = ((bf16[32,16,384]{2,1,0:T(8,128)(2,1)}), bf16[32,16,384]{2,1,0:T(8,128)(2,1)S(1)}, u32[]{:S(2)}, u32[]{:S(2)}) async-start(bf16[32,16,384]{2,1,0:T(8,128)(2,1)} %bitcast.2), calls=%async_computation | async-start | bytes 786432 | tf_op jit(solution)/shard_map/all_to_all | solution.py:26
  81.5 8.4 %collective-permute-start = (bf16[8,352,128]{2,1,0:T(8,128)(2,1)S(1)}, bf16[8,352,128]{2,1,0:T(8,128)(2,1)S(1)}, u32[]{:S(2)}, u32[]{:S(2)}) collective-permute-start(bf16[8,352,128]{2,1,0:T(8,128)(2,1)S(1)} %get-tuple-element.40), channel_id=1, source_target_pairs={{0,8},{8,0},{1,9},{9,1},{2,10},{10,2},{3,11},{11,3},{4,12},{12,4},... | collective-permute-start | bytes 2162696 | tf_op jit(solution)/shard_map/ppermute | solution.py:30
  121.7 4.9 %collective-permute-start.1 = (bf16[2016,128]{1,0:T(8,128)(2,1)S(1)}, bf16[2016,128]{1,0:T(8,128)(2,1)S(1)}, u32[]{:S(2)}, u32[]{:S(2)}) collective-permute-start(bf16[2016,128]{1,0:T(8,128)(2,1)S(1)} %get-tuple-element.51), channel_id=1, source_target_pairs={{0,8},{8,0},{1,9},{9,1},{2,10},{10,2},{3,11},{11,3},{4,12},{12,4},... | collective-permute-start | bytes 1548296 | tf_op jit(solution)/shard_map/ppermute | solution.py:30
  127.8 71.4 %copy-start.2 = (s32[512]{0:T(512)S(1)}, s32[512]{0:T(512)}, u32[]{:S(2)}) copy-start(s32[512]{0:T(512)} %param.8) | copy-start | bytes 6148
  193.4 7.7 %collective-permute-start.2 = (bf16[32,104,128]{2,1,0:T(8,128)(2,1)S(1)}, bf16[32,104,128]{2,1,0:T(8,128)(2,1)S(1)}, u32[]{:S(2)}, u32[]{:S(2)}) collective-permute-start(bf16[32,104,128]{2,1,0:T(8,128)(2,1)S(1)} %all_to_all.28.refs_1_), channel_id=1, source_target_pairs={{0,8},{8,0},{1,9},{9,1},{2,10},{10,2},{3,11},{11,3},{4,12},{12,4},... | collective-permute-start | bytes 2555912 | tf_op jit(solution)/shard_map/ppermute | solution.py:30

commit v9 on v4

--- a/solution.py
+++ b/solution.py
@@ -99,12 +99,23 @@
         rows_ref[base + 2 * half : base + 3 * half] = odd[:, 64:]
 
 
-def pack_kernel(base_ref, order_ref, emb_ref, cot_ref, out_ref):
+def pack_kernel(base_ref, both_ref, order_ref, out_ref):
     token = lax.broadcasted_iota(jnp.int32, (TOK, TOK), 0)
     onehot = jnp.where(token == order_ref[...] - base_ref[0], 1.0, 0.0).astype(BF)
-    start = mm(emb_ref[...], onehot, 1, 0)
-    both = jnp.concatenate([start, cot_ref[...].astype(F32)], axis=0)
+    start = mm(both_ref[:CG], onehot, 1, 0)
+    both = jnp.concatenate([start, both_ref[CG:].astype(F32)], axis=0)
     out_ref[...] = both.T.astype(BF)
+
+
+def blocks_kernel(weight_ref, out_ref):
+    wide = weight_ref[...].astype(F32)
+    blank = jnp.zeros((32, 128), F32)
+    for j in range(8):
+        block = wide[:, CG * j : CG * (j + 1)]
+        rest = jnp.concatenate([block[:96, 128:], block[96:, 128:]], axis=1)
+        rows = jnp.concatenate([block[:, :128], rest, blank], axis=0)
+        for part in range(8):
+            out_ref[j, :, 128 * part : 128 * (part + 1)] = rows[40 * part : 40 * (part + 1)].astype(BF)
 
 
 def near_kernel(tokens_ref, weight_ref, blocks_ref, out_ref, hidden_ref, start_ref):
@@ -124,14 +135,22 @@
     hidden_ref[...] = hidden
     act = (hidden * jax.nn.sigmoid(hidden)).astype(BF)
     for j in range(8):
-        out_ref[j, :, :TOK] = act
-        out_ref[j, :, TOK : 2 * TOK] = cot
-        out_ref[j, :, 2 * TOK :] = blocks_ref[j]
-
-
-def mid_kernel(own_ref, sent_ref, start_ref, pointwise_ref, weight_ref, middle_ref, dh_ref, grad_ref, out_ref):
+        out_ref[j, :CG, :TOK] = act
+        out_ref[j, :CG, TOK:] = cot
+        out_ref[j, CG:] = blocks_ref[j]
+
+
+def mid_kernel(
+    own_ref, sent_ref, start_ref, pointwise_ref, weight_ref, middle_ref, dh_ref, grad_ref, out_ref, columns_ref
+):
+    for j in range(8):
+        rows = jnp.concatenate(
+            [sent_ref[j, CG:, 128 * part : 128 * (part + 1)].astype(F32) for part in range(8)], axis=0
+        )
+        columns_ref[j, :, :128] = rows[:CG].astype(BF)
+        columns_ref[j, :, 128:] = jnp.concatenate([rows[CG:288, :64], rows[CG:288, 64:]], axis=0).astype(BF)
     middle = start_ref[...].astype(F32) + sum(
-        mm(pointwise_ref[j * CG : (j + 1) * CG], sent_ref[j, :, :TOK], 0, 0) for j in range(8)
+        mm(pointwise_ref[j * CG : (j + 1) * CG], sent_ref[j, :CG, :TOK], 0, 0) for j in range(8)
     )
     middle = middle.astype(BF)
     middle_ref[...] = middle
@@ -143,16 +162,46 @@
     )
     s = jax.nn.sigmoid(hidden)
     act = (hidden * s).astype(BF)
-    for j in range(8):
-        out_ref[j, :, TOK:] = mm(sent_ref[j, :, TOK : 2 * TOK], act, 1, 1).astype(BF)
-    da = sum(mm(sent_ref[j, :, 2 * TOK :], sent_ref[j, :, TOK : 2 * TOK], 0, 0) for j in range(8))
+    blank = jnp.zeros((64, TOK), BF)
+    lower = jnp.concatenate([act[128:], blank], axis=0)
+    upper = jnp.concatenate([blank, act[128:]], axis=0)
+    for j in range(8):
+        cot = sent_ref[j, :CG, TOK:]
+        rest = mm(cot[:96], lower, 1, 1) + mm(cot[96:], upper, 1, 1)
+        rows = jnp.concatenate([mm(cot, act[:128], 1, 1), rest], axis=0)
+        for part in range(4):
+            out_ref[j, CG:, 128 * part : 128 * (part + 1)] = rows[72 * part : 72 * (part + 1)].astype(BF)
+    da = sum(mm(columns_ref[j], sent_ref[j, :CG, TOK:], 0, 0) for j in range(8))
     dh = (da * s * (1.0 + hidden * (1.0 - s))).astype(BF)
     dh_ref[...] = dh
     back = conv_back(dh.astype(F32), weight_ref, FAR)
-    grad = (sent_ref[own_ref[0], :, TOK : 2 * TOK].astype(F32) + back).astype(BF)
+    grad = (sent_ref[own_ref[0], :CG, TOK:].astype(F32) + back).astype(BF)
     grad_ref[...] = grad
     for j in range(8):
-        out_ref[j, :, :TOK] = mm(pointwise_ref[j * CG : (j + 1) * CG], grad, 1, 0).astype(BF)
+        out_ref[j, :CG] = mm(pointwise_ref[j * CG : (j + 1) * CG], grad, 1, 0).astype(BF)
+
+
+def block_of(got_ref, core, out_ref, base):
+    blank = jnp.zeros((8, 64), F32)
+    for j in range(8):
+        rows = jnp.concatenate(
+            [got_ref[j, CG:, 128 * part : 128 * (part + 1)].astype(F32) for part in range(4)], axis=0
+        )
+        low = core == 0
+        wide = jnp.where(low, rows[:96], rows[96:CG])
+        thin = jnp.where(low, rows[CG:, :64], rows[CG:, 64:])
+        for part in range(4):
+            rest = thin[24 * part : 24 * (part + 1)]
+            packed = jnp.concatenate([rest[:8], rest[8:16]], axis=1), jnp.concatenate([rest[16:], blank], axis=1)
+            at = base + 160 * j + 40 * part
+            piece = jnp.concatenate([wide[24 * part : 24 * (part + 1)], *packed], axis=0)
+            out_ref[at : at + 40] = piece.astype(out_ref.dtype)
+
+
+def columns_of(grad, sent_ref, core, out_ref):
+    half = jnp.concatenate([mm(grad, sent_ref[4 * core + j, :CG, :TOK], 1, 1) for j in range(4)], axis=1)
+    for j in range(6):
+        out_ref[CG * j : CG * (j + 1)] = half[:, 128 * j : 128 * (j + 1)].astype(out_ref.dtype)
 
 
 def back_kernel(
@@ -170,32 +219,27 @@
     far_rows_ref,
     near_rows_ref,
 ):
-    da = sum(got_ref[j, :, :TOK].astype(F32) for j in range(8))
+    core = core_ref[0]
+    da = sum(got_ref[j, :CG].astype(F32) for j in range(8))
     hidden = hidden_ref[...]
     s = jax.nn.sigmoid(hidden)
     dh = (da * s * (1.0 + hidden * (1.0 - s))).astype(BF)
     dh_ref[...] = dh
     conv_rows(start_ref[...].astype(F32), dh, NEAR, near_rows_ref)
     conv_rows(middle_ref[...].astype(F32), far_dh_ref[...], FAR, far_rows_ref)
-    blank = jnp.zeros((8, 64), F32)
-    for out_ref, core in ((mine_ref, core_ref[0]), (other_ref, 1 - core_ref[0])):
-        grad = jnp.concatenate([mm(grad_ref[...], sent_ref[4 * core + j, :, :TOK], 1, 1) for j in range(4)], axis=1)
-        for j in range(6):
-            out_ref[CG * j : CG * (j + 1)] = grad[:, 128 * j : 128 * (j + 1)].astype(out_ref.dtype)
-        rows = pl.ds(pl.multiple_of(432 * core, 8), 432)
-        out_ref[1152:1584] = far_rows_ref[rows].astype(out_ref.dtype)
-        out_ref[1584:2016] = near_rows_ref[rows].astype(out_ref.dtype)
-        for j in range(8):
-            half = got_ref[j, pl.ds(pl.multiple_of(96 * core, 16), 96), TOK:].astype(F32)
-            for part in range(4):
-                piece = half[24 * part : 24 * (part + 1)]
-                rest = piece[:, 128:]
-                packed = jnp.concatenate([rest[:8], rest[8:16]], axis=1), jnp.concatenate([rest[16:], blank], axis=1)
-                at = 2016 + 160 * j + 40 * part
-                out_ref[at : at + 40] = jnp.concatenate([piece[:, :128], *packed], axis=0).astype(out_ref.dtype)
-
-
-def tokens_kernel(dh_ref, weight_ref, grad_ref, out_ref):
+    mine = pl.ds(pl.multiple_of(432 * core, 8), 432)
+    mine_ref[:432] = far_rows_ref[mine]
+    mine_ref[432:] = near_rows_ref[mine]
+    other = pl.ds(pl.multiple_of(432 - 432 * core, 8), 432)
+    other_ref[1152:1584] = far_rows_ref[other].astype(BF)
+    other_ref[1584:2016] = near_rows_ref[other].astype(BF)
+    block_of(got_ref, 1 - core, other_ref, 2016)
+    columns_of(grad_ref[...], sent_ref, 1 - core, other_ref)
+
+
+def keep_kernel(core_ref, got_ref, sent_ref, dh_ref, weight_ref, grad_ref, mine_ref, out_ref):
+    block_of(got_ref, core_ref[0], mine_ref, 1152)
+    columns_of(grad_ref[...], sent_ref, core_ref[0], mine_ref)
     back = grad_ref[...].astype(F32) + conv_back(dh_ref[...].astype(F32), weight_ref, NEAR)
     rows = back.T
     out_ref[:, :16] = rows[:, :128].reshape(32, 16, 128).astype(BF)
@@ -203,11 +247,12 @@
     out_ref[:, 16:] = jnp.concatenate([rest[:, :8], rest[:, 8:]], axis=2).astype(BF)
 
 
-def gather_kernel(mine_ref, other_ref, tokens_ref, out_ref, rows_ref):
-    rows_ref[:2016] = mine_ref[:2016] + other_ref[:2016].astype(F32)
+def gather_kernel(mine_ref, conv_ref, other_ref, tokens_ref, out_ref, rows_ref):
+    rows_ref[:1152] = mine_ref[:1152] + other_ref[:1152].astype(F32)
+    rows_ref[1152:2016] = conv_ref[...] + other_ref[1152:2016].astype(F32)
     rows_ref[2016:] = jnp.zeros((32, 128), F32)
     out_ref[:, :64] = rows_ref[...].reshape(32, 64, 128).astype(BF)
-    rest = mine_ref[2016:] + other_ref[2016:].astype(F32)
+    rest = mine_ref[1152:] + other_ref[2016:].astype(F32)
     out_ref[:, 64:ROWS] = rest.reshape(32, 40, 128).astype(BF)
     out_ref[:, ROWS:] = tokens_ref[...]
 
@@ -257,48 +302,57 @@
     far_pw_ref[...] = far_ref[...].astype(BF)
 
 
-def local(emb, order, cot, cw1, pw1, cw2, pw2):
+def step(emb, order, cot, cw1, pw1, cw2, pw2):
     core = lax.axis_index("core").astype(jnp.int32).reshape(1)
     own = lax.axis_index(GRP).astype(jnp.int32).reshape(1)
     base = (lax.axis_index(SEQ) * TOK).astype(jnp.int32).reshape(1)
 
-    (packed,) = call(pack_kernel, [((TOK, 2 * CG), BF)], (base,), (), (order.reshape(1, TOK), emb, cot), space=pltpu.HBM)
+    both = jnp.concatenate([emb, cot], axis=0)
+    (packed,) = call(pack_kernel, [((TOK, 2 * CG), BF)], (base,), (both,), (order.reshape(1, TOK),))
     packed = swap(packed.reshape(32, TOK // 32, 2 * CG), CHIPS).reshape(TOK, 2 * CG)
-    packed, own, core, w1, w2, pw1t, pw2_blocks = lax.optimization_barrier(
-        (packed, own, core, cw1.reshape(3, CG, CG), cw2.reshape(3, CG, CG), pw1.T, pw2.reshape(CG, 8, CG).transpose(1, 0, 2))
+    (blocks,) = call(blocks_kernel, [((8, 40, 2 * TOK), BF)], (), (), (pw2,))
+    packed, own, core, w1, w2, pw1t, blocks = lax.optimization_barrier(
+        (packed, own, core, cw1.reshape(3, CG, CG), cw2.reshape(3, CG, CG), pw1.T, blocks)
     )
     sent, near_hidden, start = call(
         near_kernel,
-        [((8, CG, 2 * TOK + CG), BF), ((CG, TOK), F32), ((CG, TOK), BF)],
+        [((8, CG + 40, 2 * TOK), BF), ((CG, TOK), F32), ((CG, TOK), BF)],
         (),
-        (packed, w1, pw2_blocks),
+        (packed, w1, blocks),
     )
     sent = swap(sent, GRP)
     middle, far_dh, grad_middle, parts = call(
         mid_kernel,
-        [((CG, TOK), BF), ((CG, TOK), BF), ((CG, TOK), BF), ((8, CG, TOK + CG), BF)],
+        [((CG, TOK), BF), ((CG, TOK), BF), ((CG, TOK), BF), ((8, CG + 72, TOK), BF)],
         (own,),
         (sent,),
         (start, pw1t, w2),
+        scratch=[((8, CG, CG), BF)],
     )
     got = swap(parts, GRP)
 
-    near_dh, mine, other = call(
+    near_dh, conv_mine, other = call(
         back_kernel,
-        [((CG, TOK), BF), ((3296, 128), F32), ((3296, 128), BF)],
+        [((CG, TOK), BF), ((864, 128), F32), ((3296, 128), BF)],
         (core,),
         (got, sent),
         (near_hidden, start, grad_middle, middle, far_dh),
         scratch=[((864, 128), F32), ((864, 128), F32)],
     )
     other = other_core(other)
-    (tokens,) = call(tokens_kernel, [((32, 24, 128), BF)], (), (near_dh,), (w1, grad_middle))
+    mine, tokens = call(
+        keep_kernel,
+        [((2432, 128), F32), ((32, 24, 128), BF)],
+        (core,),
+        (got, sent, near_dh),
+        (w1, grad_middle),
+    )
     (bundle,) = call(
         gather_kernel,
         [((32, ROWS + 24, 128), BF)],
         (),
         (),
-        (mine, other, tokens),
+        (mine, conv_mine, other, tokens),
         scratch=[((2048, 128), F32)],
     )
     bundle = swap(bundle, CHIPS)
@@ -327,7 +381,7 @@
     fine = Mesh(mesh.devices.reshape(4, 4, 2, 2, 4, 2), SEQ + GRP)
     placed = (P(GRP, SEQ), P(SEQ), P(GRP, SEQ), P(GRP, None), P(GRP, None), P(GRP, None), P(GRP, None))
     return jax.shard_map(
-        local,
+        step,
         mesh=fine,
         in_specs=placed,
         out_specs=(P(GRP, SEQ), P(GRP, None), P(GRP, None), P(GRP, None), P(GRP, None)),

time: 210 us -> 206 us (0.981)
  local copies, waits for them, and re-layouts: 7.46 us -> 3.67 us
  blocking collectives: 144 us -> 141 us
    all_to_all x4, blocking collectives: 144 us -> 141 us  [swap(): return lax.all_to_all(blocks, axes, 0, 0, tiled=True)]
    unnamed x15 -> x13, local copies, waits for them, and re-layouts: 5.02 us -> 3.17 us
    pallas_call x8 -> x9, Pallas kernels: 11.9 us -> 12.9 us  [call(): pl.pallas_call(body, out_shape=[jax.ShapeDtypeStruct(shape, dtype) for sh...]
  transfers between devices with their start and end apart: 3 -> 3, of which waited for: 3 -> 3; matrix products, arithmetic and copies ran while one was open for 4% -> 3% of each run, Pallas kernels for 0% -> 1%
where the time goes in v9:
time: 206 us; the launch traced here: 205 us
  blocking collectives  141 us (68%)
  starting transfers between devices  29.6 us (14%)
  Pallas kernels  12.9 us (6%)
  waiting for transfers between devices  11.2 us (5%)
  other arithmetic  4.77 us (2%)
  local copies, waits for them, and re-layouts  3.67 us (2%)
    all_to_all x4, blocking collectives, swap(): return lax.all_to_all(blocks, axes, 0, 0, tiled=True)  141 us
    all_to_all x1, starting transfers between devices, swap(): return lax.all_to_all(blocks, axes, 0, 0, tiled=True)  16.6 us
    ppermute x2, starting transfers between devices, other_core(): return lax.ppermute(values, 'core', [(0, 1), (1, 0)])  12.9 us
    pallas_call x9, Pallas kernels, call(): pl.pallas_call(body, out_shape=[jax.ShapeDtypeStruct(shape, dtype) for sh...  12.9 us
    all_to_all x1, waiting for transfers between devices, swap(): return lax.all_to_all(blocks, axes, 0, 0, tiled=True)  9.65 us
  transfers between devices with their start and end apart: 3, of which 3 were waited for; matrix products, arithmetic and copies ran while one was open for 3% of the time, Pallas kernels for 1%

profile of v9, /device:TPU:1, one launch (start us, length us, event | category | flops | bytes accessed | tf_op | source)
XLA Modules:
  0.0 204.6 jit_solution(1739104651177461218)
XLA Ops:
  0.7 1.1 pad_maximum_fusion.refs_1_
  1.8 0.7 copy-done.1
  2.5 1.2 shard_map.110
  3.6 16.6 %all-to-all-start = ((bf16[32,16,384]{2,1,0:T(8,128)(2,1)}), bf16[32,16,384]{2,1,0:T(8,128)(2,1)S(1)}, u32[]{:S(2)}, u32[]{:S(2)}) async-start(bf16[32,16,384]{2,1,0:T(8,128)(2,1)} %bitcast.2), calls=%async_computation | async-start | bytes 786432 | tf_op jit(solution)/shard_map/all_to_all | solution.py:26
  20.3 2.2 %reduce = bf16[110592]{0:T(1024)(128)(2,1)S(1)} reduce(bf16[1,110592]{1,0:T(2,128)(2,1)} %param.10, bf16[]{:T(256)} %constant.33), dimensions={0}, to_apply=%param.10.reduce_sub_computation | reduce | bytes 442370 | tf_op args[3]
  22.7 1.4 reduce.1
  25.2 9.6 %all-to-all-done = bf16[32,16,384]{2,1,0:T(8,128)(2,1)S(1)} async-done(((bf16[32,16,384]{2,1,0:T(8,128)(2,1)}), bf16[32,16,384]{2,1,0:T(8,128)(2,1)S(1)}, u32[]{:S(2)}, u32[]{:S(2)}) %all-to-all-start) | async-done | bytes 393248 | tf_op jit(solution)/shard_map/all_to_all | solution.py:26
  34.9 0.7 shard_map.112
  35.6 46.7 %all_to_all.25.refs_1_.refs_2_ = bf16[8,232,1024]{2,1,0:T(8,128)(2,1)S(1)} all-to-all(bf16[8,232,1024]{2,1,0:T(8,128)(2,1)S(1)} %get-tuple-element.33), channel_id=1, replica_groups=mesh['zh'=4,'yh'=4,'yl'=2,'core'=2,'x'=4,'zl'=2] {'x','zl'}, dimensions={0} | all-to-all | bytes 7602176 | tf_op jit(solution)/shard_map/all_to_all | solution.py:26
  82.2 3.7 %shard_map.113 = (bf16[192,512]{1,0:T(8,128)(2,1)S(1)}, bf16[192,512]{1,0:T(8,128)(2,1)S(1)}, bf16[192,512]{1,0:T(8,128)(2,1)S(1)}, bf16[8,264,512]{2,1,0:T(8,128)(2,1)S(1)}) custom-call(s32[1]{0:T(128)} %bitcast.4.refs_0_, bf16[8,232,1024]{2,1,0:T(8,128)(2,1)S(1)} %all_to_all.25.refs_1_.refs_2_, bf16[192,512]{1,0:T(8,128)(2,1)S(1)} %get-tuple-element.34.refs_2_.refs_4_, ...), custom_call_target="tpu_custom_call" | custom-call | tf_op jit(solution)/shard_map/pallas_call | solution.py:56
  85.9 25.5 %all_to_all.26.refs_1_ = bf16[8,264,512]{2,1,0:T(8,128)(2,1)S(1)} all-to-all(bf16[8,264,512]{2,1,0:T(8,128)(2,1)S(1)} %get-tuple-element.37), channel_id=1, replica_groups=mesh['zh'=4,'yh'=4,'yl'=2,'core'=2,'x'=4,'zl'=2] {'x','zl'}, dimensions={0} | all-to-all | bytes 4325376 | tf_op jit(solution)/shard_map/all_to_all | solution.py:26
  111.4 2.8 %shard_map.114 = (bf16[192,512]{1,0:T(8,128)(2,1)S(1)}, f32[864,128]{1,0:T(8,128)S(1)}, bf16[3296,128]{1,0:T(8,128)(2,1)S(1)}) custom-call(s32[1]{0:T(128)} %bitcast.5.refs_0_, bf16[8,264,512]{2,1,0:T(8,128)(2,1)S(1)} %all_to_all.26.refs_1_, bf16[8,232,1024]{2,1,0:T(8,128)(2,1)S(1)} %all_to_all.25.refs_1_.refs_2_, f32[192,512]{1,0:T(8,128)S(1)} %get-tuple-element.38.refs_3_, ...), custom_call_target="tpu_custom_call" | custom-call | tf_op jit(solution)/shard_map/pallas_call | solution.py:56
  114.2 7.6 %collective-permute-start = (bf16[3296,128]{1,0:T(8,128)(2,1)S(1)}, bf16[3296,128]{1,0:T(8,128)(2,1)S(1)}, u32[]{:S(2)}, u32[]{:S(2)}) collective-permute-start(bf16[3296,128]{1,0:T(8,128)(2,1)S(1)} %get-tuple-element.45), channel_id=1, source_target_pairs={{0,8},{8,0},{1,9},{9,1},{2,10},{10,2},{3,11},{11,3},{4,12},{12,4},... | collective-permute-start | bytes 2531336 | tf_op jit(solution)/shard_map/ppermute | solution.py:30
  121.8 1.1 shard_map.115
  122.9 0.9 collective-permute-done.refs_2_
  123.7 1.1 shard_map.116
  124.9 35.7 %all_to_all.27.refs_0_ = bf16[32,128,128]{2,1,0:T(8,128)(2,1)S(1)} all-to-all(bf16[32,128,128]{2,1,0:T(8,128)(2,1)S(1)} %shard_map.116), channel_id=1, replica_groups=mesh['zh'=4,'yh'=4,'yl'=2,'core'=2,'x'=4,'zl'=2] {'zh','yh','yl'}, dimensions={0} | all-to-all | bytes 2097152 | tf_op jit(solution)/shard_map/all_to_all | solution.py:26
  160.7 32.8 %all_to_all.28.refs_1_ = bf16[32,104,128]{2,1,0:T(8,128)(2,1)S(1)} all-to-all(bf16[32,104,128]{2,1,0:T(8,128)(2,1)S(1)} %shard_map.117), channel_id=1, replica_groups=mesh['zh'=4,'yh'=4,'yl'=2,'core'=2,'x'=4,'zl'=2] {'zh','yh','yl'}, dimensions={0} | all-to-all | bytes 1703936 | tf_op jit(solution)/shard_map/all_to_all | solution.py:26
  193.5 5.4 %collective-permute-start.1 = (bf16[32,104,128]{2,1,0:T(8,128)(2,1)S(1)}, bf16[32,104,128]{2,1,0:T(8,128)(2,1)S(1)}, u32[]{:S(2)}, u32[]{:S(2)}) collective-permute-start(bf16[32,104,128]{2,1,0:T(8,128)(2,1)S(1)} %all_to_all.28.refs_1_), channel_id=1, source_target_pairs={{0,8},{8,0},{1,9},{9,1},{2,10},{10,2},{3,11},{11,3},{4,12},{12,4},... | collective-permute-start | bytes 2555912 | tf_op jit(solution)/shard_map/ppermute | solution.py:30
  199.1 1.1 convolution_convert_fusion
  200.1 0.7 collective-permute-done.1.refs_2_
  200.9 1.6 shard_map.118
  202.4 1.1 copy.13
  203.5 1.1 copy.14
  (18 shorter events, 1.6 us)
Async XLA Ops:
  0.6 23.7 %copy-start.3 = (bf16[192,1536]{1,0:T(8,128)(2,1)S(1)}, bf16[192,1536]{1,0:T(8,128)(2,1)}, u32[]{:S(2)}) copy-start(bf16[192,1536]{1,0:T(8,128)(2,1)} %param.11) | copy-start | bytes 1769476
  1.8 0.7 copy-start.1
  2.5 20.3 %copy-start.4 = (bf16[1,110592]{1,0:T(2,128)(2,1)S(1)}, bf16[1,110592]{1,0:T(2,128)(2,1)}, u32[]{:S(2)}) copy-start(bf16[1,110592]{1,0:T(2,128)(2,1)} %param.12) | copy-start | bytes 663556
  3.6 21.0 %copy-start = (bf16[192,1536]{1,0:T(8,128)(2,1)S(1)}, bf16[192,1536]{1,0:T(8,128)(2,1)}, u32[]{:S(2)}) copy-start(bf16[192,1536]{1,0:T(8,128)(2,1)} %refs_0_.1) | copy-start | bytes 1769476
  3.6 31.3 %all-to-all-start = ((bf16[32,16,384]{2,1,0:T(8,128)(2,1)}), bf16[32,16,384]{2,1,0:T(8,128)(2,1)S(1)}, u32[]{:S(2)}, u32[]{:S(2)}) async-start(bf16[32,16,384]{2,1,0:T(8,128)(2,1)} %bitcast.2), calls=%async_computation | async-start | bytes 786432 | tf_op jit(solution)/shard_map/all_to_all | solution.py:26
  114.2 9.5 %collective-permute-start = (bf16[3296,128]{1,0:T(8,128)(2,1)S(1)}, bf16[3296,128]{1,0:T(8,128)(2,1)S(1)}, u32[]{:S(2)}, u32[]{:S(2)}) collective-permute-start(bf16[3296,128]{1,0:T(8,128)(2,1)S(1)} %get-tuple-element.45), channel_id=1, source_target_pairs={{0,8},{8,0},{1,9},{9,1},{2,10},{10,2},{3,11},{11,3},{4,12},{12,4},... | collective-permute-start | bytes 2531336 | tf_op jit(solution)/shard_map/ppermute | solution.py:30
  160.6 38.3 %copy-start.2 = (s32[512]{0:T(512)S(1)}, s32[512]{0:T(512)}, u32[]{:S(2)}) copy-start(s32[512]{0:T(512)} %param.8) | copy-start | bytes 6148
  193.5 7.4 %collective-permute-start.1 = (bf16[32,104,128]{2,1,0:T(8,128)(2,1)S(1)}, bf16[32,104,128]{2,1,0:T(8,128)(2,1)S(1)}, u32[]{:S(2)}, u32[]{:S(2)}) collective-permute-start(bf16[32,104,128]{2,1,0:T(8,128)(2,1)S(1)} %all_to_all.28.refs_1_), channel_id=1, source_target_pairs={{0,8},{8,0},{1,9},{9,1},{2,10},{10,2},{3,11},{11,3},{4,12},{12,4},... | collective-permute-start | bytes 2555912 | tf_op jit(solution)/shard_map/ppermute | solution.py:30

commit v10 on v9

--- a/solution.py
+++ b/solution.py
@@ -268,10 +268,8 @@
 
 def finish_kernel(core_ref, mine_ref, other_ref, near_pw_ref, far_pw_ref, near_conv_ref, far_conv_ref, all_ref, far_ref):
     first = core_ref[0] == 0
-    mine = mine_ref[...].astype(F32)
-    other = other_ref[...].astype(F32)
-    all_ref[0] = jnp.where(first, mine, other)
-    all_ref[1] = jnp.where(first, other, mine)
+    all_ref[0] = jnp.where(first, mine_ref[...], other_ref[...])
+    all_ref[1] = jnp.where(first, other_ref[...], mine_ref[...])
     for j in range(12):
         for part in range(3):
             near_pw_ref[64 * part : 64 * (part + 1), 128 * j : 128 * (j + 1)] = all_ref[
@@ -291,7 +289,7 @@
             for pair in range(4):
                 blocks = []
                 for j in (2 * pair, 2 * pair + 1):
-                    piece = all_ref[core, 4 * j + part, 64:ROWS]
+                    piece = all_ref[core, 4 * j + part, 64:ROWS].astype(F32)
                     rest = jnp.concatenate([piece[24:32, :64], piece[24:32, 64:], piece[32:, :64]], axis=0)
                     blocks.append((piece[:24], rest))
                 (even, even_rest), (odd, odd_rest) = blocks
@@ -370,7 +368,7 @@
         [((CG, 8 * CG), BF), ((CG, 8 * CG), BF), ((288, 384), BF), ((288, 384), BF)],
         (core,),
         (spread, other_core(spread)),
-        scratch=[((2, 32, ROWS, 128), F32), ((CG, 8 * CG), F32)],
+        scratch=[((2, 32, ROWS, 128), BF), ((CG, 8 * CG), F32)],
         mib=12,
     )
     flat = (1, 3 * CG * CG)

time: 206 us -> 206 us (level)
  no operation moved by 1% of the time
where the time goes in v10:
time: 206 us; the launch traced here: 205 us
  blocking collectives  141 us (68%)
  starting transfers between devices  29.6 us (14%)
  Pallas kernels  13.2 us (6%)
  waiting for transfers between devices  11.2 us (5%)
  other arithmetic  4.77 us (2%)
  local copies, waits for them, and re-layouts  3.67 us (2%)
    all_to_all x4, blocking collectives, swap(): return lax.all_to_all(blocks, axes, 0, 0, tiled=True)  141 us
    all_to_all x1, starting transfers between devices, swap(): return lax.all_to_all(blocks, axes, 0, 0, tiled=True)  16.6 us
    pallas_call x9, Pallas kernels, call(): pl.pallas_call(body, out_shape=[jax.ShapeDtypeStruct(shape, dtype) for sh...  13.2 us
    ppermute x2, starting transfers between devices, other_core(): return lax.ppermute(values, 'core', [(0, 1), (1, 0)])  12.9 us
    all_to_all x1, waiting for transfers between devices, swap(): return lax.all_to_all(blocks, axes, 0, 0, tiled=True)  9.65 us
  transfers between devices with their start and end apart: 3, of which 3 were waited for; matrix products, arithmetic and copies ran while one was open for 3% of the time, Pallas kernels for 1%

profile of v10, /device:TPU:1, one launch (start us, length us, event | category | flops | bytes accessed | tf_op | source)
XLA Modules:
  0.0 204.9 jit_solution(3404296040686881923)
XLA Ops:
  0.7 1.1 pad_maximum_fusion.refs_1_
  1.8 0.7 copy-done.1
  2.5 1.2 shard_map.110
  3.6 16.6 %all-to-all-start = ((bf16[32,16,384]{2,1,0:T(8,128)(2,1)}), bf16[32,16,384]{2,1,0:T(8,128)(2,1)S(1)}, u32[]{:S(2)}, u32[]{:S(2)}) async-start(bf16[32,16,384]{2,1,0:T(8,128)(2,1)} %bitcast.2), calls=%async_computation | async-start | bytes 786432 | tf_op jit(solution)/shard_map/all_to_all | solution.py:26
  20.3 2.2 %reduce = bf16[110592]{0:T(1024)(128)(2,1)S(1)} reduce(bf16[1,110592]{1,0:T(2,128)(2,1)} %param.10, bf16[]{:T(256)} %constant.33), dimensions={0}, to_apply=%param.10.reduce_sub_computation | reduce | bytes 442370 | tf_op args[3]
  22.7 1.4 reduce.1
  25.2 9.6 %all-to-all-done = bf16[32,16,384]{2,1,0:T(8,128)(2,1)S(1)} async-done(((bf16[32,16,384]{2,1,0:T(8,128)(2,1)}), bf16[32,16,384]{2,1,0:T(8,128)(2,1)S(1)}, u32[]{:S(2)}, u32[]{:S(2)}) %all-to-all-start) | async-done | bytes 393248 | tf_op jit(solution)/shard_map/all_to_all | solution.py:26
  34.9 0.7 shard_map.112
  35.6 46.7 %all_to_all.25.refs_1_.refs_2_ = bf16[8,232,1024]{2,1,0:T(8,128)(2,1)S(1)} all-to-all(bf16[8,232,1024]{2,1,0:T(8,128)(2,1)S(1)} %get-tuple-element.33), channel_id=1, replica_groups=mesh['zh'=4,'yh'=4,'yl'=2,'core'=2,'x'=4,'zl'=2] {'x','zl'}, dimensions={0} | all-to-all | bytes 7602176 | tf_op jit(solution)/shard_map/all_to_all | solution.py:26
  82.2 3.7 %shard_map.113 = (bf16[192,512]{1,0:T(8,128)(2,1)S(1)}, bf16[192,512]{1,0:T(8,128)(2,1)S(1)}, bf16[192,512]{1,0:T(8,128)(2,1)S(1)}, bf16[8,264,512]{2,1,0:T(8,128)(2,1)S(1)}) custom-call(s32[1]{0:T(128)} %bitcast.4.refs_0_, bf16[8,232,1024]{2,1,0:T(8,128)(2,1)S(1)} %all_to_all.25.refs_1_.refs_2_, bf16[192,512]{1,0:T(8,128)(2,1)S(1)} %get-tuple-element.34.refs_2_.refs_4_, ...), custom_call_target="tpu_custom_call" | custom-call | tf_op jit(solution)/shard_map/pallas_call | solution.py:56
  85.9 25.5 %all_to_all.26.refs_1_ = bf16[8,264,512]{2,1,0:T(8,128)(2,1)S(1)} all-to-all(bf16[8,264,512]{2,1,0:T(8,128)(2,1)S(1)} %get-tuple-element.37), channel_id=1, replica_groups=mesh['zh'=4,'yh'=4,'yl'=2,'core'=2,'x'=4,'zl'=2] {'x','zl'}, dimensions={0} | all-to-all | bytes 4325376 | tf_op jit(solution)/shard_map/all_to_all | solution.py:26
  111.4 2.8 %shard_map.114 = (bf16[192,512]{1,0:T(8,128)(2,1)S(1)}, f32[864,128]{1,0:T(8,128)S(1)}, bf16[3296,128]{1,0:T(8,128)(2,1)S(1)}) custom-call(s32[1]{0:T(128)} %bitcast.5.refs_0_, bf16[8,264,512]{2,1,0:T(8,128)(2,1)S(1)} %all_to_all.26.refs_1_, bf16[8,232,1024]{2,1,0:T(8,128)(2,1)S(1)} %all_to_all.25.refs_1_.refs_2_, f32[192,512]{1,0:T(8,128)S(1)} %get-tuple-element.38.refs_3_, ...), custom_call_target="tpu_custom_call" | custom-call | tf_op jit(solution)/shard_map/pallas_call | solution.py:56
  114.2 7.6 %collective-permute-start = (bf16[3296,128]{1,0:T(8,128)(2,1)S(1)}, bf16[3296,128]{1,0:T(8,128)(2,1)S(1)}, u32[]{:S(2)}, u32[]{:S(2)}) collective-permute-start(bf16[3296,128]{1,0:T(8,128)(2,1)S(1)} %get-tuple-element.45), channel_id=1, source_target_pairs={{0,8},{8,0},{1,9},{9,1},{2,10},{10,2},{3,11},{11,3},{4,12},{12,4},... | collective-permute-start | bytes 2531336 | tf_op jit(solution)/shard_map/ppermute | solution.py:30
  121.8 1.1 shard_map.115
  122.9 0.9 collective-permute-done.refs_2_
  123.7 1.1 shard_map.116
  124.9 35.7 %all_to_all.27.refs_0_ = bf16[32,128,128]{2,1,0:T(8,128)(2,1)S(1)} all-to-all(bf16[32,128,128]{2,1,0:T(8,128)(2,1)S(1)} %shard_map.116), channel_id=1, replica_groups=mesh['zh'=4,'yh'=4,'yl'=2,'core'=2,'x'=4,'zl'=2] {'zh','yh','yl'}, dimensions={0} | all-to-all | bytes 2097152 | tf_op jit(solution)/shard_map/all_to_all | solution.py:26
  160.7 32.8 %all_to_all.28.refs_1_ = bf16[32,104,128]{2,1,0:T(8,128)(2,1)S(1)} all-to-all(bf16[32,104,128]{2,1,0:T(8,128)(2,1)S(1)} %shard_map.117), channel_id=1, replica_groups=mesh['zh'=4,'yh'=4,'yl'=2,'core'=2,'x'=4,'zl'=2] {'zh','yh','yl'}, dimensions={0} | all-to-all | bytes 1703936 | tf_op jit(solution)/shard_map/all_to_all | solution.py:26
  193.5 5.4 %collective-permute-start.1 = (bf16[32,104,128]{2,1,0:T(8,128)(2,1)S(1)}, bf16[32,104,128]{2,1,0:T(8,128)(2,1)S(1)}, u32[]{:S(2)}, u32[]{:S(2)}) collective-permute-start(bf16[32,104,128]{2,1,0:T(8,128)(2,1)S(1)} %all_to_all.28.refs_1_), channel_id=1, source_target_pairs={{0,8},{8,0},{1,9},{9,1},{2,10},{10,2},{3,11},{11,3},{4,12},{12,4},... | collective-permute-start | bytes 2555912 | tf_op jit(solution)/shard_map/ppermute | solution.py:30
  199.1 1.1 convolution_convert_fusion
  200.1 0.7 collective-permute-done.1.refs_2_
  200.9 1.9 shard_map.118
  202.7 1.1 copy.13
  203.8 1.1 copy.14
  (18 shorter events, 1.6 us)
Async XLA Ops:
  0.6 23.7 %copy-start.3 = (bf16[192,1536]{1,0:T(8,128)(2,1)S(1)}, bf16[192,1536]{1,0:T(8,128)(2,1)}, u32[]{:S(2)}) copy-start(bf16[192,1536]{1,0:T(8,128)(2,1)} %param.11) | copy-start | bytes 1769476
  1.8 0.7 copy-start.1
  2.5 20.3 %copy-start.4 = (bf16[1,110592]{1,0:T(2,128)(2,1)S(1)}, bf16[1,110592]{1,0:T(2,128)(2,1)}, u32[]{:S(2)}) copy-start(bf16[1,110592]{1,0:T(2,128)(2,1)} %param.12) | copy-start | bytes 663556
  3.6 21.0 %copy-start = (bf16[192,1536]{1,0:T(8,128)(2,1)S(1)}, bf16[192,1536]{1,0:T(8,128)(2,1)}, u32[]{:S(2)}) copy-start(bf16[192,1536]{1,0:T(8,128)(2,1)} %refs_0_.1) | copy-start | bytes 1769476
  3.6 31.3 %all-to-all-start = ((bf16[32,16,384]{2,1,0:T(8,128)(2,1)}), bf16[32,16,384]{2,1,0:T(8,128)(2,1)S(1)}, u32[]{:S(2)}, u32[]{:S(2)}) async-start(bf16[32,16,384]{2,1,0:T(8,128)(2,1)} %bitcast.2), calls=%async_computation | async-start | bytes 786432 | tf_op jit(solution)/shard_map/all_to_all | solution.py:26
  114.2 9.5 %collective-permute-start = (bf16[3296,128]{1,0:T(8,128)(2,1)S(1)}, bf16[3296,128]{1,0:T(8,128)(2,1)S(1)}, u32[]{:S(2)}, u32[]{:S(2)}) collective-permute-start(bf16[3296,128]{1,0:T(8,128)(2,1)S(1)} %get-tuple-element.45), channel_id=1, source_target_pairs={{0,8},{8,0},{1,9},{9,1},{2,10},{10,2},{3,11},{11,3},{4,12},{12,4},... | collective-permute-start | bytes 2531336 | tf_op jit(solution)/shard_map/ppermute | solution.py:30
  160.6 38.3 %copy-start.2 = (s32[512]{0:T(512)S(1)}, s32[512]{0:T(512)}, u32[]{:S(2)}) copy-start(s32[512]{0:T(512)} %param.8) | copy-start | bytes 6148
  193.5 7.4 %collective-permute-start.1 = (bf16[32,104,128]{2,1,0:T(8,128)(2,1)S(1)}, bf16[32,104,128]{2,1,0:T(8,128)(2,1)S(1)}, u32[]{:S(2)}, u32[]{:S(2)}) collective-permute-start(bf16[32,104,128]{2,1,0:T(8,128)(2,1)S(1)} %all_to_all.28.refs_1_), channel_id=1, source_target_pairs={{0,8},{8,0},{1,9},{9,1},{2,10},{10,2},{3,11},{11,3},{4,12},{12,4},... | collective-permute-start | bytes 2555912 | tf_op jit(solution)/shard_map/ppermute | solution.py:30
